TPU v7x, 256 devices: a whole 4x4x8 slice. The times are simulated.
256 devices in a mesh: blk: 128 (over z, y, x_lo, core), tok: 2 (over x_hi).
Axes of the slice: x: 4 (x_hi: 2, x_lo: 2; x = x_hi * 2 + x_lo), y: 4, z: 8, core: 2. Of those that a mesh axis runs over, the one named last changes fastest.
Arguments:
- tokens: bfloat16 [512, 8192], P(('blk', 'tok')), may hold values from -6 to 6
- upstream: bfloat16 [512, 8192], P(('blk', 'tok')), may hold values from -6 to 6
- gate_weight: bfloat16 [14336, 8192], P('blk'), may hold values from -0.0625 to 0.0625
- up_weight: bfloat16 [14336, 8192], P('blk'), may hold values from -0.0625 to 0.0625
- down_weight: bfloat16 [14336, 8192], P('blk'), may hold values from -0.046875 to 0.046875
Outputs:
- mixed: bfloat16 [512, 8192], P(('blk', 'tok'))
- input_grad: bfloat16 [512, 8192], P(('blk', 'tok'))
- gate_weight_grad: bfloat16 [14336, 8192], P('blk', 'tok')
- up_weight_grad: bfloat16 [14336, 8192], P('blk', 'tok')
- down_weight_grad: bfloat16 [14336, 8192], P('blk', 'tok')
All inputs are finite; a program needn't handle non-finite values.
Results may differ from a plain program's by a relative error of at most 0.0049.
Values may be sent and summed in bfloat16 or wider, within the bound.
No kernel may reach another device: no remote copies, remote signals or barrier semaphores. Data moves between devices by JAX's collectives and lax.ppermute only.
A program may use at most 128 MiB of HBM per device.

v0:
```python
import functools

import jax
import jax.numpy as jnp
from jax import lax
from jax.experimental import pallas as pl
from jax.experimental.pallas import tpu as pltpu
from jax.sharding import Mesh
from jax.sharding import PartitionSpec as P

AXES = ("z", "y", "x", "core", "tok")
BLK = ("z", "y", "x", "core")
PLANE = ("y", "x")
PAIRS = ("tok", "core")
F32 = jnp.float32
BF16 = jnp.bfloat16
VMEM = pl.BlockSpec(memory_space=pltpu.VMEM)
SMEM = pl.BlockSpec(memory_space=pltpu.SMEM)
PARAMS = pltpu.CompilerParams(vmem_limit_bytes=40 * 1024 * 1024)


def shifted(block, axis, distance):
    count = lax.axis_size(axis)
    return lax.ppermute(block, axis, [(i, (i + distance) % count) for i in range(count)])


def exchanged(blocks, axes):
    return lax.all_to_all(blocks, axes, 0, 0, tiled=True)


def by_rows(left, right):
    return lax.dot_general(left, right, (((1,), (1,)), ((), ())), preferred_element_type=F32)


def by_columns(left, right):
    return lax.dot_general(left, right, (((0,), (0,)), ((), ())), preferred_element_type=F32)


def called(kernel, out_shape, *args, specs=None, scratch=(), **kwargs):
    specs = specs or [VMEM] * len(args)
    return pl.pallas_call(
        functools.partial(kernel, **kwargs),
        out_shape=out_shape,
        in_specs=specs,
        out_specs=jax.tree.map(lambda _: VMEM, out_shape),
        scratch_shapes=scratch,
        compiler_params=PARAMS,
    )(*args)


def called_at(kernel, out_shape, places, *args, index=None, scratch=(), **kwargs):
    def whole(shape):
        return pl.BlockSpec(shape, lambda *_: (0,) * len(shape))

    specs = [
        whole(arg.shape) if place is None else pl.BlockSpec(*place)
        for arg, place in zip(args, places, strict=True)
    ]
    grid = pltpu.PrefetchScalarGridSpec(
        num_scalar_prefetch=1,
        grid=(1,),
        in_specs=specs,
        out_specs=jax.tree.map(lambda o: whole(o.shape), out_shape),
        scratch_shapes=scratch,
    )
    return pl.pallas_call(
        functools.partial(kernel, **kwargs),
        out_shape=out_shape,
        grid_spec=grid,
        compiler_params=PARAMS,
    )(jnp.zeros((1,), jnp.int32) if index is None else index, *args)


def shape_of(shape, kind=BF16):
    return jax.ShapeDtypeStruct(shape, kind)


def deal_kernel(tokens_ref, upstream_ref, first_ref, second_ref, *, quarters):
    part = tokens_ref.shape[1] // quarters
    for q in range(quarters):
        rows = tokens_ref[:, q * part : (q + 1) * part]
        grads = upstream_ref[:, q * part : (q + 1) * part]
        for j in range(first_ref.shape[0] // quarters):
            first_ref[j * quarters + q] = rows
        for j in range(second_ref.shape[0] // quarters):
            second_ref[j * quarters + q] = grads


def merge_kernel(blocks_ref, out_ref, rows_ref):
    n, pair, _ = blocks_ref.shape
    for j in range(n):
        rows_ref[j * pair : (j + 1) * pair, :] = blocks_ref[j].astype(F32)
    out_ref[...] = rows_ref[...].astype(BF16)


def merge_from_kernel(first_ref, blocks_ref, out_ref, rows_ref, *, outer):
    n, pair, _ = blocks_ref.shape
    per = n // outer
    for k in range(outer):
        member = lax.rem(first_ref[0] + k, outer)
        for q in range(per):
            at = (k * per + q) * pair
            rows_ref[at : at + pair, :] = blocks_ref[member * per + q].astype(F32)
    rows = rows_ref[...].astype(BF16)
    for j in range(out_ref.shape[0]):
        out_ref[j] = rows


def stack_kernel(*refs, place):
    *block_refs, left_ref, right_ref, out_ref = refs
    height = left_ref.shape[0]
    middle = left_ref.shape[1]
    places = [k for k in range(len(block_refs) + 1) if k != place]
    for k, block_ref in zip(places, block_refs, strict=True):
        out_ref[k * height : (k + 1) * height, :] = block_ref[...]
    out_ref[place * height : (place + 1) * height, :middle] = left_ref[...]
    out_ref[place * height : (place + 1) * height, middle:] = right_ref[...]


def pack_kernel(_, gate_ref, up_ref, down_ref, out_ref):
    units = gate_ref.shape[0]
    for j, ref in enumerate((gate_ref, up_ref, down_ref)):
        out_ref[j * units : (j + 1) * units, :] = ref[...]


def weights_kernel(_, gate_ref, up_ref, down_ref, got_ref, in_ref, out_ref):
    units = gate_ref.shape[0]
    in_ref[:units, :] = gate_ref[...]
    in_ref[units : 2 * units, :] = up_ref[...]
    in_ref[2 * units :, :] = got_ref[: 2 * units, :]
    out_ref[:units, :] = down_ref[...]
    out_ref[units:, :] = got_ref[2 * units :, :]


def middle_kernel(sum_ref, got_ref, hid_ref, hid_got_ref, out_ref):
    units = hid_ref.shape[0]
    gate_value = sum_ref[:units, :] + got_ref[:units, :]
    up_value = sum_ref[units:, :] + got_ref[units:, :]
    hidden_grad = hid_ref[...] + hid_got_ref[...]
    gate_sigmoid = jax.nn.sigmoid(gate_value)
    swish_gate = gate_value * gate_sigmoid
    gate_grad = hidden_grad * up_value * gate_sigmoid * (1.0 + gate_value * (1.0 - gate_sigmoid))
    out_ref[:units, :] = gate_grad.astype(BF16)
    out_ref[units : 2 * units, :] = (hidden_grad * swish_gate).astype(BF16)
    out_ref[2 * units :, :] = (swish_gate * up_value).astype(BF16)


def pair_kernel(own_ref, got_ref, in_ref, hidden_ref):
    double = in_ref.shape[0] // 2
    in_ref[:double, :] = own_ref[:double, :]
    in_ref[double:, :] = got_ref[:double, :]
    hidden_ref[: double // 2, :] = own_ref[double:, :]
    hidden_ref[double // 2 :, :] = got_ref[double:, :]


def both_of(left_ref, right_ref):
    return jnp.concatenate([left_ref[...], right_ref[...]], axis=1)


def open_kernel(_, left_ref, right_ref, up_ref, down_ref):
    term = both_of(left_ref, right_ref)
    middle = up_ref.shape[1]
    up_ref[...] = term[:, :middle].astype(BF16)
    down_ref[...] = term[:, middle:].astype(BF16)


def turn_kernel(_, la_ref, ra_ref, lb_ref, rb_ref, came_up_ref, came_down_ref, up_ref, down_ref):
    ahead, behind = both_of(la_ref, ra_ref), both_of(lb_ref, rb_ref)
    reach = came_up_ref.shape[1]
    width = up_ref.shape[1]
    start = width - came_down_ref.shape[1]
    up_ref[:, :reach] = (ahead[:, :reach] + came_up_ref[...].astype(F32)).astype(BF16)
    if reach < width:
        up_ref[:, reach:] = ahead[:, reach:].astype(BF16)
        down_ref[:, :start] = behind[:, :start].astype(BF16)
    down_ref[:, start:] = (behind[:, start:] + came_down_ref[...].astype(F32)).astype(BF16)


def close_kernel(_, left_ref, right_ref, came_up_ref, came_down_ref, out_ref, rows_ref):
    n, pair, _ = out_ref.shape
    total = both_of(left_ref, right_ref)
    total = total + came_up_ref[...].astype(F32) + came_down_ref[...].astype(F32)
    rows_ref[...] = total
    for j in range(n):
        out_ref[j] = rows_ref[j * pair : (j + 1) * pair, :].astype(BF16)


def split_from_kernel(first_ref, terms_ref, out_ref, rows_ref, *, outer):
    n, pair, _ = out_ref.shape
    per = n // outer
    total = terms_ref[0].astype(F32)
    for j in range(1, terms_ref.shape[0]):
        total = total + terms_ref[j].astype(F32)
    rows_ref[...] = total
    for k in range(outer):
        member = lax.rem(first_ref[0] + k, outer)
        for q in range(per):
            at = (k * per + q) * pair
            out_ref[member * per + q] = rows_ref[at : at + pair, :].astype(BF16)


def total_kernel(first_ref, second_ref, mixed_ref, input_ref, *, quarters):
    part = input_ref.shape[1] // quarters
    cut = first_ref.shape[2] - part

    def summed(ref, q):
        total = ref[q].astype(F32)
        for j in range(1, ref.shape[0] // quarters):
            total = total + ref[j * quarters + q].astype(F32)
        return total.astype(BF16)

    for q in range(quarters):
        at = q * part
        total = summed(first_ref, q)
        input_ref[:, at : at + part] = total[:, :part]
        mixed_ref[:, at : at + cut] = total[:, part:]
        mixed_ref[:, at + cut : at + part] = summed(second_ref, q)


def ring_reduced(left, right, count, pair):
    height = left.shape[0] // count
    width = left.shape[1] + right.shape[1]
    half, middle = count // 2, width // 256 * 128

    def at(k):
        return [
            ((height, a.shape[1]), functools.partial(lambda k, *_: (k, 0), k)) for a in (left, right)
        ]

    up, down = called_at(
        open_kernel,
        (shape_of((height, middle)), shape_of((height, width - middle))),
        at(half),
        left,
        right,
    )
    for k in range(half - 1, 0, -1):
        up, down = shifted(up, "z", 1), shifted(down, "z", -1)
        up, down = called_at(
            turn_kernel,
            (shape_of((height, width)), shape_of((height, width))),
            [*at(k), *at(count - k), None, None],
            left,
            right,
            left,
            right,
            up,
            down,
        )
    up, down = shifted(up, "z", 1), shifted(down, "z", -1)
    return called_at(
        close_kernel,
        shape_of((height // pair, pair, width)),
        [*at(0), None, None],
        left,
        right,
        up,
        down,
        scratch=[pltpu.VMEM((height, width), F32)],
    )


def local(tokens, upstream, gate_weight, up_weight, down_weight):
    core = lax.axis_index("core")
    tok = lax.axis_index("tok")
    n_z = lax.axis_size("z")
    n_plane = lax.axis_size("y") * lax.axis_size("x")
    n_core = lax.axis_size("core")
    quarters = n_core * lax.axis_size("tok")
    pair, width = tokens.shape
    part = width // quarters
    cut = part // 8 * 3
    units = gate_weight.shape[0]
    n = pair * quarters
    n_line, n_rows = n_z * n, n_plane * n
    count = n_z * n_plane * n
    own_at = (tok * n_core + core).astype(jnp.int32).reshape(1)
    other_at = (tok * n_core + 1 - core).astype(jnp.int32).reshape(1)
    z_index = lax.axis_index("z").astype(jnp.int32).reshape(1)

    first, second = called(
        deal_kernel,
        (
            shape_of((n_plane * quarters, pair, part)),
            shape_of((n_z * quarters, pair, part)),
        ),
        tokens,
        upstream,
        quarters=quarters,
    )
    weights = (gate_weight, up_weight, down_weight)
    column = ((units, part), lambda i, at: (0, at[0]))
    sent = called_at(pack_kernel, shape_of((3 * units, part)), [column] * 3, *weights, index=other_at)
    got = shifted(sent, "core", 1)
    first = exchanged(first, (*PLANE, *PAIRS))
    rows = called(
        merge_kernel, shape_of((n_rows, part)), first, scratch=[pltpu.VMEM((n_rows, part), F32)]
    )
    rows, second = lax.optimization_barrier((rows, second))
    half, middle = n_z // 2, part // 2
    ring = [rows] + [None] * (n_z - 1)
    for k in range(1, half):
        ring[k] = shifted(ring[k - 1], "z", -1)
        ring[-k] = shifted(ring[1 - k], "z", 1)
        if k == 1:
            in_weights, out_weights = called_at(
                weights_kernel,
                (shape_of((4 * units, part)), shape_of((2 * units, part))),
                [column] * 3 + [None],
                *weights,
                got,
                index=own_at,
            )
            ring[1], in_weights, out_weights = lax.optimization_barrier(
                (ring[1], in_weights, out_weights)
            )
    rows = called(
        stack_kernel,
        shape_of((count, part)),
        *(block for k, block in enumerate(ring) if k != half),
        shifted(ring[half - 1][:, :middle], "z", -1),
        shifted(ring[half + 1][:, middle:], "z", 1),
        place=half,
    )
    grads = called(
        merge_from_kernel,
        shape_of((n_plane, n_line, part)),
        z_index,
        exchanged(second, ("z", *PAIRS)),
        specs=[SMEM, VMEM],
        scratch=[pltpu.VMEM((n_line, part), F32)],
        outer=n_z,
    )
    grads = exchanged(grads, PLANE).reshape(n_plane, n_z, n, part)
    grads = grads.swapaxes(0, 1).reshape(count, part)

    gate_up = shifted(by_rows(in_weights[2 * units :], rows), "core", 1)
    gate_up = by_rows(in_weights[: 2 * units], rows) + gate_up
    hidden_grad = shifted(by_rows(out_weights[units:], grads), "core", 1)
    hidden_grad = by_rows(out_weights[:units], grads) + hidden_grad
    own = called(
        middle_kernel,
        shape_of((3 * units, count)),
        gate_up,
        shifted(gate_up, "tok", 1),
        hidden_grad,
        shifted(hidden_grad, "tok", 1),
    )
    in_grads, hidden = called(
        pair_kernel,
        (shape_of((4 * units, count)), shape_of((2 * units, count))),
        own,
        shifted(own, "core", 1),
    )

    rest = by_columns(hidden, out_weights[:, cut:]).astype(BF16)
    rest = rest.reshape(n_z, n_plane, n, part - cut).swapaxes(0, 1)
    rest = rest.reshape(n_plane, n_line, part - cut)
    rest, in_grads, hidden = lax.optimization_barrier((rest, in_grads, hidden))
    rest = called(
        split_from_kernel,
        shape_of((n_z * quarters, pair, part - cut)),
        z_index,
        exchanged(rest, PLANE),
        specs=[SMEM, VMEM],
        scratch=[pltpu.VMEM((n_line, part - cut), F32)],
        outer=n_z,
    )
    rest = exchanged(rest, ("z", *PAIRS))
    summed = ring_reduced(
        by_columns(in_grads, in_weights), by_columns(hidden, out_weights[:, :cut]), n_z, pair
    )
    summed, rest = lax.optimization_barrier((summed, rest))
    mixed, input_grad = called(
        total_kernel,
        (shape_of((pair, width)), shape_of((pair, width))),
        exchanged(summed, (*PLANE, *PAIRS)),
        rest,
        quarters=quarters,
    )

    def product(left, right):
        return jnp.dot(left, right, preferred_element_type=F32).astype(BF16)

    got_in = shifted(product(in_grads[2 * units :], rows), "core", 1)
    got_out = shifted(product(hidden[units:], grads), "core", 1)
    in_weight_grad = product(in_grads[: 2 * units], rows)
    out_weight_grad = product(hidden[:units], grads)

    def side_by_side(mine, others):
        left = jnp.where(core == 0, mine, others)
        right = jnp.where(core == 0, others, mine)
        return jnp.concatenate([left, right], axis=1)

    return (
        mixed,
        input_grad,
        side_by_side(in_weight_grad[:units], got_in[:units]),
        side_by_side(in_weight_grad[units:], got_in[units:]),
        side_by_side(out_weight_grad, got_out),
    )


def solution(mesh):
    finer = Mesh(mesh.devices.reshape(8, 4, 2, 2, mesh.shape["tok"]), AXES)
    return jax.shard_map(
        local,
        mesh=finer,
        in_specs=(P(AXES, None), P(AXES, None), P(BLK, None), P(BLK, None), P(BLK, None)),
        out_specs=(P(AXES, None), P(AXES, None), P(BLK, "tok"), P(BLK, "tok"), P(BLK, "tok")),
        check_vma=False,
    )
```

profile of v0, /device:TPU:1, one launch (start us, length us, event | category | flops | bytes accessed | tf_op | source)
XLA Modules:
  0.0 197.1 jit_solution(4347401581226923946)
XLA Ops:
  3.0 8.6 %all-to-all-start = ((bf16[32,2,2048]{2,1,0:T(2,128)(2,1)}), bf16[32,2,2048]{2,1,0:T(2,128)(2,1)S(1)}, u32[]{:S(2)}, u32[]{:S(2)}) async-start(bf16[32,2,2048]{2,1,0:T(2,128)(2,1)} %get-tuple-element.31), calls=%async_computation | async-start | bytes 524288 | tf_op jit(solution)/shard_map/all_to_all | solution.py:28
  17.5 2.7 %all-to-all-done.blocks_ref = bf16[32,2,2048]{2,1,0:T(2,128)(2,1)S(1)} async-done(((bf16[32,2,2048]{2,1,0:T(2,128)(2,1)}), bf16[32,2,2048]{2,1,0:T(2,128)(2,1)S(1)}, u32[]{:S(2)}, u32[]{:S(2)}) %all-to-all-start) | async-done | bytes 262176 | tf_op jit(solution)/shard_map/all_to_all | solution.py:28
  20.4 9.8 %all-to-all-start.1 = ((bf16[32,2,2048]{2,1,0:T(2,128)(2,1)}), bf16[32,2,2048]{2,1,0:T(2,128)(2,1)S(1)}, u32[]{:S(2)}, u32[]{:S(2)}) async-start(bf16[32,2,2048]{2,1,0:T(2,128)(2,1)} %get-tuple-element.39), calls=%async_computation.1 | async-start | bytes 524288 | tf_op jit(solution)/shard_map/all_to_all | solution.py:28
  30.2 12.9 %all-to-all-done.1.blocks_ref = bf16[32,2,2048]{2,1,0:T(2,128)(2,1)S(1)} async-done(((bf16[32,2,2048]{2,1,0:T(2,128)(2,1)}), bf16[32,2,2048]{2,1,0:T(2,128)(2,1)S(1)}, u32[]{:S(2)}, u32[]{:S(2)}) %all-to-all-start.1) | async-done | bytes 262176 | tf_op jit(solution)/shard_map/all_to_all | solution.py:28
  44.8 4.5 %all-to-all-start.2 = ((bf16[8,64,2048]{2,1,0:T(8,128)(2,1)}), bf16[8,64,2048]{2,1,0:T(8,128)(2,1)}, u32[]{:S(2)}, u32[]{:S(2)}) async-start(bf16[8,64,2048]{2,1,0:T(8,128)(2,1)} %shard_map.97), calls=%async_computation.2 | async-start | bytes 4194304 | tf_op jit(solution)/shard_map/all_to_all | solution.py:28
  49.4 2.6 %collective-permute-start = (bf16[64,2048]{1,0:T(8,128)(2,1)S(1)}, bf16[64,2048]{1,0:T(8,128)(2,1)}, u32[]{:S(2)}, u32[]{:S(2)}) collective-permute-start(bf16[64,2048]{1,0:T(8,128)(2,1)S(1)} %shard_map.93.refs_0_), channel_id=1, source_target_pairs={{0,224},{32,0},{64,32},{96,64},{128,96},{160,128},{192,160},{224,1... | collective-permute-start | bytes 786440 | tf_op jit(solution)/shard_map/ppermute | solution.py:24
  52.0 6.1 %collective-permute-done.4.refs_6_ = bf16[64,2048]{1,0:T(8,128)(2,1)} collective-permute-done((bf16[64,2048]{1,0:T(8,128)(2,1)S(1)}, bf16[64,2048]{1,0:T(8,128)(2,1)}, u32[]{:S(2)}, u32[]{:S(2)}) %collective-permute-start.4) | collective-permute-done | bytes 262176 | tf_op jit(solution)/shard_map/ppermute | solution.py:24
  63.8 2.7 %collective-permute-start.2 = (bf16[64,2048]{1,0:T(8,128)(2,1)}, bf16[64,2048]{1,0:T(8,128)(2,1)S(1)}, u32[]{:S(2)}, u32[]{:S(2)}) collective-permute-start(bf16[64,2048]{1,0:T(8,128)(2,1)} %collective-permute-done.refs_1_), channel_id=1, source_target_pairs={{0,224},{32,0},{64,32},{96,64},{128,96},{160,128},{192,160},{224,1... | collective-permute-start | bytes 786440 | tf_op jit(solution)/shard_map/ppermute | solution.py:24
  66.6 4.4 %collective-permute-done.2.refs_2_ = bf16[64,2048]{1,0:T(8,128)(2,1)S(1)} collective-permute-done((bf16[64,2048]{1,0:T(8,128)(2,1)}, bf16[64,2048]{1,0:T(8,128)(2,1)S(1)}, u32[]{:S(2)}, u32[]{:S(2)}) %collective-permute-start.2) | collective-permute-done | bytes 262176 | tf_op jit(solution)/shard_map/ppermute | solution.py:24
  71.0 3.4 %collective-permute-start.3 = (bf16[64,2048]{1,0:T(8,128)(2,1)S(1)}, bf16[64,2048]{1,0:T(8,128)(2,1)S(1)}, u32[]{:S(2)}, u32[]{:S(2)}) collective-permute-start(bf16[64,2048]{1,0:T(8,128)(2,1)S(1)} %collective-permute-done.2.refs_2_), channel_id=1, source_target_pairs={{0,224},{32,0},{64,32},{96,64},{128,96},{160,128},{192,160},{224,1... | collective-permute-start | bytes 786440 | tf_op jit(solution)/shard_map/ppermute | solution.py:24
  74.5 3.2 %collective-permute-done.3.refs_3_ = bf16[64,2048]{1,0:T(8,128)(2,1)S(1)} collective-permute-done((bf16[64,2048]{1,0:T(8,128)(2,1)S(1)}, bf16[64,2048]{1,0:T(8,128)(2,1)S(1)}, u32[]{:S(2)}, u32[]{:S(2)}) %collective-permute-start.3) | collective-permute-done | bytes 262176 | tf_op jit(solution)/shard_map/ppermute | solution.py:24
  77.7 3.2 %collective-permute-start.7 = (bf16[64,1024]{1,0:T(8,128)(2,1)S(1)}, bf16[64,1024]{1,0:T(8,128)(2,1)S(1)}, u32[]{:S(2)}, u32[]{:S(2)}) collective-permute-start(bf16[64,1024]{1,0:T(8,128)(2,1)S(1)} %slice.64), channel_id=1, source_target_pairs={{0,224},{32,0},{64,32},{96,64},{128,96},{160,128},{192,160},{224,1... | collective-permute-start | bytes 393224 | tf_op jit(solution)/shard_map/ppermute | solution.py:24
  85.6 4.4 %collective-permute-start.9 = (f32[224,512]{1,0:T(8,128)}, f32[224,512]{1,0:T(8,128)S(1)}, u32[]{:S(2)}, u32[]{:S(2)}) collective-permute-start(f32[224,512]{1,0:T(8,128)} %fusion), channel_id=1, source_target_pairs={{0,2},{2,0},{1,3},{3,1},{4,6},{6,4},{5,7},{7,5},{8,10},{10,8},{9,1... | collective-permute-start | bytes 1376264 | tf_op jit(solution)/shard_map/ppermute | solution.py:24
  96.2 2.7 %collective-permute-start.12 = (f32[112,512]{1,0:T(8,128)S(1)}, f32[112,512]{1,0:T(8,128)S(1)}, u32[]{:S(2)}, u32[]{:S(2)}) collective-permute-start(f32[112,512]{1,0:T(8,128)S(1)} %convolution_add_fusion.1.hid_ref), channel_id=1, source_target_pairs={{0,1},{1,0},{2,3},{3,2},{4,5},{5,4},{6,7},{7,6},{8,9},{9,8},{10,11... | collective-permute-start | bytes 688136 | tf_op jit(solution)/shard_map/ppermute | solution.py:24
  99.0 9.8 %collective-permute-done.10.got_ref = f32[224,512]{1,0:T(8,128)S(1)} collective-permute-done((f32[224,512]{1,0:T(8,128)S(1)}, f32[224,512]{1,0:T(8,128)S(1)}, u32[]{:S(2)}, u32[]{:S(2)}) %collective-permute-start.10) | collective-permute-done | bytes 458784 | tf_op jit(solution)/shard_map/ppermute | solution.py:24
  108.7 4.9 %collective-permute-done.12.hid_got_ref = f32[112,512]{1,0:T(8,128)S(1)} collective-permute-done((f32[112,512]{1,0:T(8,128)S(1)}, f32[112,512]{1,0:T(8,128)S(1)}, u32[]{:S(2)}, u32[]{:S(2)}) %collective-permute-start.12) | collective-permute-done | bytes 229408 | tf_op jit(solution)/shard_map/ppermute | solution.py:24
  119.8 4.6 %all-to-all-start.3 = ((bf16[8,64,1280]{2,1,0:T(8,128)(2,1)}), bf16[8,64,1280]{2,1,0:T(8,128)(2,1)S(1)}, u32[]{:S(2)}, u32[]{:S(2)}) async-start(bf16[8,64,1280]{2,1,0:T(8,128)(2,1)} %bitcast.29), calls=%async_computation.3 | async-start | bytes 2621440 | tf_op jit(solution)/shard_map/all_to_all | solution.py:28
  125.0 2.9 %fusion.13.left_ref.la_ref.lb_ref = f32[512,2048]{1,0:T(8,128)S(1)} fusion(bf16[448,512]{1,0:T(8,128)(2,1)} %copy-done.12, bf16[448,2048]{1,0:T(8,128)(2,1)} %copy-done.10), kind=kOutput, calls=%fused_computation.30 | convolution fusion | flops 939524096 | bytes 6488064 | tf_op jit(solution)/shard_map/dot_general | solution.py:36
  128.1 3.4 %collective-permute-start.15 = (bf16[64,1408]{1,0:T(8,128)(2,1)S(1)}, bf16[64,1408]{1,0:T(8,128)(2,1)S(1)}, u32[]{:S(2)}, u32[]{:S(2)}) collective-permute-start(bf16[64,1408]{1,0:T(8,128)(2,1)S(1)} %get-tuple-element.45), channel_id=1, source_target_pairs={{0,224},{32,0},{64,32},{96,64},{128,96},{160,128},{192,160},{224,1... | collective-permute-start | bytes 540680 | tf_op jit(solution)/shard_map/ppermute | solution.py:24
  133.5 2.9 %collective-permute-done.14.came_up_ref = bf16[64,1408]{1,0:T(8,128)(2,1)S(1)} collective-permute-done((bf16[64,1408]{1,0:T(8,128)(2,1)S(1)}, bf16[64,1408]{1,0:T(8,128)(2,1)S(1)}, u32[]{:S(2)}, u32[]{:S(2)}) %collective-permute-start.14) | collective-permute-done | bytes 180256 | tf_op jit(solution)/shard_map/ppermute | solution.py:24
  136.6 2.7 %collective-permute-start.17 = (bf16[64,2816]{1,0:T(8,128)(2,1)S(1)}, bf16[64,2816]{1,0:T(8,128)(2,1)S(1)}, u32[]{:S(2)}, u32[]{:S(2)}) collective-permute-start(bf16[64,2816]{1,0:T(8,128)(2,1)S(1)} %get-tuple-element.47), channel_id=1, source_target_pairs={{0,224},{32,0},{64,32},{96,64},{128,96},{160,128},{192,160},{224,1... | collective-permute-start | bytes 1081352 | tf_op jit(solution)/shard_map/ppermute | solution.py:24
  141.4 5.8 %collective-permute-done.16.came_up_ref = bf16[64,2816]{1,0:T(8,128)(2,1)S(1)} collective-permute-done((bf16[64,2816]{1,0:T(8,128)(2,1)S(1)}, bf16[64,2816]{1,0:T(8,128)(2,1)S(1)}, u32[]{:S(2)}, u32[]{:S(2)}) %collective-permute-start.16) | collective-permute-done | bytes 360480 | tf_op jit(solution)/shard_map/ppermute | solution.py:24
  147.4 2.7 %collective-permute-start.19 = (bf16[64,2816]{1,0:T(8,128)(2,1)S(1)}, bf16[64,2816]{1,0:T(8,128)(2,1)S(1)}, u32[]{:S(2)}, u32[]{:S(2)}) collective-permute-start(bf16[64,2816]{1,0:T(8,128)(2,1)S(1)} %get-tuple-element.49), channel_id=1, source_target_pairs={{0,224},{32,0},{64,32},{96,64},{128,96},{160,128},{192,160},{224,1... | collective-permute-start | bytes 1081352 | tf_op jit(solution)/shard_map/ppermute | solution.py:24
  151.1 6.0 %collective-permute-done.18.came_up_ref = bf16[64,2816]{1,0:T(8,128)(2,1)S(1)} collective-permute-done((bf16[64,2816]{1,0:T(8,128)(2,1)S(1)}, bf16[64,2816]{1,0:T(8,128)(2,1)S(1)}, u32[]{:S(2)}, u32[]{:S(2)}) %collective-permute-start.18) | collective-permute-done | bytes 360480 | tf_op jit(solution)/shard_map/ppermute | solution.py:24
  158.1 2.7 %collective-permute-start.21 = (bf16[64,2816]{1,0:T(8,128)(2,1)}, bf16[64,2816]{1,0:T(8,128)(2,1)}, u32[]{:S(2)}, u32[]{:S(2)}) collective-permute-start(bf16[64,2816]{1,0:T(8,128)(2,1)} %get-tuple-element.51), channel_id=1, source_target_pairs={{0,224},{32,0},{64,32},{96,64},{128,96},{160,128},{192,160},{224,1... | collective-permute-start | bytes 1081352 | tf_op jit(solution)/shard_map/ppermute | solution.py:24
  161.7 7.0 %all-to-all-start.4 = ((bf16[32,2,1280]{2,1,0:T(2,128)(2,1)}), bf16[32,2,1280]{2,1,0:T(2,128)(2,1)S(1)}, u32[]{:S(2)}, u32[]{:S(2)}) async-start(bf16[32,2,1280]{2,1,0:T(2,128)(2,1)} %shard_map.105), calls=%async_computation.4 | async-start | bytes 327680 | tf_op jit(solution)/shard_map/all_to_all | solution.py:28
  168.7 2.5 %broadcast_select_fusion.3 = (bf16[112,2048]{1,0:T(8,128)(2,1)S(1)}, bf16[112,2048]{1,0:T(8,128)(2,1)S(1)}, bf16[112,2048]{1,0:T(8,128)(2,1)}, bf16[112,2048]{1,0:T(8,128)(2,1)}) fusion(pred[]{:T(512)S(6)} %eq.2, bf16[224,2048]{1,0:T(8,128)(2,1)} %collective-permute-done.22, bf16[224,2048]{1,0:T(8,128)(2,1)} %convolution_convert_fusion.2), kind=kLoop, calls=%fused_computation.21 | loop fusion | flops 917504 | bytes 3670017 | tf_op jit(solution)/shard_map/jit(_where)/select_n | solution.py:391
  171.3 2.2 %copy-done.1 = f32[512,2048]{1,0:T(8,128)S(1)} copy-done((f32[512,2048]{1,0:T(8,128)S(1)}, f32[512,2048]{1,0:T(8,128)}, u32[]{:S(2)}) %copy-start.1) | copy-done | bytes 4194328
  175.5 4.6 %all-to-all-done.4.second_ref = bf16[32,2,1280]{2,1,0:T(2,128)(2,1)S(1)} async-done(((bf16[32,2,1280]{2,1,0:T(2,128)(2,1)}), bf16[32,2,1280]{2,1,0:T(2,128)(2,1)S(1)}, u32[]{:S(2)}, u32[]{:S(2)}) %all-to-all-start.4) | async-done | bytes 163872 | tf_op jit(solution)/shard_map/all_to_all | solution.py:28
  180.1 6.6 %all-to-all-start.5 = ((bf16[32,2,2816]{2,1,0:T(2,128)(2,1)}), bf16[32,2,2816]{2,1,0:T(2,128)(2,1)S(1)}, u32[]{:S(2)}, u32[]{:S(2)}) async-start(bf16[32,2,2816]{2,1,0:T(2,128)(2,1)} %shard_map.104), calls=%async_computation.5 | async-start | bytes 720896 | tf_op jit(solution)/shard_map/all_to_all | solution.py:28
  186.8 2.5 %pad_maximum_fusion = (bf16[112,4096]{1,0:T(8,128)(2,1)}, bf16[112,4096]{1,0:T(8,128)(2,1)}) fusion(bf16[112,2048]{1,0:T(8,128)(2,1)S(1)} %get-tuple-element.58, bf16[112,2048]{1,0:T(8,128)(2,1)} %get-tuple-element.60, bf16[112,2048]{1,0:T(8,128)(2,1)} %get-tuple-element.59, bf16[112,2048]{1,0:T(8,128)(2,1)S(1)} %get-tuple-element.57), kind=kLoop, calls=%fused_computation.8 | loop fusion | flops 3670016 | bytes 3670016 | tf_op jit(solution)/shard_map/concatenate | solution.py:393
  189.3 7.1 %all-to-all-done.5.first_ref = bf16[32,2,2816]{2,1,0:T(2,128)(2,1)S(1)} async-done(((bf16[32,2,2816]{2,1,0:T(2,128)(2,1)}), bf16[32,2,2816]{2,1,0:T(2,128)(2,1)S(1)}, u32[]{:S(2)}, u32[]{:S(2)}) %all-to-all-start.5) | async-done | bytes 360480 | tf_op jit(solution)/shard_map/all_to_all | solution.py:28
  (103 shorter events, 43.9 us)
Async XLA Ops:
  3.0 17.2 %all-to-all-start = ((bf16[32,2,2048]{2,1,0:T(2,128)(2,1)}), bf16[32,2,2048]{2,1,0:T(2,128)(2,1)S(1)}, u32[]{:S(2)}, u32[]{:S(2)}) async-start(bf16[32,2,2048]{2,1,0:T(2,128)(2,1)} %get-tuple-element.31), calls=%async_computation | async-start | bytes 524288 | tf_op jit(solution)/shard_map/all_to_all | solution.py:28
  17.3 40.9 %collective-permute-start.1 = (bf16[336,2048]{1,0:T(8,128)(2,1)}, bf16[336,2048]{1,0:T(8,128)(2,1)S(1)}, u32[]{:S(2)}, u32[]{:S(2)}) collective-permute-start(bf16[336,2048]{1,0:T(8,128)(2,1)} %shard_map.94), channel_id=1, source_target_pairs={{0,2},{2,0},{1,3},{3,1},{4,6},{6,4},{5,7},{7,5},{8,10},{10,8},{9,1... | collective-permute-start | bytes 4128776 | tf_op jit(solution)/shard_map/ppermute | solution.py:24
  20.4 22.8 %all-to-all-start.1 = ((bf16[32,2,2048]{2,1,0:T(2,128)(2,1)}), bf16[32,2,2048]{2,1,0:T(2,128)(2,1)S(1)}, u32[]{:S(2)}, u32[]{:S(2)}) async-start(bf16[32,2,2048]{2,1,0:T(2,128)(2,1)} %get-tuple-element.39), calls=%async_computation.1 | async-start | bytes 524288 | tf_op jit(solution)/shard_map/all_to_all | solution.py:28
  44.8 45.2 %all-to-all-start.2 = ((bf16[8,64,2048]{2,1,0:T(8,128)(2,1)}), bf16[8,64,2048]{2,1,0:T(8,128)(2,1)}, u32[]{:S(2)}, u32[]{:S(2)}) async-start(bf16[8,64,2048]{2,1,0:T(8,128)(2,1)} %shard_map.97), calls=%async_computation.2 | async-start | bytes 4194304 | tf_op jit(solution)/shard_map/all_to_all | solution.py:28
  49.3 8.9 %collective-permute-start.4 = (bf16[64,2048]{1,0:T(8,128)(2,1)S(1)}, bf16[64,2048]{1,0:T(8,128)(2,1)}, u32[]{:S(2)}, u32[]{:S(2)}) collective-permute-start(bf16[64,2048]{1,0:T(8,128)(2,1)S(1)} %shard_map.93.refs_0_), channel_id=1, source_target_pairs={{0,32},{32,64},{64,96},{96,128},{128,160},{160,192},{192,224},{224... | collective-permute-start | bytes 786440 | tf_op jit(solution)/shard_map/ppermute | solution.py:24
  49.4 14.4 %collective-permute-start = (bf16[64,2048]{1,0:T(8,128)(2,1)S(1)}, bf16[64,2048]{1,0:T(8,128)(2,1)}, u32[]{:S(2)}, u32[]{:S(2)}) collective-permute-start(bf16[64,2048]{1,0:T(8,128)(2,1)S(1)} %shard_map.93.refs_0_), channel_id=1, source_target_pairs={{0,224},{32,0},{64,32},{96,64},{128,96},{160,128},{192,160},{224,1... | collective-permute-start | bytes 786440 | tf_op jit(solution)/shard_map/ppermute | solution.py:24
  58.1 8.4 %collective-permute-start.5 = (bf16[64,2048]{1,0:T(8,128)(2,1)}, bf16[64,2048]{1,0:T(8,128)(2,1)S(1)}, u32[]{:S(2)}, u32[]{:S(2)}) collective-permute-start(bf16[64,2048]{1,0:T(8,128)(2,1)} %collective-permute-done.4.refs_6_), channel_id=1, source_target_pairs={{0,32},{32,64},{64,96},{96,128},{128,160},{160,192},{192,224},{224... | collective-permute-start | bytes 786440 | tf_op jit(solution)/shard_map/ppermute | solution.py:24
  63.8 20.2 %copy-start.10 = (bf16[448,2048]{1,0:T(8,128)(2,1)}, bf16[448,2048]{1,0:T(8,128)(2,1)S(1)}, u32[]{:S(2)}) copy-start(bf16[448,2048]{1,0:T(8,128)(2,1)S(1)} %get-tuple-element.36) | copy-start | bytes 5505028
  63.8 7.2 %collective-permute-start.2 = (bf16[64,2048]{1,0:T(8,128)(2,1)}, bf16[64,2048]{1,0:T(8,128)(2,1)S(1)}, u32[]{:S(2)}, u32[]{:S(2)}) collective-permute-start(bf16[64,2048]{1,0:T(8,128)(2,1)} %collective-permute-done.refs_1_), channel_id=1, source_target_pairs={{0,224},{32,0},{64,32},{96,64},{128,96},{160,128},{192,160},{224,1... | collective-permute-start | bytes 786440 | tf_op jit(solution)/shard_map/ppermute | solution.py:24
  66.6 7.8 %collective-permute-start.6 = (bf16[64,2048]{1,0:T(8,128)(2,1)S(1)}, bf16[64,2048]{1,0:T(8,128)(2,1)S(1)}, u32[]{:S(2)}, u32[]{:S(2)}) collective-permute-start(bf16[64,2048]{1,0:T(8,128)(2,1)S(1)} %collective-permute-done.5.refs_5_), channel_id=1, source_target_pairs={{0,32},{32,64},{64,96},{96,128},{128,160},{160,192},{192,224},{224... | collective-permute-start | bytes 786440 | tf_op jit(solution)/shard_map/ppermute | solution.py:24
  71.0 6.7 %collective-permute-start.3 = (bf16[64,2048]{1,0:T(8,128)(2,1)S(1)}, bf16[64,2048]{1,0:T(8,128)(2,1)S(1)}, u32[]{:S(2)}, u32[]{:S(2)}) collective-permute-start(bf16[64,2048]{1,0:T(8,128)(2,1)S(1)} %collective-permute-done.2.refs_2_), channel_id=1, source_target_pairs={{0,224},{32,0},{64,32},{96,64},{128,96},{160,128},{192,160},{224,1... | collective-permute-start | bytes 786440 | tf_op jit(solution)/shard_map/ppermute | solution.py:24
  74.4 6.5 %collective-permute-start.8 = (bf16[64,1024]{1,0:T(8,128)(2,1)S(1)}, bf16[64,1024]{1,0:T(8,128)(2,1)S(1)}, u32[]{:S(2)}, u32[]{:S(2)}) collective-permute-start(bf16[64,1024]{1,0:T(8,128)(2,1)S(1)} %slice.65), channel_id=1, source_target_pairs={{0,32},{32,64},{64,96},{96,128},{128,160},{160,192},{192,224},{224... | collective-permute-start | bytes 393224 | tf_op jit(solution)/shard_map/ppermute | solution.py:24
  77.7 5.1 %collective-permute-start.7 = (bf16[64,1024]{1,0:T(8,128)(2,1)S(1)}, bf16[64,1024]{1,0:T(8,128)(2,1)S(1)}, u32[]{:S(2)}, u32[]{:S(2)}) collective-permute-start(bf16[64,1024]{1,0:T(8,128)(2,1)S(1)} %slice.64), channel_id=1, source_target_pairs={{0,224},{32,0},{64,32},{96,64},{128,96},{160,128},{192,160},{224,1... | collective-permute-start | bytes 393224 | tf_op jit(solution)/shard_map/ppermute | solution.py:24
  85.6 7.0 %collective-permute-start.9 = (f32[224,512]{1,0:T(8,128)}, f32[224,512]{1,0:T(8,128)S(1)}, u32[]{:S(2)}, u32[]{:S(2)}) collective-permute-start(f32[224,512]{1,0:T(8,128)} %fusion), channel_id=1, source_target_pairs={{0,2},{2,0},{1,3},{3,1},{4,6},{6,4},{5,7},{7,5},{8,10},{10,8},{9,1... | collective-permute-start | bytes 1376264 | tf_op jit(solution)/shard_map/ppermute | solution.py:24
  92.6 2.9 %collective-permute-start.11 = (f32[112,512]{1,0:T(8,128)S(1)}, f32[112,512]{1,0:T(8,128)S(1)}, u32[]{:S(2)}, u32[]{:S(2)}) collective-permute-start(f32[112,512]{1,0:T(8,128)S(1)} %fusion.4), channel_id=1, source_target_pairs={{0,2},{2,0},{1,3},{3,1},{4,6},{6,4},{5,7},{7,5},{8,10},{10,8},{9,1... | collective-permute-start | bytes 688136 | tf_op jit(solution)/shard_map/ppermute | solution.py:24
  94.8 13.9 %collective-permute-start.10 = (f32[224,512]{1,0:T(8,128)S(1)}, f32[224,512]{1,0:T(8,128)S(1)}, u32[]{:S(2)}, u32[]{:S(2)}) collective-permute-start(f32[224,512]{1,0:T(8,128)S(1)} %convolution_add_fusion.sum_ref), channel_id=1, source_target_pairs={{0,1},{1,0},{2,3},{3,2},{4,5},{5,4},{6,7},{7,6},{8,9},{9,8},{10,11... | collective-permute-start | bytes 1376264 | tf_op jit(solution)/shard_map/ppermute | solution.py:24
  96.2 17.4 %collective-permute-start.12 = (f32[112,512]{1,0:T(8,128)S(1)}, f32[112,512]{1,0:T(8,128)S(1)}, u32[]{:S(2)}, u32[]{:S(2)}) collective-permute-start(f32[112,512]{1,0:T(8,128)S(1)} %convolution_add_fusion.1.hid_ref), channel_id=1, source_target_pairs={{0,1},{1,0},{2,3},{3,2},{4,5},{5,4},{6,7},{7,6},{8,9},{9,8},{10,11... | collective-permute-start | bytes 688136 | tf_op jit(solution)/shard_map/ppermute | solution.py:24
  113.8 2.1 %collective-permute-start.13 = (bf16[336,512]{1,0:T(8,128)(2,1)S(1)}, bf16[336,512]{1,0:T(8,128)(2,1)S(1)}, u32[]{:S(2)}, u32[]{:S(2)}) collective-permute-start(bf16[336,512]{1,0:T(8,128)(2,1)S(1)} %shard_map.98.own_ref), channel_id=1, source_target_pairs={{0,2},{2,0},{1,3},{3,1},{4,6},{6,4},{5,7},{7,5},{8,10},{10,8},{9,1... | collective-permute-start | bytes 1032200 | tf_op jit(solution)/shard_map/ppermute | solution.py:24
  119.8 41.0 %all-to-all-start.3 = ((bf16[8,64,1280]{2,1,0:T(8,128)(2,1)}), bf16[8,64,1280]{2,1,0:T(8,128)(2,1)S(1)}, u32[]{:S(2)}, u32[]{:S(2)}) async-start(bf16[8,64,1280]{2,1,0:T(8,128)(2,1)} %bitcast.29), calls=%async_computation.3 | async-start | bytes 2621440 | tf_op jit(solution)/shard_map/all_to_all | solution.py:28
  124.4 16.5 %collective-permute-start.23 = (bf16[112,2048]{1,0:T(8,128)(2,1)}, bf16[112,2048]{1,0:T(8,128)(2,1)S(1)}, u32[]{:S(2)}, u32[]{:S(2)}) collective-permute-start(bf16[112,2048]{1,0:T(8,128)(2,1)} %convolution_convert_fusion.3), channel_id=1, source_target_pairs={{0,2},{2,0},{1,3},{3,1},{4,6},{6,4},{5,7},{7,5},{8,10},{10,8},{9,1... | collective-permute-start | bytes 1376264 | tf_op jit(solution)/shard_map/ppermute | solution.py:24
  128.0 29.1 %copy-start = (f32[512,2048]{1,0:T(8,128)}, f32[512,2048]{1,0:T(8,128)S(1)}, u32[]{:S(2)}) copy-start(f32[512,2048]{1,0:T(8,128)S(1)} %fusion.13.left_ref.la_ref.lb_ref) | copy-start | bytes 12582916
  128.0 8.4 %collective-permute-start.14 = (bf16[64,1408]{1,0:T(8,128)(2,1)S(1)}, bf16[64,1408]{1,0:T(8,128)(2,1)S(1)}, u32[]{:S(2)}, u32[]{:S(2)}) collective-permute-start(bf16[64,1408]{1,0:T(8,128)(2,1)S(1)} %get-tuple-element.44), channel_id=1, source_target_pairs={{0,32},{32,64},{64,96},{96,128},{128,160},{160,192},{192,224},{224... | collective-permute-start | bytes 540680 | tf_op jit(solution)/shard_map/ppermute | solution.py:24
  128.1 8.3 %collective-permute-start.15 = (bf16[64,1408]{1,0:T(8,128)(2,1)S(1)}, bf16[64,1408]{1,0:T(8,128)(2,1)S(1)}, u32[]{:S(2)}, u32[]{:S(2)}) collective-permute-start(bf16[64,1408]{1,0:T(8,128)(2,1)S(1)} %get-tuple-element.45), channel_id=1, source_target_pairs={{0,224},{32,0},{64,32},{96,64},{128,96},{160,128},{192,160},{224,1... | collective-permute-start | bytes 540680 | tf_op jit(solution)/shard_map/ppermute | solution.py:24
  133.2 35.6 %collective-permute-start.22 = (bf16[224,2048]{1,0:T(8,128)(2,1)}, bf16[224,2048]{1,0:T(8,128)(2,1)}, u32[]{:S(2)}, u32[]{:S(2)}) collective-permute-start(bf16[224,2048]{1,0:T(8,128)(2,1)} %convolution_convert_fusion.1), channel_id=1, source_target_pairs={{0,2},{2,0},{1,3},{3,1},{4,6},{6,4},{5,7},{7,5},{8,10},{10,8},{9,1... | collective-permute-start | bytes 2752520 | tf_op jit(solution)/shard_map/ppermute | solution.py:24
  136.5 10.7 %collective-permute-start.16 = (bf16[64,2816]{1,0:T(8,128)(2,1)S(1)}, bf16[64,2816]{1,0:T(8,128)(2,1)S(1)}, u32[]{:S(2)}, u32[]{:S(2)}) collective-permute-start(bf16[64,2816]{1,0:T(8,128)(2,1)S(1)} %get-tuple-element.46), channel_id=1, source_target_pairs={{0,32},{32,64},{64,96},{96,128},{128,160},{160,192},{192,224},{224... | collective-permute-start | bytes 1081352 | tf_op jit(solution)/shard_map/ppermute | solution.py:24
  136.6 10.6 %collective-permute-start.17 = (bf16[64,2816]{1,0:T(8,128)(2,1)S(1)}, bf16[64,2816]{1,0:T(8,128)(2,1)S(1)}, u32[]{:S(2)}, u32[]{:S(2)}) collective-permute-start(bf16[64,2816]{1,0:T(8,128)(2,1)S(1)} %get-tuple-element.47), channel_id=1, source_target_pairs={{0,224},{32,0},{64,32},{96,64},{128,96},{160,128},{192,160},{224,1... | collective-permute-start | bytes 1081352 | tf_op jit(solution)/shard_map/ppermute | solution.py:24
  147.3 9.7 %collective-permute-start.18 = (bf16[64,2816]{1,0:T(8,128)(2,1)S(1)}, bf16[64,2816]{1,0:T(8,128)(2,1)S(1)}, u32[]{:S(2)}, u32[]{:S(2)}) collective-permute-start(bf16[64,2816]{1,0:T(8,128)(2,1)S(1)} %get-tuple-element.48), channel_id=1, source_target_pairs={{0,32},{32,64},{64,96},{96,128},{128,160},{160,192},{192,224},{224... | collective-permute-start | bytes 1081352 | tf_op jit(solution)/shard_map/ppermute | solution.py:24
  147.4 9.7 %collective-permute-start.19 = (bf16[64,2816]{1,0:T(8,128)(2,1)S(1)}, bf16[64,2816]{1,0:T(8,128)(2,1)S(1)}, u32[]{:S(2)}, u32[]{:S(2)}) collective-permute-start(bf16[64,2816]{1,0:T(8,128)(2,1)S(1)} %get-tuple-element.49), channel_id=1, source_target_pairs={{0,224},{32,0},{64,32},{96,64},{128,96},{160,128},{192,160},{224,1... | collective-permute-start | bytes 1081352 | tf_op jit(solution)/shard_map/ppermute | solution.py:24
  158.1 13.2 %collective-permute-start.20 = (bf16[64,2816]{1,0:T(8,128)(2,1)}, bf16[64,2816]{1,0:T(8,128)(2,1)S(1)}, u32[]{:S(2)}, u32[]{:S(2)}) collective-permute-start(bf16[64,2816]{1,0:T(8,128)(2,1)} %get-tuple-element.50), channel_id=1, source_target_pairs={{0,32},{32,64},{64,96},{96,128},{128,160},{160,192},{192,224},{224... | collective-permute-start | bytes 1081352 | tf_op jit(solution)/shard_map/ppermute | solution.py:24
  158.1 13.2 %collective-permute-start.21 = (bf16[64,2816]{1,0:T(8,128)(2,1)}, bf16[64,2816]{1,0:T(8,128)(2,1)}, u32[]{:S(2)}, u32[]{:S(2)}) collective-permute-start(bf16[64,2816]{1,0:T(8,128)(2,1)} %get-tuple-element.51), channel_id=1, source_target_pairs={{0,224},{32,0},{64,32},{96,64},{128,96},{160,128},{192,160},{224,1... | collective-permute-start | bytes 1081352 | tf_op jit(solution)/shard_map/ppermute | solution.py:24
  161.7 18.4 %all-to-all-start.4 = ((bf16[32,2,1280]{2,1,0:T(2,128)(2,1)}), bf16[32,2,1280]{2,1,0:T(2,128)(2,1)S(1)}, u32[]{:S(2)}, u32[]{:S(2)}) async-start(bf16[32,2,1280]{2,1,0:T(2,128)(2,1)} %shard_map.105), calls=%async_computation.4 | async-start | bytes 327680 | tf_op jit(solution)/shard_map/all_to_all | solution.py:28
  180.1 16.2 %all-to-all-start.5 = ((bf16[32,2,2816]{2,1,0:T(2,128)(2,1)}), bf16[32,2,2816]{2,1,0:T(2,128)(2,1)S(1)}, u32[]{:S(2)}, u32[]{:S(2)}) async-start(bf16[32,2,2816]{2,1,0:T(2,128)(2,1)} %shard_map.104), calls=%async_computation.5 | async-start | bytes 720896 | tf_op jit(solution)/shard_map/all_to_all | solution.py:28
  (19 other events, 58.2 us)
where the time goes:
time: 198 us; the launch traced here: 197 us
  starting transfers between devices  74.8 us (38%)
  waiting for transfers between devices  73.7 us (37%)
  local copies, waits for them, and re-layouts  18.3 us (9%)
  matrix products  12.8 us (6%)
  Pallas kernels  10.4 us (5%)
  other arithmetic  6.04 us (3%)
    ppermute x24, waiting for transfers between devices, shifted(): lax.ppermute(block, axis, [(i, (i + distance) % count) for i in range(cou...  46.4 us
    all_to_all x6, starting transfers between devices, exchanged(): return lax.all_to_all(blocks, axes, 0, 0, tiled=True)  41.1 us
    ppermute x24, starting transfers between devices, shifted(): lax.ppermute(block, axis, [(i, (i + distance) % count) for i in range(cou...  33.7 us
    all_to_all x6, waiting for transfers between devices, exchanged(): return lax.all_to_all(blocks, axes, 0, 0, tiled=True)  27.3 us
    unnamed x42, local copies, waits for them, and re-layouts  15.4 us
    pallas_call x8, Pallas kernels, called(): pl.pallas_call(functools.partial(kernel, **kwargs), out_shape=out_shape,...  5.7 us
    dot_general x4, matrix products, product(): return jnp.dot(left, right, preferred_element_type=F32).astype(BF16)  4.95 us
    pallas_call x7, Pallas kernels, called_at(): pl.pallas_call(functools.partial(kernel, **kwargs), out_shape=out_shape,...  4.71 us
  transfers between devices with their start and end apart: 30, of which 14 were waited for; matrix products, arithmetic and copies ran while one was open for 9% of the time, Pallas kernels for 4%

commit v1 on v0

--- a/solution.py
+++ b/solution.py
@@ -16,7 +16,8 @@
 BF16 = jnp.bfloat16
 VMEM = pl.BlockSpec(memory_space=pltpu.VMEM)
 SMEM = pl.BlockSpec(memory_space=pltpu.SMEM)
-PARAMS = pltpu.CompilerParams(vmem_limit_bytes=40 * 1024 * 1024)
+PARAMS = pltpu.CompilerParams(vmem_limit_bytes=20 * 1024 * 1024)
+LARGE = pltpu.CompilerParams(vmem_limit_bytes=58 * 1024 * 1024)
 
 
 def shifted(block, axis, distance):
@@ -36,7 +37,7 @@
     return lax.dot_general(left, right, (((0,), (0,)), ((), ())), preferred_element_type=F32)
 
 
-def called(kernel, out_shape, *args, specs=None, scratch=(), **kwargs):
+def called(kernel, out_shape, *args, specs=None, scratch=(), params=PARAMS, **kwargs):
     specs = specs or [VMEM] * len(args)
     return pl.pallas_call(
         functools.partial(kernel, **kwargs),
@@ -44,11 +45,11 @@
         in_specs=specs,
         out_specs=jax.tree.map(lambda _: VMEM, out_shape),
         scratch_shapes=scratch,
-        compiler_params=PARAMS,
+        compiler_params=params,
     )(*args)
 
 
-def called_at(kernel, out_shape, places, *args, index=None, scratch=(), **kwargs):
+def called_at(kernel, out_shape, places, *args, index=None, scratch=(), params=PARAMS, **kwargs):
     def whole(shape):
         return pl.BlockSpec(shape, lambda *_: (0,) * len(shape))
 
@@ -67,7 +68,7 @@
         functools.partial(kernel, **kwargs),
         out_shape=out_shape,
         grid_spec=grid,
-        compiler_params=PARAMS,
+        compiler_params=params,
     )(jnp.zeros((1,), jnp.int32) if index is None else index, *args)
 
 
@@ -77,13 +78,17 @@
 
 def deal_kernel(tokens_ref, upstream_ref, first_ref, second_ref, *, quarters):
     part = tokens_ref.shape[1] // quarters
+    cut = first_ref.shape[2] - part
     for q in range(quarters):
-        rows = tokens_ref[:, q * part : (q + 1) * part]
-        grads = upstream_ref[:, q * part : (q + 1) * part]
+        at = q * part
+        rows = tokens_ref[:, at : at + part]
+        grads = upstream_ref[:, at : at + cut]
+        rest = upstream_ref[:, at + cut : at + part]
         for j in range(first_ref.shape[0] // quarters):
-            first_ref[j * quarters + q] = rows
+            first_ref[j * quarters + q, :, :part] = rows
+            first_ref[j * quarters + q, :, part:] = grads
         for j in range(second_ref.shape[0] // quarters):
-            second_ref[j * quarters + q] = grads
+            second_ref[j * quarters + q] = rest
 
 
 def merge_kernel(blocks_ref, out_ref, rows_ref):
@@ -106,15 +111,24 @@
         out_ref[j] = rows
 
 
-def stack_kernel(*refs, place):
-    *block_refs, left_ref, right_ref, out_ref = refs
-    height = left_ref.shape[0]
-    middle = left_ref.shape[1]
+def stack_kernel(*refs, place, n):
+    *block_refs, left_ref, right_ref, rest_ref, rows_ref, grads_ref = refs
+    height, middle = left_ref.shape
+    part = rows_ref.shape[1]
+    cut = block_refs[0].shape[1] - part
     places = [k for k in range(len(block_refs) + 1) if k != place]
     for k, block_ref in zip(places, block_refs, strict=True):
-        out_ref[k * height : (k + 1) * height, :] = block_ref[...]
-    out_ref[place * height : (place + 1) * height, :middle] = left_ref[...]
-    out_ref[place * height : (place + 1) * height, middle:] = right_ref[...]
+        at = slice(k * height, (k + 1) * height)
+        rows_ref[at, :] = block_ref[:, :part]
+        grads_ref[at, :cut] = block_ref[:, part:]
+    at = slice(place * height, (place + 1) * height)
+    rows_ref[at, :middle] = left_ref[...]
+    rows_ref[at, middle:] = right_ref[:, : part - middle]
+    grads_ref[at, :cut] = right_ref[:, part - middle :]
+    for k in range(len(block_refs) + 1):
+        for j in range(rest_ref.shape[0]):
+            at = k * height + j * n
+            grads_ref[at : at + n, cut:] = rest_ref[j, k * n : (k + 1) * n, :]
 
 
 def pack_kernel(_, gate_ref, up_ref, down_ref, out_ref):
@@ -134,9 +148,9 @@
 
 def middle_kernel(sum_ref, got_ref, hid_ref, hid_got_ref, out_ref):
     units = hid_ref.shape[0]
-    gate_value = sum_ref[:units, :] + got_ref[:units, :]
-    up_value = sum_ref[units:, :] + got_ref[units:, :]
-    hidden_grad = hid_ref[...] + hid_got_ref[...]
+    gate_value = sum_ref[:units, :] + got_ref[:units, :].astype(F32)
+    up_value = sum_ref[units:, :] + got_ref[units:, :].astype(F32)
+    hidden_grad = hid_ref[...] + hid_got_ref[...].astype(F32)
     gate_sigmoid = jax.nn.sigmoid(gate_value)
     swish_gate = gate_value * gate_sigmoid
     gate_grad = hidden_grad * up_value * gate_sigmoid * (1.0 + gate_value * (1.0 - gate_sigmoid))
@@ -200,7 +214,7 @@
 
 
 def total_kernel(first_ref, second_ref, mixed_ref, input_ref, *, quarters):
-    part = input_ref.shape[1] // quarters
+    part = mixed_ref.shape[1] // quarters
     cut = first_ref.shape[2] - part
 
     def summed(ref, q):
@@ -212,12 +226,12 @@
     for q in range(quarters):
         at = q * part
         total = summed(first_ref, q)
-        input_ref[:, at : at + part] = total[:, :part]
-        mixed_ref[:, at : at + cut] = total[:, part:]
-        mixed_ref[:, at + cut : at + part] = summed(second_ref, q)
-
-
-def ring_reduced(left, right, count, pair):
+        mixed_ref[:, at : at + part] = total[:, :part]
+        input_ref[:, at : at + cut] = total[:, part:]
+        input_ref[:, at + cut : at + part] = summed(second_ref, q)
+
+
+def ring_reduced(left, right, count, pair, beside):
     height = left.shape[0] // count
     width = left.shape[1] + right.shape[1]
     half, middle = count // 2, width // 256 * 128
@@ -236,6 +250,8 @@
     )
     for k in range(half - 1, 0, -1):
         up, down = shifted(up, "z", 1), shifted(down, "z", -1)
+        if k == 1:
+            up, down, beside = lax.optimization_barrier((up, down, beside))
         up, down = called_at(
             turn_kernel,
             (shape_of((height, width)), shape_of((height, width))),
@@ -248,7 +264,7 @@
             down,
         )
     up, down = shifted(up, "z", 1), shifted(down, "z", -1)
-    return called_at(
+    summed = called_at(
         close_kernel,
         shape_of((height // pair, pair, width)),
         [*at(0), None, None],
@@ -258,6 +274,7 @@
         down,
         scratch=[pltpu.VMEM((height, width), F32)],
     )
+    return summed, beside
 
 
 def local(tokens, upstream, gate_weight, up_weight, down_weight):
@@ -269,7 +286,8 @@
     quarters = n_core * lax.axis_size("tok")
     pair, width = tokens.shape
     part = width // quarters
-    cut = part // 8 * 3
+    cut = part // 8 * 4
+    turn = part // 8 * 3
     units = gate_weight.shape[0]
     n = pair * quarters
     n_line, n_rows = n_z * n, n_plane * n
@@ -281,58 +299,61 @@
     first, second = called(
         deal_kernel,
         (
-            shape_of((n_plane * quarters, pair, part)),
-            shape_of((n_z * quarters, pair, part)),
+            shape_of((n_plane * quarters, pair, part + cut)),
+            shape_of((n_z * quarters, pair, part - cut)),
         ),
         tokens,
         upstream,
         quarters=quarters,
     )
-    weights = (gate_weight, up_weight, down_weight)
+    first, *weights = lax.optimization_barrier((first, gate_weight, up_weight, down_weight))
     column = ((units, part), lambda i, at: (0, at[0]))
-    sent = called_at(pack_kernel, shape_of((3 * units, part)), [column] * 3, *weights, index=other_at)
+    sent = called_at(pack_kernel, shape_of((3 * units, part)), [column] * 3, *weights, index=other_at, params=LARGE)
     got = shifted(sent, "core", 1)
     first = exchanged(first, (*PLANE, *PAIRS))
+    in_weights, out_weights = called_at(
+        weights_kernel,
+        (shape_of((4 * units, part)), shape_of((2 * units, part))),
+        [column] * 3 + [None],
+        *weights,
+        got,
+        index=own_at,
+        params=LARGE,
+    )
+    first, in_weights, out_weights = lax.optimization_barrier((first, in_weights, out_weights))
     rows = called(
-        merge_kernel, shape_of((n_rows, part)), first, scratch=[pltpu.VMEM((n_rows, part), F32)]
+        merge_kernel,
+        shape_of((n_rows, part + cut)),
+        first,
+        scratch=[pltpu.VMEM((n_rows, part + cut), F32)],
     )
     rows, second = lax.optimization_barrier((rows, second))
-    half, middle = n_z // 2, part // 2
+    half, middle = n_z // 2, (part + cut) // 256 * 128
     ring = [rows] + [None] * (n_z - 1)
     for k in range(1, half):
         ring[k] = shifted(ring[k - 1], "z", -1)
         ring[-k] = shifted(ring[1 - k], "z", 1)
-        if k == 1:
-            in_weights, out_weights = called_at(
-                weights_kernel,
-                (shape_of((4 * units, part)), shape_of((2 * units, part))),
-                [column] * 3 + [None],
-                *weights,
-                got,
-                index=own_at,
-            )
-            ring[1], in_weights, out_weights = lax.optimization_barrier(
-                (ring[1], in_weights, out_weights)
-            )
-    rows = called(
+    rest = called(
+        merge_from_kernel,
+        shape_of((n_plane, n_line, part - cut)),
+        z_index,
+        exchanged(second, ("z", *PAIRS)),
+        specs=[SMEM, VMEM],
+        scratch=[pltpu.VMEM((n_line, part - cut), F32)],
+        outer=n_z,
+    )
+    rest = exchanged(rest, PLANE)
+    rows, grads = called(
         stack_kernel,
-        shape_of((count, part)),
+        (shape_of((count, part)), shape_of((count, part))),
         *(block for k, block in enumerate(ring) if k != half),
         shifted(ring[half - 1][:, :middle], "z", -1),
         shifted(ring[half + 1][:, middle:], "z", 1),
+        rest,
         place=half,
-    )
-    grads = called(
-        merge_from_kernel,
-        shape_of((n_plane, n_line, part)),
-        z_index,
-        exchanged(second, ("z", *PAIRS)),
-        specs=[SMEM, VMEM],
-        scratch=[pltpu.VMEM((n_line, part), F32)],
-        outer=n_z,
-    )
-    grads = exchanged(grads, PLANE).reshape(n_plane, n_z, n, part)
-    grads = grads.swapaxes(0, 1).reshape(count, part)
+        n=n,
+        params=LARGE,
+    )
 
     gate_up = shifted(by_rows(in_weights[2 * units :], rows), "core", 1)
     gate_up = by_rows(in_weights[: 2 * units], rows) + gate_up
@@ -342,9 +363,9 @@
         middle_kernel,
         shape_of((3 * units, count)),
         gate_up,
-        shifted(gate_up, "tok", 1),
+        shifted(gate_up.astype(BF16), "tok", 1),
         hidden_grad,
-        shifted(hidden_grad, "tok", 1),
+        shifted(hidden_grad.astype(BF16), "tok", 1),
     )
     in_grads, hidden = called(
         pair_kernel,
@@ -353,23 +374,27 @@
         shifted(own, "core", 1),
     )
 
-    rest = by_columns(hidden, out_weights[:, cut:]).astype(BF16)
-    rest = rest.reshape(n_z, n_plane, n, part - cut).swapaxes(0, 1)
-    rest = rest.reshape(n_plane, n_line, part - cut)
+    rest = by_columns(in_grads, in_weights[:, turn:]).astype(BF16)
+    rest = rest.reshape(n_z, n_plane, n, part - turn).swapaxes(0, 1)
+    rest = rest.reshape(n_plane, n_line, part - turn)
     rest, in_grads, hidden = lax.optimization_barrier((rest, in_grads, hidden))
     rest = called(
         split_from_kernel,
-        shape_of((n_z * quarters, pair, part - cut)),
+        shape_of((n_z * quarters, pair, part - turn)),
         z_index,
         exchanged(rest, PLANE),
         specs=[SMEM, VMEM],
-        scratch=[pltpu.VMEM((n_line, part - cut), F32)],
+        scratch=[pltpu.VMEM((n_line, part - turn), F32)],
         outer=n_z,
     )
+    summed, rest = ring_reduced(
+        by_columns(hidden, out_weights),
+        by_columns(in_grads, in_weights[:, :turn]),
+        n_z,
+        pair,
+        rest,
+    )
     rest = exchanged(rest, ("z", *PAIRS))
-    summed = ring_reduced(
-        by_columns(in_grads, in_weights), by_columns(hidden, out_weights[:, :cut]), n_z, pair
-    )
     summed, rest = lax.optimization_barrier((summed, rest))
     mixed, input_grad = called(
         total_kernel,

time: 198 us -> 188 us (0.949)
  waiting for transfers between devices: 73.7 us -> 63.2 us
  local copies, waits for them, and re-layouts: 18.3 us -> 9.64 us
  Pallas kernels: 10.4 us -> 18 us
  matrix products: 12.8 us -> 16.8 us
    all_to_all x6, waiting for transfers between devices: 27.3 us -> 19.3 us  [exchanged(): return lax.all_to_all(blocks, axes, 0, 0, tiled=True)]
    unnamed x42 -> x48, local copies, waits for them, and re-layouts: 15.4 us -> 7.73 us
    pallas_call x7, Pallas kernels: 4.71 us -> 9.32 us  [called_at(): pl.pallas_call(functools.partial(kernel, **kwargs), out_shape=out_shape,...]
    all_to_all x6, starting transfers between devices: 41.1 us -> 37 us  [exchanged(): return lax.all_to_all(blocks, axes, 0, 0, tiled=True)]
    pallas_call x8, Pallas kernels: 5.7 us -> 8.67 us  [called(): pl.pallas_call(functools.partial(kernel, **kwargs), out_shape=out_shape,...]
    dot_general x3, matrix products: 3.88 us -> 6.62 us  [by_columns(): lax.dot_general(left, right, (((0,), (0,)), ((), ())), preferred_element_...]
    ppermute x24, waiting for transfers between devices: 46.4 us -> 43.9 us  [shifted(): lax.ppermute(block, axis, [(i, (i + distance) % count) for i in range(cou...]
    ppermute x24, starting transfers between devices: 33.7 us -> 36 us  [shifted(): lax.ppermute(block, axis, [(i, (i + distance) % count) for i in range(cou...]
  transfers between devices with their start and end apart: 30 -> 30, of which waited for: 14 -> 14; matrix products, arithmetic and copies ran while one was open for 9% -> 7% of each run, Pallas kernels for 4% -> 5%
where the time goes in v1:
time: 188 us; the launch traced here: 187 us
  starting transfers between devices  73 us (39%)
  waiting for transfers between devices  63.2 us (34%)
  Pallas kernels  18 us (10%)
  matrix products  16.8 us (9%)
  local copies, waits for them, and re-layouts  9.64 us (5%)
  other arithmetic  5.61 us (3%)
    ppermute x24, waiting for transfers between devices, shifted(): lax.ppermute(block, axis, [(i, (i + distance) % count) for i in range(cou...  43.9 us
    all_to_all x6, starting transfers between devices, exchanged(): return lax.all_to_all(blocks, axes, 0, 0, tiled=True)  37 us
    ppermute x24, starting transfers between devices, shifted(): lax.ppermute(block, axis, [(i, (i + distance) % count) for i in range(cou...  36 us
    all_to_all x6, waiting for transfers between devices, exchanged(): return lax.all_to_all(blocks, axes, 0, 0, tiled=True)  19.3 us
    pallas_call x7, Pallas kernels, called_at(): pl.pallas_call(functools.partial(kernel, **kwargs), out_shape=out_shape,...  9.32 us
    pallas_call x8, Pallas kernels, called(): pl.pallas_call(functools.partial(kernel, **kwargs), out_shape=out_shape,...  8.67 us
    unnamed x48, local copies, waits for them, and re-layouts  7.73 us
    dot_general x3, matrix products, by_columns(): lax.dot_general(left, right, (((0,), (0,)), ((), ())), preferred_element_...  6.62 us
  transfers between devices with their start and end apart: 30, of which 14 were waited for; matrix products, arithmetic and copies ran while one was open for 7% of the time, Pallas kernels for 5%

profile of v1, /device:TPU:1, one launch (start us, length us, event | category | flops | bytes accessed | tf_op | source)
XLA Modules:
  0.0 187.2 jit_solution(15404530570271494956)
XLA Ops:
  3.0 2.5 %shard_map.93 = bf16[336,2048]{1,0:T(8,128)(2,1)} custom-call(s32[1]{0:T(128)} %bitcast.1._, bf16[112,8192]{1,0:T(8,128)(2,1)} %gate_ref.1, bf16[112,8192]{1,0:T(8,128)(2,1)} %up_ref.1, bf16[112,8192]{1,0:T(8,128)(2,1)} %down_ref.1), custom_call_target="tpu_custom_call" | custom-call | tf_op jit(solution)/shard_map/pallas_call | solution.py:67
  5.5 3.2 %collective-permute-start = (bf16[336,2048]{1,0:T(8,128)(2,1)}, bf16[336,2048]{1,0:T(8,128)(2,1)S(1)}, u32[]{:S(2)}, u32[]{:S(2)}) collective-permute-start(bf16[336,2048]{1,0:T(8,128)(2,1)} %shard_map.93), channel_id=1, source_target_pairs={{0,2},{2,0},{1,3},{3,1},{4,6},{6,4},{5,7},{7,5},{8,10},{10,8},{9,1... | collective-permute-start | bytes 4128776 | tf_op jit(solution)/shard_map/ppermute | solution.py:25
  8.7 5.5 %all-to-all-start = ((bf16[32,2,3072]{2,1,0:T(2,128)(2,1)}), bf16[32,2,3072]{2,1,0:T(2,128)(2,1)S(1)}, u32[]{:S(2)}, u32[]{:S(2)}) async-start(bf16[32,2,3072]{2,1,0:T(2,128)(2,1)} %get-tuple-element.41), calls=%async_computation | async-start | bytes 786432 | tf_op jit(solution)/shard_map/all_to_all | solution.py:29
  15.3 3.4 %shard_map.94 = (bf16[448,2048]{1,0:T(8,128)(2,1)}, bf16[224,2048]{1,0:T(8,128)(2,1)}) custom-call(s32[1]{0:T(128)} %bitcast._, bf16[112,8192]{1,0:T(8,128)(2,1)} %gate_ref.1, bf16[112,8192]{1,0:T(8,128)(2,1)} %up_ref.1, bf16[112,8192]{1,0:T(8,128)(2,1)} %down_ref.1, bf16[336,2048]{1,0:T(8,128)(2,1)} %copy-done.17), custom_call_target="tpu_custom_call" | custom-call | tf_op jit(solution)/shard_map/pallas_call | solution.py:67
  18.7 5.4 %all-to-all-done.blocks_ref = bf16[32,2,3072]{2,1,0:T(2,128)(2,1)S(1)} async-done(((bf16[32,2,3072]{2,1,0:T(2,128)(2,1)}), bf16[32,2,3072]{2,1,0:T(2,128)(2,1)S(1)}, u32[]{:S(2)}, u32[]{:S(2)}) %all-to-all-start) | async-done | bytes 393248 | tf_op jit(solution)/shard_map/all_to_all | solution.py:29
  26.1 4.0 %collective-permute-start.1 = (bf16[64,3072]{1,0:T(8,128)(2,1)S(1)}, bf16[64,3072]{1,0:T(8,128)(2,1)S(1)}, u32[]{:S(2)}, u32[]{:S(2)}) collective-permute-start(bf16[64,3072]{1,0:T(8,128)(2,1)S(1)} %shard_map.95.refs_0_), channel_id=1, source_target_pairs={{0,224},{32,0},{64,32},{96,64},{128,96},{160,128},{192,160},{224,1... | collective-permute-start | bytes 1179656 | tf_op jit(solution)/shard_map/ppermute | solution.py:25
  30.1 7.4 %all-to-all-start.1 = ((bf16[32,2,1024]{2,1,0:T(2,128)(2,1)}), bf16[32,2,1024]{2,1,0:T(2,128)(2,1)S(1)}, u32[]{:S(2)}, u32[]{:S(2)}) async-start(bf16[32,2,1024]{2,1,0:T(2,128)(2,1)} %get-tuple-element.51), calls=%async_computation.1 | async-start | bytes 262144 | tf_op jit(solution)/shard_map/all_to_all | solution.py:29
  39.3 2.7 %collective-permute-start.2 = (bf16[64,3072]{1,0:T(8,128)(2,1)S(1)}, bf16[64,3072]{1,0:T(8,128)(2,1)}, u32[]{:S(2)}, u32[]{:S(2)}) collective-permute-start(bf16[64,3072]{1,0:T(8,128)(2,1)S(1)} %collective-permute-done.1.refs_1_), channel_id=1, source_target_pairs={{0,224},{32,0},{64,32},{96,64},{128,96},{160,128},{192,160},{224,1... | collective-permute-start | bytes 1179656 | tf_op jit(solution)/shard_map/ppermute | solution.py:25
  41.9 6.6 %all-to-all-done.1.blocks_ref = bf16[32,2,1024]{2,1,0:T(2,128)(2,1)S(1)} async-done(((bf16[32,2,1024]{2,1,0:T(2,128)(2,1)}), bf16[32,2,1024]{2,1,0:T(2,128)(2,1)S(1)}, u32[]{:S(2)}, u32[]{:S(2)}) %all-to-all-start.1) | async-done | bytes 131104 | tf_op jit(solution)/shard_map/all_to_all | solution.py:29
  49.7 3.6 %all-to-all-start.2 = ((bf16[8,64,1024]{2,1,0:T(8,128)(2,1)}), bf16[8,64,1024]{2,1,0:T(8,128)(2,1)S(1)}, u32[]{:S(2)}, u32[]{:S(2)}) async-start(bf16[8,64,1024]{2,1,0:T(8,128)(2,1)} %shard_map.96), calls=%async_computation.2 | async-start | bytes 2097152 | tf_op jit(solution)/shard_map/all_to_all | solution.py:29
  53.7 2.3 %collective-permute-start.3 = (bf16[64,3072]{1,0:T(8,128)(2,1)}, bf16[64,3072]{1,0:T(8,128)(2,1)S(1)}, u32[]{:S(2)}, u32[]{:S(2)}) collective-permute-start(bf16[64,3072]{1,0:T(8,128)(2,1)} %collective-permute-done.2.refs_2_), channel_id=1, source_target_pairs={{0,224},{32,0},{64,32},{96,64},{128,96},{160,128},{192,160},{224,1... | collective-permute-start | bytes 1179656 | tf_op jit(solution)/shard_map/ppermute | solution.py:25
  56.0 9.2 %collective-permute-done.6.refs_4_ = bf16[64,3072]{1,0:T(8,128)(2,1)S(1)} collective-permute-done((bf16[64,3072]{1,0:T(8,128)(2,1)S(1)}, bf16[64,3072]{1,0:T(8,128)(2,1)S(1)}, u32[]{:S(2)}, u32[]{:S(2)}) %collective-permute-start.6) | collective-permute-done | bytes 393248 | tf_op jit(solution)/shard_map/ppermute | solution.py:25
  66.1 2.7 %collective-permute-start.7 = (bf16[64,1536]{1,0:T(8,128)(2,1)S(1)}, bf16[64,1536]{1,0:T(8,128)(2,1)S(1)}, u32[]{:S(2)}, u32[]{:S(2)}) collective-permute-start(bf16[64,1536]{1,0:T(8,128)(2,1)S(1)} %slice.64), channel_id=1, source_target_pairs={{0,224},{32,0},{64,32},{96,64},{128,96},{160,128},{192,160},{224,1... | collective-permute-start | bytes 589832 | tf_op jit(solution)/shard_map/ppermute | solution.py:25
  69.0 4.1 %collective-permute-done.8.refs_8_ = bf16[64,1536]{1,0:T(8,128)(2,1)} collective-permute-done((bf16[64,1536]{1,0:T(8,128)(2,1)}, bf16[64,1536]{1,0:T(8,128)(2,1)}, u32[]{:S(2)}, u32[]{:S(2)}) %collective-permute-start.8) | collective-permute-done | bytes 196640 | tf_op jit(solution)/shard_map/ppermute | solution.py:25
  73.9 4.5 %shard_map.97 = (bf16[512,2048]{1,0:T(8,128)(2,1)}, bf16[512,2048]{1,0:T(8,128)(2,1)}) custom-call(bf16[64,3072]{1,0:T(8,128)(2,1)} %copy-done.2, bf16[64,3072]{1,0:T(8,128)(2,1)} %copy-done.21, bf16[64,3072]{1,0:T(8,128)(2,1)} %collective-permute-done.2.refs_2_, bf16[64,3072]{1,0:T(8,128)(2,1)} %copy-done.19, bf16[64,3072]{1,0:T(8,128)(2,1)} %copy-done.18, ...), custom_call_target="tpu_custom_call" | custom-call | tf_op jit(solution)/shard_map/pallas_call | solution.py:42
  78.4 2.8 %fusion.1 = f32[224,512]{1,0:T(8,128)S(1)} fusion(bf16[512,2048]{1,0:T(8,128)(2,1)} %get-tuple-element.52, bf16[448,2048]{1,0:T(8,128)(2,1)} %get-tuple-element.47), kind=kOutput, calls=%fused_computation.12 | convolution fusion | flops 469762048 | bytes 3473408 | tf_op jit(solution)/shard_map/dot_general | solution.py:33
  89.5 6.9 %collective-permute-done.12.hid_got_ref = bf16[112,512]{1,0:T(8,128)(2,1)S(1)} collective-permute-done((bf16[112,512]{1,0:T(8,128)(2,1)S(1)}, bf16[112,512]{1,0:T(8,128)(2,1)S(1)}, u32[]{:S(2)}, u32[]{:S(2)}) %collective-permute-start.12) | collective-permute-done | bytes 114720 | tf_op jit(solution)/shard_map/ppermute | solution.py:25
  99.2 2.2 %convolution_convert_fusion = bf16[512,1280]{1,0:T(8,128)(2,1)S(1)} fusion(bf16[448,512]{1,0:T(8,128)(2,1)S(1)} %get-tuple-element.58, bf16[448,2048]{1,0:T(8,128)(2,1)} %get-tuple-element.47), kind=kOutput, calls=%fused_computation | convolution fusion | flops 587857920 | bytes 2916352 | tf_op jit(solution)/shard_map/dot_general | solution.py:37
  103.8 2.7 %fusion.15.left_ref.la_ref.lb_ref = f32[512,2048]{1,0:T(8,128)} fusion(bf16[224,512]{1,0:T(8,128)(2,1)S(1)} %get-tuple-element.57, bf16[224,2048]{1,0:T(8,128)(2,1)S(1)} %copy-done.13), kind=kOutput, calls=%fused_computation.32 | convolution fusion | flops 469762048 | bytes 5341184 | tf_op jit(solution)/shard_map/dot_general | solution.py:37
  108.2 4.7 %all-to-all-start.3 = ((bf16[8,64,1280]{2,1,0:T(8,128)(2,1)}), bf16[8,64,1280]{2,1,0:T(8,128)(2,1)S(1)}, u32[]{:S(2)}, u32[]{:S(2)}) async-start(bf16[8,64,1280]{2,1,0:T(8,128)(2,1)} %bitcast.21), calls=%async_computation.3 | async-start | bytes 2621440 | tf_op jit(solution)/shard_map/all_to_all | solution.py:29
  116.0 2.7 %collective-permute-start.15 = (bf16[64,1408]{1,0:T(8,128)(2,1)S(1)}, bf16[64,1408]{1,0:T(8,128)(2,1)S(1)}, u32[]{:S(2)}, u32[]{:S(2)}) collective-permute-start(bf16[64,1408]{1,0:T(8,128)(2,1)S(1)} %get-tuple-element.60), channel_id=1, source_target_pairs={{0,224},{32,0},{64,32},{96,64},{128,96},{160,128},{192,160},{224,1... | collective-permute-start | bytes 540680 | tf_op jit(solution)/shard_map/ppermute | solution.py:25
  120.8 2.5 %collective-permute-done.14.came_up_ref = bf16[64,1408]{1,0:T(8,128)(2,1)S(1)} collective-permute-done((bf16[64,1408]{1,0:T(8,128)(2,1)S(1)}, bf16[64,1408]{1,0:T(8,128)(2,1)S(1)}, u32[]{:S(2)}, u32[]{:S(2)}) %collective-permute-start.14) | collective-permute-done | bytes 180256 | tf_op jit(solution)/shard_map/ppermute | solution.py:25
  123.6 2.7 %collective-permute-start.17 = (bf16[64,2816]{1,0:T(8,128)(2,1)S(1)}, bf16[64,2816]{1,0:T(8,128)(2,1)S(1)}, u32[]{:S(2)}, u32[]{:S(2)}) collective-permute-start(bf16[64,2816]{1,0:T(8,128)(2,1)S(1)} %get-tuple-element.62), channel_id=1, source_target_pairs={{0,224},{32,0},{64,32},{96,64},{128,96},{160,128},{192,160},{224,1... | collective-permute-start | bytes 1081352 | tf_op jit(solution)/shard_map/ppermute | solution.py:25
  128.3 5.6 %collective-permute-done.16.came_up_ref = bf16[64,2816]{1,0:T(8,128)(2,1)S(1)} collective-permute-done((bf16[64,2816]{1,0:T(8,128)(2,1)S(1)}, bf16[64,2816]{1,0:T(8,128)(2,1)S(1)}, u32[]{:S(2)}, u32[]{:S(2)}) %collective-permute-start.16) | collective-permute-done | bytes 360480 | tf_op jit(solution)/shard_map/ppermute | solution.py:25
  134.9 2.7 %collective-permute-start.19 = (bf16[64,2816]{1,0:T(8,128)(2,1)}, bf16[64,2816]{1,0:T(8,128)(2,1)}, u32[]{:S(2)}, u32[]{:S(2)}) collective-permute-start(bf16[64,2816]{1,0:T(8,128)(2,1)} %get-tuple-element.64), channel_id=1, source_target_pairs={{0,224},{32,0},{64,32},{96,64},{128,96},{160,128},{192,160},{224,1... | collective-permute-start | bytes 1081352 | tf_op jit(solution)/shard_map/ppermute | solution.py:25
  139.5 5.0 %collective-permute-done.18.came_up_ref = bf16[64,2816]{1,0:T(8,128)(2,1)S(1)} collective-permute-done((bf16[64,2816]{1,0:T(8,128)(2,1)}, bf16[64,2816]{1,0:T(8,128)(2,1)S(1)}, u32[]{:S(2)}, u32[]{:S(2)}) %collective-permute-start.18) | collective-permute-done | bytes 360480 | tf_op jit(solution)/shard_map/ppermute | solution.py:25
  144.5 7.4 %all-to-all-start.4 = ((bf16[32,2,1280]{2,1,0:T(2,128)(2,1)}), bf16[32,2,1280]{2,1,0:T(2,128)(2,1)S(1)}, u32[]{:S(2)}, u32[]{:S(2)}) async-start(bf16[32,2,1280]{2,1,0:T(2,128)(2,1)} %shard_map.103), calls=%async_computation.4 | async-start | bytes 327680 | tf_op jit(solution)/shard_map/all_to_all | solution.py:29
  158.2 2.2 %broadcast_select_fusion.3 = (bf16[112,2048]{1,0:T(8,128)(2,1)S(1)}, bf16[112,2048]{1,0:T(8,128)(2,1)S(1)}, bf16[112,2048]{1,0:T(8,128)(2,1)}, bf16[112,2048]{1,0:T(8,128)(2,1)}) fusion(pred[]{:T(512)S(6)} %eq.2, bf16[224,2048]{1,0:T(8,128)(2,1)} %collective-permute-done.22, bf16[224,2048]{1,0:T(8,128)(2,1)S(1)} %copy-done.14), kind=kLoop, calls=%fused_computation.23 | loop fusion | flops 917504 | bytes 3670017 | tf_op jit(solution)/shard_map/jit(_where)/select_n | solution.py:416
  160.5 7.0 %collective-permute-done.20.came_up_ref = bf16[64,2816]{1,0:T(8,128)(2,1)S(1)} collective-permute-done((bf16[64,2816]{1,0:T(8,128)(2,1)S(1)}, bf16[64,2816]{1,0:T(8,128)(2,1)S(1)}, u32[]{:S(2)}, u32[]{:S(2)}) %collective-permute-start.20) | collective-permute-done | bytes 360480 | tf_op jit(solution)/shard_map/ppermute | solution.py:25
  168.5 8.4 %all-to-all-start.5 = ((bf16[32,2,2816]{2,1,0:T(2,128)(2,1)}), bf16[32,2,2816]{2,1,0:T(2,128)(2,1)S(1)}, u32[]{:S(2)}, u32[]{:S(2)}) async-start(bf16[32,2,2816]{2,1,0:T(2,128)(2,1)} %shard_map.105), calls=%async_computation.5 | async-start | bytes 720896 | tf_op jit(solution)/shard_map/all_to_all | solution.py:29
  176.9 2.4 %pad_maximum_fusion = (bf16[112,4096]{1,0:T(8,128)(2,1)}, bf16[112,4096]{1,0:T(8,128)(2,1)}) fusion(bf16[112,2048]{1,0:T(8,128)(2,1)S(1)} %get-tuple-element.76, bf16[112,2048]{1,0:T(8,128)(2,1)} %get-tuple-element.78, bf16[112,2048]{1,0:T(8,128)(2,1)S(1)} %copy-done.15, bf16[112,2048]{1,0:T(8,128)(2,1)S(1)} %get-tuple-element.75), kind=kLoop, calls=%fused_computation.9 | loop fusion | flops 3670016 | bytes 3670016 | tf_op jit(solution)/shard_map/concatenate | solution.py:418
  179.3 7.2 %all-to-all-done.5.first_ref = bf16[32,2,2816]{2,1,0:T(2,128)(2,1)S(1)} async-done(((bf16[32,2,2816]{2,1,0:T(2,128)(2,1)}), bf16[32,2,2816]{2,1,0:T(2,128)(2,1)S(1)}, u32[]{:S(2)}, u32[]{:S(2)}) %all-to-all-start.5) | async-done | bytes 360480 | tf_op jit(solution)/shard_map/all_to_all | solution.py:29
  (108 shorter events, 44.0 us)
Async XLA Ops:
  5.5 8.7 %collective-permute-start = (bf16[336,2048]{1,0:T(8,128)(2,1)}, bf16[336,2048]{1,0:T(8,128)(2,1)S(1)}, u32[]{:S(2)}, u32[]{:S(2)}) collective-permute-start(bf16[336,2048]{1,0:T(8,128)(2,1)} %shard_map.93), channel_id=1, source_target_pairs={{0,2},{2,0},{1,3},{3,1},{4,6},{6,4},{5,7},{7,5},{8,10},{10,8},{9,1... | collective-permute-start | bytes 4128776 | tf_op jit(solution)/shard_map/ppermute | solution.py:25
  8.7 15.4 %all-to-all-start = ((bf16[32,2,3072]{2,1,0:T(2,128)(2,1)}), bf16[32,2,3072]{2,1,0:T(2,128)(2,1)S(1)}, u32[]{:S(2)}, u32[]{:S(2)}) async-start(bf16[32,2,3072]{2,1,0:T(2,128)(2,1)} %get-tuple-element.41), calls=%async_computation | async-start | bytes 786432 | tf_op jit(solution)/shard_map/all_to_all | solution.py:29
  24.4 41.6 %copy-start.2 = (bf16[64,3072]{1,0:T(8,128)(2,1)}, bf16[64,3072]{1,0:T(8,128)(2,1)S(1)}, u32[]{:S(2)}) copy-start(bf16[64,3072]{1,0:T(8,128)(2,1)S(1)} %shard_map.95.refs_0_) | copy-start | bytes 1179652
  24.4 14.9 %collective-permute-start.4 = (bf16[64,3072]{1,0:T(8,128)(2,1)S(1)}, bf16[64,3072]{1,0:T(8,128)(2,1)S(1)}, u32[]{:S(2)}, u32[]{:S(2)}) collective-permute-start(bf16[64,3072]{1,0:T(8,128)(2,1)S(1)} %shard_map.95.refs_0_), channel_id=1, source_target_pairs={{0,32},{32,64},{64,96},{96,128},{128,160},{160,192},{192,224},{224... | collective-permute-start | bytes 1179656 | tf_op jit(solution)/shard_map/ppermute | solution.py:25
  26.1 13.2 %collective-permute-start.1 = (bf16[64,3072]{1,0:T(8,128)(2,1)S(1)}, bf16[64,3072]{1,0:T(8,128)(2,1)S(1)}, u32[]{:S(2)}, u32[]{:S(2)}) collective-permute-start(bf16[64,3072]{1,0:T(8,128)(2,1)S(1)} %shard_map.95.refs_0_), channel_id=1, source_target_pairs={{0,224},{32,0},{64,32},{96,64},{128,96},{160,128},{192,160},{224,1... | collective-permute-start | bytes 1179656 | tf_op jit(solution)/shard_map/ppermute | solution.py:25
  30.1 18.4 %all-to-all-start.1 = ((bf16[32,2,1024]{2,1,0:T(2,128)(2,1)}), bf16[32,2,1024]{2,1,0:T(2,128)(2,1)S(1)}, u32[]{:S(2)}, u32[]{:S(2)}) async-start(bf16[32,2,1024]{2,1,0:T(2,128)(2,1)} %get-tuple-element.51), calls=%async_computation.1 | async-start | bytes 262144 | tf_op jit(solution)/shard_map/all_to_all | solution.py:29
  39.3 26.7 %copy-start.20 = (bf16[64,3072]{1,0:T(8,128)(2,1)}, bf16[64,3072]{1,0:T(8,128)(2,1)S(1)}, u32[]{:S(2)}) copy-start(bf16[64,3072]{1,0:T(8,128)(2,1)S(1)} %collective-permute-done.4.refs_6_) | copy-start | bytes 1179652
  39.3 14.0 %collective-permute-start.5 = (bf16[64,3072]{1,0:T(8,128)(2,1)S(1)}, bf16[64,3072]{1,0:T(8,128)(2,1)S(1)}, u32[]{:S(2)}, u32[]{:S(2)}) collective-permute-start(bf16[64,3072]{1,0:T(8,128)(2,1)S(1)} %collective-permute-done.4.refs_6_), channel_id=1, source_target_pairs={{0,32},{32,64},{64,96},{96,128},{128,160},{160,192},{192,224},{224... | collective-permute-start | bytes 1179656 | tf_op jit(solution)/shard_map/ppermute | solution.py:25
  39.3 14.4 %collective-permute-start.2 = (bf16[64,3072]{1,0:T(8,128)(2,1)S(1)}, bf16[64,3072]{1,0:T(8,128)(2,1)}, u32[]{:S(2)}, u32[]{:S(2)}) collective-permute-start(bf16[64,3072]{1,0:T(8,128)(2,1)S(1)} %collective-permute-done.1.refs_1_), channel_id=1, source_target_pairs={{0,224},{32,0},{64,32},{96,64},{128,96},{160,128},{192,160},{224,1... | collective-permute-start | bytes 1179656 | tf_op jit(solution)/shard_map/ppermute | solution.py:25
  49.7 19.4 %all-to-all-start.2 = ((bf16[8,64,1024]{2,1,0:T(8,128)(2,1)}), bf16[8,64,1024]{2,1,0:T(8,128)(2,1)S(1)}, u32[]{:S(2)}, u32[]{:S(2)}) async-start(bf16[8,64,1024]{2,1,0:T(8,128)(2,1)} %shard_map.96), calls=%async_computation.2 | async-start | bytes 2097152 | tf_op jit(solution)/shard_map/all_to_all | solution.py:29
  53.3 12.0 %collective-permute-start.6 = (bf16[64,3072]{1,0:T(8,128)(2,1)S(1)}, bf16[64,3072]{1,0:T(8,128)(2,1)S(1)}, u32[]{:S(2)}, u32[]{:S(2)}) collective-permute-start(bf16[64,3072]{1,0:T(8,128)(2,1)S(1)} %collective-permute-done.5.refs_5_), channel_id=1, source_target_pairs={{0,32},{32,64},{64,96},{96,128},{128,160},{160,192},{192,224},{224... | collective-permute-start | bytes 1179656 | tf_op jit(solution)/shard_map/ppermute | solution.py:25
  53.7 12.4 %collective-permute-start.3 = (bf16[64,3072]{1,0:T(8,128)(2,1)}, bf16[64,3072]{1,0:T(8,128)(2,1)S(1)}, u32[]{:S(2)}, u32[]{:S(2)}) collective-permute-start(bf16[64,3072]{1,0:T(8,128)(2,1)} %collective-permute-done.2.refs_2_), channel_id=1, source_target_pairs={{0,224},{32,0},{64,32},{96,64},{128,96},{160,128},{192,160},{224,1... | collective-permute-start | bytes 1179656 | tf_op jit(solution)/shard_map/ppermute | solution.py:25
  66.0 7.2 %collective-permute-start.8 = (bf16[64,1536]{1,0:T(8,128)(2,1)}, bf16[64,1536]{1,0:T(8,128)(2,1)}, u32[]{:S(2)}, u32[]{:S(2)}) collective-permute-start(bf16[64,1536]{1,0:T(8,128)(2,1)} %slice.65), channel_id=1, source_target_pairs={{0,32},{32,64},{64,96},{96,128},{128,160},{160,192},{192,224},{224... | collective-permute-start | bytes 589832 | tf_op jit(solution)/shard_map/ppermute | solution.py:25
  66.1 7.1 %collective-permute-start.7 = (bf16[64,1536]{1,0:T(8,128)(2,1)S(1)}, bf16[64,1536]{1,0:T(8,128)(2,1)S(1)}, u32[]{:S(2)}, u32[]{:S(2)}) collective-permute-start(bf16[64,1536]{1,0:T(8,128)(2,1)S(1)} %slice.64), channel_id=1, source_target_pairs={{0,224},{32,0},{64,32},{96,64},{128,96},{160,128},{192,160},{224,1... | collective-permute-start | bytes 589832 | tf_op jit(solution)/shard_map/ppermute | solution.py:25
  81.2 3.3 %collective-permute-start.9 = (f32[224,512]{1,0:T(8,128)S(1)}, f32[224,512]{1,0:T(8,128)S(1)}, u32[]{:S(2)}, u32[]{:S(2)}) collective-permute-start(f32[224,512]{1,0:T(8,128)S(1)} %fusion.1), channel_id=1, source_target_pairs={{0,2},{2,0},{1,3},{3,1},{4,6},{6,4},{5,7},{7,5},{8,10},{10,8},{9,1... | collective-permute-start | bytes 1376264 | tf_op jit(solution)/shard_map/ppermute | solution.py:25
  83.9 2.6 %collective-permute-start.11 = (f32[112,512]{1,0:T(8,128)S(1)}, f32[112,512]{1,0:T(8,128)S(1)}, u32[]{:S(2)}, u32[]{:S(2)}) collective-permute-start(f32[112,512]{1,0:T(8,128)S(1)} %fusion.6), channel_id=1, source_target_pairs={{0,2},{2,0},{1,3},{3,1},{4,6},{6,4},{5,7},{7,5},{8,10},{10,8},{9,1... | collective-permute-start | bytes 688136 | tf_op jit(solution)/shard_map/ppermute | solution.py:25
  85.3 11.0 %collective-permute-start.10 = (bf16[224,512]{1,0:T(8,128)(2,1)S(1)}, bf16[224,512]{1,0:T(8,128)(2,1)S(1)}, u32[]{:S(2)}, u32[]{:S(2)}) collective-permute-start(bf16[224,512]{1,0:T(8,128)(2,1)S(1)} %get-tuple-element.81), channel_id=1, source_target_pairs={{0,1},{1,0},{2,3},{3,2},{4,5},{5,4},{6,7},{7,6},{8,9},{9,8},{10,11... | collective-permute-start | bytes 688136 | tf_op jit(solution)/shard_map/ppermute | solution.py:25
  87.3 9.1 %collective-permute-start.12 = (bf16[112,512]{1,0:T(8,128)(2,1)S(1)}, bf16[112,512]{1,0:T(8,128)(2,1)S(1)}, u32[]{:S(2)}, u32[]{:S(2)}) collective-permute-start(bf16[112,512]{1,0:T(8,128)(2,1)S(1)} %get-tuple-element.83), channel_id=1, source_target_pairs={{0,1},{1,0},{2,3},{3,2},{4,5},{5,4},{6,7},{7,6},{8,9},{9,8},{10,11... | collective-permute-start | bytes 344072 | tf_op jit(solution)/shard_map/ppermute | solution.py:25
  96.5 2.6 %collective-permute-start.13 = (bf16[336,512]{1,0:T(8,128)(2,1)S(1)}, bf16[336,512]{1,0:T(8,128)(2,1)S(1)}, u32[]{:S(2)}, u32[]{:S(2)}) collective-permute-start(bf16[336,512]{1,0:T(8,128)(2,1)S(1)} %shard_map.98.own_ref), channel_id=1, source_target_pairs={{0,2},{2,0},{1,3},{3,1},{4,6},{6,4},{5,7},{7,5},{8,10},{10,8},{9,1... | collective-permute-start | bytes 1032200 | tf_op jit(solution)/shard_map/ppermute | solution.py:25
  108.2 30.3 %all-to-all-start.3 = ((bf16[8,64,1280]{2,1,0:T(8,128)(2,1)}), bf16[8,64,1280]{2,1,0:T(8,128)(2,1)S(1)}, u32[]{:S(2)}, u32[]{:S(2)}) async-start(bf16[8,64,1280]{2,1,0:T(8,128)(2,1)} %bitcast.21), calls=%async_computation.3 | async-start | bytes 2621440 | tf_op jit(solution)/shard_map/all_to_all | solution.py:29
  113.0 14.8 %collective-permute-start.23 = (bf16[112,2048]{1,0:T(8,128)(2,1)}, bf16[112,2048]{1,0:T(8,128)(2,1)S(1)}, u32[]{:S(2)}, u32[]{:S(2)}) collective-permute-start(bf16[112,2048]{1,0:T(8,128)(2,1)} %convolution_convert_fusion.3), channel_id=1, source_target_pairs={{0,2},{2,0},{1,3},{3,1},{4,6},{6,4},{5,7},{7,5},{8,10},{10,8},{9,1... | collective-permute-start | bytes 1376264 | tf_op jit(solution)/shard_map/ppermute | solution.py:25
  115.9 7.5 %collective-permute-start.14 = (bf16[64,1408]{1,0:T(8,128)(2,1)S(1)}, bf16[64,1408]{1,0:T(8,128)(2,1)S(1)}, u32[]{:S(2)}, u32[]{:S(2)}) collective-permute-start(bf16[64,1408]{1,0:T(8,128)(2,1)S(1)} %get-tuple-element.59), channel_id=1, source_target_pairs={{0,32},{32,64},{64,96},{96,128},{128,160},{160,192},{192,224},{224... | collective-permute-start | bytes 540680 | tf_op jit(solution)/shard_map/ppermute | solution.py:25
  116.0 7.4 %collective-permute-start.15 = (bf16[64,1408]{1,0:T(8,128)(2,1)S(1)}, bf16[64,1408]{1,0:T(8,128)(2,1)S(1)}, u32[]{:S(2)}, u32[]{:S(2)}) collective-permute-start(bf16[64,1408]{1,0:T(8,128)(2,1)S(1)} %get-tuple-element.60), channel_id=1, source_target_pairs={{0,224},{32,0},{64,32},{96,64},{128,96},{160,128},{192,160},{224,1... | collective-permute-start | bytes 540680 | tf_op jit(solution)/shard_map/ppermute | solution.py:25
  120.2 38.0 %collective-permute-start.22 = (bf16[224,2048]{1,0:T(8,128)(2,1)}, bf16[224,2048]{1,0:T(8,128)(2,1)}, u32[]{:S(2)}, u32[]{:S(2)}) collective-permute-start(bf16[224,2048]{1,0:T(8,128)(2,1)} %convolution_convert_fusion.1), channel_id=1, source_target_pairs={{0,2},{2,0},{1,3},{3,1},{4,6},{6,4},{5,7},{7,5},{8,10},{10,8},{9,1... | collective-permute-start | bytes 2752520 | tf_op jit(solution)/shard_map/ppermute | solution.py:25
  123.5 10.4 %collective-permute-start.16 = (bf16[64,2816]{1,0:T(8,128)(2,1)S(1)}, bf16[64,2816]{1,0:T(8,128)(2,1)S(1)}, u32[]{:S(2)}, u32[]{:S(2)}) collective-permute-start(bf16[64,2816]{1,0:T(8,128)(2,1)S(1)} %get-tuple-element.61), channel_id=1, source_target_pairs={{0,32},{32,64},{64,96},{96,128},{128,160},{160,192},{192,224},{224... | collective-permute-start | bytes 1081352 | tf_op jit(solution)/shard_map/ppermute | solution.py:25
  123.6 10.3 %collective-permute-start.17 = (bf16[64,2816]{1,0:T(8,128)(2,1)S(1)}, bf16[64,2816]{1,0:T(8,128)(2,1)S(1)}, u32[]{:S(2)}, u32[]{:S(2)}) collective-permute-start(bf16[64,2816]{1,0:T(8,128)(2,1)S(1)} %get-tuple-element.62), channel_id=1, source_target_pairs={{0,224},{32,0},{64,32},{96,64},{128,96},{160,128},{192,160},{224,1... | collective-permute-start | bytes 1081352 | tf_op jit(solution)/shard_map/ppermute | solution.py:25
  134.9 9.6 %collective-permute-start.18 = (bf16[64,2816]{1,0:T(8,128)(2,1)}, bf16[64,2816]{1,0:T(8,128)(2,1)S(1)}, u32[]{:S(2)}, u32[]{:S(2)}) collective-permute-start(bf16[64,2816]{1,0:T(8,128)(2,1)} %get-tuple-element.63), channel_id=1, source_target_pairs={{0,32},{32,64},{64,96},{96,128},{128,160},{160,192},{192,224},{224... | collective-permute-start | bytes 1081352 | tf_op jit(solution)/shard_map/ppermute | solution.py:25
  134.9 9.6 %collective-permute-start.19 = (bf16[64,2816]{1,0:T(8,128)(2,1)}, bf16[64,2816]{1,0:T(8,128)(2,1)}, u32[]{:S(2)}, u32[]{:S(2)}) collective-permute-start(bf16[64,2816]{1,0:T(8,128)(2,1)} %get-tuple-element.64), channel_id=1, source_target_pairs={{0,224},{32,0},{64,32},{96,64},{128,96},{160,128},{192,160},{224,1... | collective-permute-start | bytes 1081352 | tf_op jit(solution)/shard_map/ppermute | solution.py:25
  144.5 24.0 %all-to-all-start.4 = ((bf16[32,2,1280]{2,1,0:T(2,128)(2,1)}), bf16[32,2,1280]{2,1,0:T(2,128)(2,1)S(1)}, u32[]{:S(2)}, u32[]{:S(2)}) async-start(bf16[32,2,1280]{2,1,0:T(2,128)(2,1)} %shard_map.103), calls=%async_computation.4 | async-start | bytes 327680 | tf_op jit(solution)/shard_map/all_to_all | solution.py:29
  155.4 12.1 %collective-permute-start.20 = (bf16[64,2816]{1,0:T(8,128)(2,1)S(1)}, bf16[64,2816]{1,0:T(8,128)(2,1)S(1)}, u32[]{:S(2)}, u32[]{:S(2)}) collective-permute-start(bf16[64,2816]{1,0:T(8,128)(2,1)S(1)} %get-tuple-element.68), channel_id=1, source_target_pairs={{0,32},{32,64},{64,96},{96,128},{128,160},{160,192},{192,224},{224... | collective-permute-start | bytes 1081352 | tf_op jit(solution)/shard_map/ppermute | solution.py:25
  156.8 10.6 %collective-permute-start.21 = (bf16[64,2816]{1,0:T(8,128)(2,1)S(1)}, bf16[64,2816]{1,0:T(8,128)(2,1)S(1)}, u32[]{:S(2)}, u32[]{:S(2)}) collective-permute-start(bf16[64,2816]{1,0:T(8,128)(2,1)S(1)} %get-tuple-element.69), channel_id=1, source_target_pairs={{0,224},{32,0},{64,32},{96,64},{128,96},{160,128},{192,160},{224,1... | collective-permute-start | bytes 1081352 | tf_op jit(solution)/shard_map/ppermute | solution.py:25
  168.5 18.0 %all-to-all-start.5 = ((bf16[32,2,2816]{2,1,0:T(2,128)(2,1)}), bf16[32,2,2816]{2,1,0:T(2,128)(2,1)S(1)}, u32[]{:S(2)}, u32[]{:S(2)}) async-start(bf16[32,2,2816]{2,1,0:T(2,128)(2,1)} %shard_map.105), calls=%async_computation.5 | async-start | bytes 720896 | tf_op jit(solution)/shard_map/all_to_all | solution.py:29
  (22 other events, 127.8 us)

commit v2 on v0

v2 whole, which is shorter than its diff:
```python
import functools

import jax
import jax.numpy as jnp
from jax import lax
from jax.experimental import pallas as pl
from jax.experimental.pallas import tpu as pltpu
from jax.sharding import Mesh
from jax.sharding import PartitionSpec as P

AXES = ("z", "y", "x", "core", "tok")
BLK = ("z", "y", "x", "core")
PLANE = ("y", "x")
PAIRS = ("tok", "core")
F32 = jnp.float32
BF16 = jnp.bfloat16
VMEM = pl.BlockSpec(memory_space=pltpu.VMEM)
SMEM = pl.BlockSpec(memory_space=pltpu.SMEM)
ANY = pl.BlockSpec(memory_space=pl.ANY)
PARAMS = pltpu.CompilerParams(vmem_limit_bytes=20 * 1024 * 1024)
LARGE = pltpu.CompilerParams(vmem_limit_bytes=58 * 1024 * 1024)


def shifted(block, axis, distance):
    count = lax.axis_size(axis)
    return lax.ppermute(block, axis, [(i, (i + distance) % count) for i in range(count)])


def exchanged(blocks, axes):
    return lax.all_to_all(blocks, axes, 0, 0, tiled=True)


def by_rows(left, right):
    return lax.dot_general(left, right, (((1,), (1,)), ((), ())), preferred_element_type=F32)


def by_columns(left, right):
    return lax.dot_general(left, right, (((0,), (0,)), ((), ())), preferred_element_type=F32)


def called(kernel, out_shape, *args, specs=None, scratch=(), **kwargs):
    specs = specs or [VMEM] * len(args)
    return pl.pallas_call(
        functools.partial(kernel, **kwargs),
        out_shape=out_shape,
        in_specs=specs,
        out_specs=jax.tree.map(lambda _: VMEM, out_shape),
        scratch_shapes=scratch,
        compiler_params=PARAMS,
    )(*args)


def called_at(kernel, out_shape, places, *args, index=None, scratch=(), **kwargs):
    def whole(shape):
        return pl.BlockSpec(shape, lambda *_: (0,) * len(shape))

    specs = [
        whole(arg.shape) if place is None else pl.BlockSpec(*place)
        for arg, place in zip(args, places, strict=True)
    ]
    grid = pltpu.PrefetchScalarGridSpec(
        num_scalar_prefetch=1,
        grid=(1,),
        in_specs=specs,
        out_specs=jax.tree.map(lambda o: whole(o.shape), out_shape),
        scratch_shapes=scratch,
    )
    return pl.pallas_call(
        functools.partial(kernel, **kwargs),
        out_shape=out_shape,
        grid_spec=grid,
        compiler_params=PARAMS,
    )(jnp.zeros((1,), jnp.int32) if index is None else index, *args)


def shape_of(shape, kind=BF16):
    return jax.ShapeDtypeStruct(shape, kind)


def deal_kernel(tokens_ref, upstream_ref, out_ref, *, quarters):
    part = tokens_ref.shape[1] // quarters
    for q in range(quarters):
        rows = tokens_ref[:, q * part : (q + 1) * part]
        grads = upstream_ref[:, q * part : (q + 1) * part]
        for j in range(out_ref.shape[0] // quarters):
            out_ref[j * quarters + q, :, :part] = rows
            out_ref[j * quarters + q, :, part:] = grads


def merge_kernel(blocks_ref, left_ref, right_ref, rows_ref):
    n, pair, _ = blocks_ref.shape
    for j in range(n):
        rows_ref[j * pair : (j + 1) * pair, :] = blocks_ref[j].astype(F32)
    left_ref[...] = rows_ref[:, : left_ref.shape[1]].astype(BF16)
    right_ref[...] = rows_ref[:, left_ref.shape[1] :].astype(BF16)


def copied(pairs, sem):
    copies = [pltpu.make_async_copy(src, dst, sem.at[j]) for j, (src, dst) in enumerate(pairs)]
    for copy in copies:
        copy.start()
    for copy in copies:
        copy.wait()


def pack_kernel(at_ref, gate_ref, up_ref, down_ref, out_ref, sem):
    units, part = gate_ref.shape[0], out_ref.shape[1]
    columns = pl.ds(pl.multiple_of(at_ref[0] * part, part), part)
    copied(
        [
            (ref.at[:, columns], out_ref.at[pl.ds(j * units, units), :])
            for j, ref in enumerate((gate_ref, up_ref, down_ref))
        ],
        sem,
    )


def weights_kernel(at_ref, gate_ref, up_ref, down_ref, got_ref, in_ref, out_ref, sem):
    units, part = gate_ref.shape[0], in_ref.shape[1]
    columns = pl.ds(pl.multiple_of(at_ref[0] * part, part), part)
    copied(
        [
            (gate_ref.at[:, columns], in_ref.at[pl.ds(0, units), :]),
            (up_ref.at[:, columns], in_ref.at[pl.ds(units, units), :]),
            (got_ref.at[pl.ds(0, 2 * units), :], in_ref.at[pl.ds(2 * units, 2 * units), :]),
            (down_ref.at[:, columns], out_ref.at[pl.ds(0, units), :]),
            (got_ref.at[pl.ds(2 * units, units), :], out_ref.at[pl.ds(units, units), :]),
        ],
        sem,
    )


def moved(kernel, out_shape, count, *args, at=None, params=PARAMS):
    return pl.pallas_call(
        kernel,
        out_shape=out_shape,
        in_specs=([] if at is None else [SMEM]) + [ANY] * len(args),
        out_specs=jax.tree.map(lambda _: ANY, out_shape),
        scratch_shapes=[pltpu.SemaphoreType.DMA((count,))],
        compiler_params=params,
    )(*([] if at is None else [at]), *args)


def stack_kernel(*refs, place):
    *block_refs, left_ref, right_ref, out_ref, sem = refs
    height, middle = left_ref.shape
    width = out_ref.shape[1]
    places = [k for k in range(len(block_refs) + 1) if k != place]
    at = pl.ds(place * height, height)
    copied(
        [
            *(
                (ref, out_ref.at[pl.ds(k * height, height), :])
                for k, ref in zip(places, block_refs, strict=True)
            ),
            (left_ref, out_ref.at[at, pl.ds(0, middle)]),
            (right_ref, out_ref.at[at, pl.ds(middle, width - middle)]),
        ],
        sem,
    )


def middle_kernel(sum_ref, got_ref, hid_ref, hid_got_ref, out_ref):
    units = hid_ref.shape[0]
    gate_value = sum_ref[:units, :] + got_ref[:units, :]
    up_value = sum_ref[units:, :] + got_ref[units:, :]
    hidden_grad = hid_ref[...] + hid_got_ref[...]
    gate_sigmoid = jax.nn.sigmoid(gate_value)
    swish_gate = gate_value * gate_sigmoid
    gate_grad = hidden_grad * up_value * gate_sigmoid * (1.0 + gate_value * (1.0 - gate_sigmoid))
    out_ref[:units, :] = gate_grad.astype(BF16)
    out_ref[units : 2 * units, :] = (hidden_grad * swish_gate).astype(BF16)
    out_ref[2 * units :, :] = (swish_gate * up_value).astype(BF16)


def pair_kernel(own_ref, got_ref, in_ref, hidden_ref):
    double = in_ref.shape[0] // 2
    in_ref[:double, :] = own_ref[:double, :]
    in_ref[double:, :] = got_ref[:double, :]
    hidden_ref[: double // 2, :] = own_ref[double:, :]
    hidden_ref[double // 2 :, :] = got_ref[double:, :]


def turn_kernel(_, left_ref, right_ref, came_ref, out_ref, *, whole, up):
    width = left_ref.shape[1]
    left, right = left_ref[...], right_ref[...]
    if whole or up:
        left = left + came_ref[:, :width].astype(F32)
    if whole or not up:
        right = right + came_ref[:, came_ref.shape[1] - width :].astype(F32)
    out_ref[:, :width] = left.astype(BF16)
    out_ref[:, width:] = right.astype(BF16)


def close_kernel(_, left_ref, right_ref, came_up_ref, came_down_ref, out_ref, rows_ref):
    n, pair, _ = out_ref.shape
    width = left_ref.shape[1]
    came = came_up_ref[...].astype(F32) + came_down_ref[...].astype(F32)
    rows_ref[:, :width] = left_ref[...] + came[:, :width]
    rows_ref[:, width:] = right_ref[...] + came[:, width:]
    for j in range(n):
        out_ref[j] = rows_ref[j * pair : (j + 1) * pair, :].astype(BF16)


def total_kernel(blocks_ref, mixed_ref, input_ref, *, quarters):
    part = mixed_ref.shape[1] // quarters
    for q in range(quarters):
        total = blocks_ref[q].astype(F32)
        for j in range(1, blocks_ref.shape[0] // quarters):
            total = total + blocks_ref[j * quarters + q].astype(F32)
        total = total.astype(BF16)
        mixed_ref[:, q * part : (q + 1) * part] = total[:, :part]
        input_ref[:, q * part : (q + 1) * part] = total[:, part:]


def rings_gathered(first, second):
    count = lax.axis_size("z")
    half, middle = count // 2, first.shape[1] // 2
    lead, kept, late = [first] * (count + 1), [first] * (count + 1), [second] * (count + 1)

    def step(ring, k):
        if k < half:
            return shifted(ring[k - 1], "z", -1), shifted(ring[1 - k], "z", 1)
        return (
            shifted(ring[k - 1][:, :middle], "z", -1),
            shifted(ring[1 - k][:, middle:], "z", 1),
        )

    for k in range(1, half + 1):
        lead[k], lead[-k] = step(lead, k)
        kept[k], kept[-k], late[k - 1], late[1 - k] = lax.optimization_barrier(
            (lead[k], lead[-k], late[k - 1], late[1 - k])
        )
        late[k], late[-k] = step(late, k)
    return kept, late


def stacked(ring):
    half = (len(ring) - 1) // 2
    height, width = ring[0].shape
    blocks = [*ring[:half], *ring[-half + 1 :][: half - 1]]
    return moved(
        functools.partial(stack_kernel, place=half),
        shape_of((2 * half * height, width)),
        2 * half + 1,
        *blocks,
        ring[half],
        ring[-half],
    )


def rings_reduced(factors, height, pair):
    count = lax.axis_size("z")
    half = count // 2
    width = factors[0][1].shape[1]
    lefts = [left for left, _ in factors]
    terms = {}

    def multiply(first, last):
        found = [
            by_columns(left[:, first * height : last * height], right)
            for left, (_, right) in zip(lefts, factors, strict=True)
        ]
        for k in range(first, last):
            terms[k] = found, k - first

    def added(kernel, out_shape, k, *came, scratch=(), **kwargs):
        found, j = terms[k % count]
        place = ((height, width), lambda *_: (j, 0))
        places = [place, place] + [None] * len(came)
        return called_at(kernel, out_shape, places, *found, *came, scratch=scratch, **kwargs)

    multiply(half - 2, half + 2)
    found, j = terms[half]
    up, down = (f[j * height : (j + 1) * height].astype(BF16) for f in found)
    both = shape_of((height, 2 * width))
    for k in range(half - 1, 0, -1):
        up, down = shifted(up, "z", 1), shifted(down, "z", -1)
        if k == half - 1:
            up, down, *lefts = lax.optimization_barrier((up, down, *lefts))
            multiply(half + 2, count)
            multiply(0, half - 2)
        up = added(turn_kernel, both, k, up, whole=k < half - 1, up=True)
        down = added(turn_kernel, both, -k, down, whole=k < half - 1, up=False)
    up, down = shifted(up, "z", 1), shifted(down, "z", -1)
    summed = added(
        close_kernel,
        shape_of((height // pair, pair, 2 * width)),
        0,
        up,
        down,
        scratch=[pltpu.VMEM((height, 2 * width), F32)],
    )
    return summed, lefts


def local(tokens, upstream, gate_weight, up_weight, down_weight):
    core = lax.axis_index("core")
    tok = lax.axis_index("tok")
    n_z = lax.axis_size("z")
    n_plane = lax.axis_size("y") * lax.axis_size("x")
    n_core = lax.axis_size("core")
    quarters = n_core * lax.axis_size("tok")
    pair, width = tokens.shape
    part = width // quarters
    units = gate_weight.shape[0]
    n = pair * quarters
    n_rows = n_plane * n
    count = n_z * n_plane * n
    own_at = (tok * n_core + core).astype(jnp.int32).reshape(1)
    other_at = (tok * n_core + 1 - core).astype(jnp.int32).reshape(1)

    dealt = called(
        deal_kernel,
        shape_of((n_plane * quarters, pair, 2 * part)),
        tokens,
        upstream,
        quarters=quarters,
    )
    dealt, *weights = lax.optimization_barrier((dealt, gate_weight, up_weight, down_weight))
    sent = moved(pack_kernel, shape_of((3 * units, part)), 3, *weights, at=other_at, params=LARGE)
    in_weights, out_weights = moved(
        weights_kernel,
        (shape_of((4 * units, part)), shape_of((2 * units, part))),
        5,
        *weights,
        shifted(sent, "core", 1),
        at=own_at,
        params=LARGE,
    )
    dealt = exchanged(dealt, (*PLANE, *PAIRS))
    dealt, in_weights, out_weights = lax.optimization_barrier((dealt, in_weights, out_weights))
    rows, grads = called(
        merge_kernel,
        (shape_of((n_rows, part)), shape_of((n_rows, part))),
        dealt,
        scratch=[pltpu.VMEM((n_rows, 2 * part), F32)],
    )
    rows, grads = rings_gathered(rows, grads)
    rows = stacked(rows)

    gate_up = shifted(by_rows(in_weights[2 * units :], rows), "core", 1)
    gate_up = by_rows(in_weights[: 2 * units], rows) + gate_up
    grads = stacked(grads)
    hidden_grad = shifted(by_rows(out_weights[units:], grads), "core", 1)
    hidden_grad = by_rows(out_weights[:units], grads) + hidden_grad
    own = called(
        middle_kernel,
        shape_of((3 * units, count)),
        gate_up,
        shifted(gate_up, "tok", 1),
        hidden_grad,
        shifted(hidden_grad, "tok", 1),
    )
    in_grads, hidden = called(
        pair_kernel,
        (shape_of((4 * units, count)), shape_of((2 * units, count))),
        own,
        shifted(own, "core", 1),
    )

    summed, (hidden, in_grads) = rings_reduced(
        [(hidden, out_weights), (in_grads, in_weights)], n_rows, pair
    )
    mixed, input_grad = called(
        total_kernel,
        (shape_of((pair, width)), shape_of((pair, width))),
        exchanged(summed, (*PLANE, *PAIRS)),
        quarters=quarters,
    )

    def product(left, right):
        return jnp.dot(left, right, preferred_element_type=F32).astype(BF16)

    got_in = shifted(product(in_grads[2 * units :], rows), "core", 1)
    got_out = shifted(product(hidden[units:], grads), "core", 1)
    in_weight_grad = product(in_grads[: 2 * units], rows)
    out_weight_grad = product(hidden[:units], grads)

    def side_by_side(mine, others):
        left = jnp.where(core == 0, mine, others)
        right = jnp.where(core == 0, others, mine)
        return jnp.concatenate([left, right], axis=1)

    return (
        mixed,
        input_grad,
        side_by_side(in_weight_grad[:units], got_in[:units]),
        side_by_side(in_weight_grad[units:], got_in[units:]),
        side_by_side(out_weight_grad, got_out),
    )


def solution(mesh):
    finer = Mesh(mesh.devices.reshape(8, 4, 2, 2, mesh.shape["tok"]), AXES)
    return jax.shard_map(
        local,
        mesh=finer,
        in_specs=(P(AXES, None), P(AXES, None), P(BLK, None), P(BLK, None), P(BLK, None)),
        out_specs=(P(AXES, None), P(AXES, None), P(BLK, "tok"), P(BLK, "tok"), P(BLK, "tok")),
        check_vma=False,
    )
```

time: 198 us -> 312 us (1.58)
  Pallas kernels: 10.4 us -> 132 us
  waiting for transfers between devices: 73.7 us -> 97.8 us
  starting transfers between devices: 74.8 us -> 58.8 us
  local copies, waits for them, and re-layouts: 18.3 us -> 6.88 us
    pallas_call x0 -> x4, Pallas kernels: none -> 128 us  [moved(): pl.pallas_call(kernel, out_shape=out_shape, in_specs=([] if at is None el...]
    ppermute x24 -> x32, waiting for transfers between devices: 46.4 us -> 89 us  [shifted(): lax.ppermute(block, axis, [(i, (i + distance) % count) for i in range(cou...]
    all_to_all x6 -> x2, starting transfers between devices: 41.1 us -> 16 us  [exchanged(): return lax.all_to_all(blocks, axes, 0, 0, tiled=True)]
    all_to_all x6 -> x2, waiting for transfers between devices: 27.3 us -> 8.8 us  [exchanged(): return lax.all_to_all(blocks, axes, 0, 0, tiled=True)]
    unnamed x42 -> x28, local copies, waits for them, and re-layouts: 15.4 us -> 5.37 us
    ppermute x24 -> x32, starting transfers between devices: 33.7 us -> 42.8 us  [shifted(): lax.ppermute(block, axis, [(i, (i + distance) % count) for i in range(cou...]
    pallas_call x8 -> x5, Pallas kernels: 5.7 us -> 2.09 us  [called(): pl.pallas_call(functools.partial(kernel, **kwargs), out_shape=out_shape,...]
  transfers between devices with their start and end apart: 30 -> 34, of which waited for: 14 -> 22; matrix products, arithmetic and copies ran while one was open for 9% -> 3% of each run, Pallas kernels for 4% -> 28%
where the time goes in v2:
time: 312 us
  Pallas kernels  132 us (42%)
  waiting for transfers between devices  97.8 us (31%)
  starting transfers between devices  58.8 us (19%)
  matrix products  11.7 us (4%)
  local copies, waits for them, and re-layouts  6.88 us (2%)
  other arithmetic  3.64 us (1%)
    pallas_call x4, Pallas kernels, moved(): pl.pallas_call(kernel, out_shape=out_shape, in_specs=([] if at is None el...  128 us
    ppermute x32, waiting for transfers between devices, shifted(): lax.ppermute(block, axis, [(i, (i + distance) % count) for i in range(cou...  89 us
    ppermute x32, starting transfers between devices, shifted(): lax.ppermute(block, axis, [(i, (i + distance) % count) for i in range(cou...  42.8 us
    all_to_all x2, starting transfers between devices, exchanged(): return lax.all_to_all(blocks, axes, 0, 0, tiled=True)  16 us
    all_to_all x2, waiting for transfers between devices, exchanged(): return lax.all_to_all(blocks, axes, 0, 0, tiled=True)  8.8 us
  transfers between devices with their start and end apart: 34, of which 22 were waited for; matrix products, arithmetic and copies ran while one was open for 3% of the time, Pallas kernels for 28%

profile of v2, /device:TPU:1, one launch (start us, length us, event | category | flops | bytes accessed | tf_op | source)
XLA Modules:
  0.0 311.6 jit_solution(3694664213093335172)
XLA Ops:
  3.0 42.8 %shard_map.93 = bf16[336,2048]{1,0:T(8,128)(2,1)} custom-call(s32[1]{0:T(128)} %bitcast.1.at_ref, bf16[112,8192]{1,0:T(8,128)(2,1)} %gate_ref.1, bf16[112,8192]{1,0:T(8,128)(2,1)} %up_ref.1, bf16[112,8192]{1,0:T(8,128)(2,1)} %down_ref.1), custom_call_target="tpu_custom_call" | custom-call | tf_op jit(solution)/shard_map/pallas_call | solution.py:134
  45.8 3.3 %collective-permute-start = (bf16[336,2048]{1,0:T(8,128)(2,1)}, bf16[336,2048]{1,0:T(8,128)(2,1)S(1)}, u32[]{:S(2)}, u32[]{:S(2)}) collective-permute-start(bf16[336,2048]{1,0:T(8,128)(2,1)} %shard_map.93), channel_id=1, source_target_pairs={{0,2},{2,0},{1,3},{3,1},{4,6},{6,4},{5,7},{7,5},{8,10},{10,8},{9,1... | collective-permute-start | bytes 4128776 | tf_op jit(solution)/shard_map/ppermute | solution.py:26
  49.1 5.5 %all-to-all-start = ((bf16[32,2,4096]{2,1,0:T(2,128)(2,1)}), bf16[32,2,4096]{2,1,0:T(2,128)(2,1)S(1)}, u32[]{:S(2)}, u32[]{:S(2)}) async-start(bf16[32,2,4096]{2,1,0:T(2,128)(2,1)} %shard_map.92), calls=%async_computation | async-start | bytes 1048576 | tf_op jit(solution)/shard_map/all_to_all | solution.py:30
  55.7 84.5 %shard_map.94 = (bf16[448,2048]{1,0:T(8,128)(2,1)}, bf16[224,2048]{1,0:T(8,128)(2,1)}) custom-call(s32[1]{0:T(128)} %bitcast.at_ref, bf16[112,8192]{1,0:T(8,128)(2,1)} %gate_ref.1, bf16[112,8192]{1,0:T(8,128)(2,1)} %up_ref.1, bf16[112,8192]{1,0:T(8,128)(2,1)} %down_ref.1, bf16[336,2048]{1,0:T(8,128)(2,1)} %copy-done.13), custom_call_target="tpu_custom_call" | custom-call | tf_op jit(solution)/shard_map/pallas_call | solution.py:134
  140.6 5.7 %collective-permute-start.1 = (bf16[64,2048]{1,0:T(8,128)(2,1)S(1)}, bf16[64,2048]{1,0:T(8,128)(2,1)S(1)}, u32[]{:S(2)}, u32[]{:S(2)}) collective-permute-start(bf16[64,2048]{1,0:T(8,128)(2,1)S(1)} %get-tuple-element.47.refs_0_), channel_id=1, source_target_pairs={{0,224},{32,0},{64,32},{96,64},{128,96},{160,128},{192,160},{224,1... | collective-permute-start | bytes 786440 | tf_op jit(solution)/shard_map/ppermute | solution.py:26
  146.3 5.5 %collective-permute-done.1.refs_1_ = bf16[64,2048]{1,0:T(8,128)(2,1)S(1)} collective-permute-done((bf16[64,2048]{1,0:T(8,128)(2,1)S(1)}, bf16[64,2048]{1,0:T(8,128)(2,1)S(1)}, u32[]{:S(2)}, u32[]{:S(2)}) %collective-permute-start.1) | collective-permute-done | bytes 262176 | tf_op jit(solution)/shard_map/ppermute | solution.py:26
  151.8 3.1 collective-permute-done.2.refs_6_
  157.8 3.4 %collective-permute-done.5.refs_1_ = bf16[64,2048]{1,0:T(8,128)(2,1)S(1)} collective-permute-done((bf16[64,2048]{1,0:T(8,128)(2,1)S(1)}, bf16[64,2048]{1,0:T(8,128)(2,1)S(1)}, u32[]{:S(2)}, u32[]{:S(2)}) %collective-permute-start.5) | collective-permute-done | bytes 262176 | tf_op jit(solution)/shard_map/ppermute | solution.py:26
  162.9 4.0 %collective-permute-done.3.refs_2_ = bf16[64,2048]{1,0:T(8,128)(2,1)S(1)} collective-permute-done((bf16[64,2048]{1,0:T(8,128)(2,1)S(1)}, bf16[64,2048]{1,0:T(8,128)(2,1)S(1)}, u32[]{:S(2)}, u32[]{:S(2)}) %collective-permute-start.3) | collective-permute-done | bytes 262176 | tf_op jit(solution)/shard_map/ppermute | solution.py:26
  168.5 2.7 collective-permute-start.9
  172.6 2.6 collective-permute-done.10.refs_5_
  175.2 4.6 %collective-permute-done.7.refs_3_ = bf16[64,2048]{1,0:T(8,128)(2,1)S(1)} collective-permute-done((bf16[64,2048]{1,0:T(8,128)(2,1)S(1)}, bf16[64,2048]{1,0:T(8,128)(2,1)S(1)}, u32[]{:S(2)}, u32[]{:S(2)}) %collective-permute-start.7) | collective-permute-done | bytes 262176 | tf_op jit(solution)/shard_map/ppermute | solution.py:26
  180.8 2.4 collective-permute-start.13
  183.3 2.7 collective-permute-start.11
  186.3 2.0 collective-permute-done.11.refs_7_
  188.3 3.6 %collective-permute-done.12.refs_8_ = bf16[64,1024]{1,0:T(8,128)(2,1)S(1)} collective-permute-done((bf16[64,1024]{1,0:T(8,128)(2,1)S(1)}, bf16[64,1024]{1,0:T(8,128)(2,1)S(1)}, u32[]{:S(2)}, u32[]{:S(2)}) %collective-permute-start.12) | collective-permute-done | bytes 131104 | tf_op jit(solution)/shard_map/ppermute | solution.py:26
  193.0 5.0 %collective-permute-start.15 = (f32[224,512]{1,0:T(8,128)S(1)}, f32[224,512]{1,0:T(8,128)S(1)}, u32[]{:S(2)}, u32[]{:S(2)}) collective-permute-start(f32[224,512]{1,0:T(8,128)S(1)} %fusion), channel_id=1, source_target_pairs={{0,2},{2,0},{1,3},{3,1},{4,6},{6,4},{5,7},{7,5},{8,10},{10,8},{9,1... | collective-permute-start | bytes 1376264 | tf_op jit(solution)/shard_map/ppermute | solution.py:26
  199.6 3.5 %collective-permute-done.17.refs_7_ = bf16[64,1024]{1,0:T(8,128)(2,1)S(1)} collective-permute-done((bf16[64,1024]{1,0:T(8,128)(2,1)S(1)}, bf16[64,1024]{1,0:T(8,128)(2,1)S(1)}, u32[]{:S(2)}, u32[]{:S(2)}) %collective-permute-start.17) | collective-permute-done | bytes 131104 | tf_op jit(solution)/shard_map/ppermute | solution.py:26
  207.3 2.7 collective-permute-start.16
  211.3 14.6 %collective-permute-done.20.hid_got_ref = f32[112,512]{1,0:T(8,128)S(1)} collective-permute-done((f32[112,512]{1,0:T(8,128)S(1)}, f32[112,512]{1,0:T(8,128)S(1)}, u32[]{:S(2)}, u32[]{:S(2)}) %collective-permute-start.20) | collective-permute-done | bytes 229408 | tf_op jit(solution)/shard_map/ppermute | solution.py:26
  235.2 3.7 %collective-permute-done.23.came_ref = bf16[64,2048]{1,0:T(8,128)(2,1)S(1)} collective-permute-done((bf16[64,2048]{1,0:T(8,128)(2,1)}, bf16[64,2048]{1,0:T(8,128)(2,1)S(1)}, u32[]{:S(2)}, u32[]{:S(2)}) %collective-permute-start.23) | collective-permute-done | bytes 262176 | tf_op jit(solution)/shard_map/ppermute | solution.py:26
  238.9 3.6 %collective-permute-done.22.came_ref = bf16[64,2048]{1,0:T(8,128)(2,1)S(1)} collective-permute-done((bf16[64,2048]{1,0:T(8,128)(2,1)}, bf16[64,2048]{1,0:T(8,128)(2,1)S(1)}, u32[]{:S(2)}, u32[]{:S(2)}) %collective-permute-start.22) | collective-permute-done | bytes 262176 | tf_op jit(solution)/shard_map/ppermute | solution.py:26
  242.5 3.2 %convolution_convert_fusion = bf16[224,2048]{1,0:T(8,128)(2,1)} fusion(bf16[512,2048]{1,0:T(8,128)(2,1)} %copy-done.4, bf16[448,512]{1,0:T(8,128)(2,1)S(1)} %get-tuple-element.68), kind=kOutput, calls=%fused_computation | convolution fusion | flops 470220800 | bytes 3244032 | tf_op jit(solution)/shard_map/dot_general | solution.py:373
  250.5 1.6 convolution_convert_fusion.1
  252.1 8.8 %collective-permute-done.27.came_ref = bf16[64,4096]{1,0:T(8,128)(2,1)S(1)} collective-permute-done((bf16[64,4096]{1,0:T(8,128)(2,1)S(1)}, bf16[64,4096]{1,0:T(8,128)(2,1)S(1)}, u32[]{:S(2)}, u32[]{:S(2)}) %collective-permute-start.27) | collective-permute-done | bytes 524320 | tf_op jit(solution)/shard_map/ppermute | solution.py:26
  260.9 1.6 collective-permute-start.28
  263.5 8.9 %collective-permute-done.28.came_ref = bf16[64,4096]{1,0:T(8,128)(2,1)S(1)} collective-permute-done((bf16[64,4096]{1,0:T(8,128)(2,1)S(1)}, bf16[64,4096]{1,0:T(8,128)(2,1)S(1)}, u32[]{:S(2)}, u32[]{:S(2)}) %collective-permute-start.28) | collective-permute-done | bytes 524320 | tf_op jit(solution)/shard_map/ppermute | solution.py:26
  272.5 3.1 %collective-permute-start.29 = (bf16[64,4096]{1,0:T(8,128)(2,1)S(1)}, bf16[64,4096]{1,0:T(8,128)(2,1)S(1)}, u32[]{:S(2)}, u32[]{:S(2)}) collective-permute-start(bf16[64,4096]{1,0:T(8,128)(2,1)S(1)} %shard_map.105), channel_id=1, source_target_pairs={{0,224},{32,0},{64,32},{96,64},{128,96},{160,128},{192,160},{224,1... | collective-permute-start | bytes 1572872 | tf_op jit(solution)/shard_map/ppermute | solution.py:26
  277.3 6.9 %collective-permute-done.29.came_down_ref = bf16[64,4096]{1,0:T(8,128)(2,1)S(1)} collective-permute-done((bf16[64,4096]{1,0:T(8,128)(2,1)S(1)}, bf16[64,4096]{1,0:T(8,128)(2,1)S(1)}, u32[]{:S(2)}, u32[]{:S(2)}) %collective-permute-start.29) | collective-permute-done | bytes 524320 | tf_op jit(solution)/shard_map/ppermute | solution.py:26
  284.2 3.3 %collective-permute-done.26.came_up_ref = bf16[64,4096]{1,0:T(8,128)(2,1)S(1)} collective-permute-done((bf16[64,4096]{1,0:T(8,128)(2,1)S(1)}, bf16[64,4096]{1,0:T(8,128)(2,1)S(1)}, u32[]{:S(2)}, u32[]{:S(2)}) %collective-permute-start.26) | collective-permute-done | bytes 524320 | tf_op jit(solution)/shard_map/ppermute | solution.py:26
  288.8 10.6 %all-to-all-start.1 = ((bf16[32,2,4096]{2,1,0:T(2,128)(2,1)}), bf16[32,2,4096]{2,1,0:T(2,128)(2,1)S(1)}, u32[]{:S(2)}, u32[]{:S(2)}) async-start(bf16[32,2,4096]{2,1,0:T(2,128)(2,1)} %shard_map.106), calls=%async_computation.1 | async-start | bytes 1048576 | tf_op jit(solution)/shard_map/all_to_all | solution.py:30
  302.1 8.8 %all-to-all-done.1.blocks_ref = bf16[32,2,4096]{2,1,0:T(2,128)(2,1)S(1)} async-done(((bf16[32,2,4096]{2,1,0:T(2,128)(2,1)}), bf16[32,2,4096]{2,1,0:T(2,128)(2,1)S(1)}, u32[]{:S(2)}, u32[]{:S(2)}) %all-to-all-start.1) | async-done | bytes 524320 | tf_op jit(solution)/shard_map/all_to_all | solution.py:30
  (103 shorter events, 42.3 us)
Async XLA Ops:
  45.8 8.8 %collective-permute-start = (bf16[336,2048]{1,0:T(8,128)(2,1)}, bf16[336,2048]{1,0:T(8,128)(2,1)S(1)}, u32[]{:S(2)}, u32[]{:S(2)}) collective-permute-start(bf16[336,2048]{1,0:T(8,128)(2,1)} %shard_map.93), channel_id=1, source_target_pairs={{0,2},{2,0},{1,3},{3,1},{4,6},{6,4},{5,7},{7,5},{8,10},{10,8},{9,1... | collective-permute-start | bytes 4128776 | tf_op jit(solution)/shard_map/ppermute | solution.py:26
  49.1 91.1 %all-to-all-start = ((bf16[32,2,4096]{2,1,0:T(2,128)(2,1)}), bf16[32,2,4096]{2,1,0:T(2,128)(2,1)S(1)}, u32[]{:S(2)}, u32[]{:S(2)}) async-start(bf16[32,2,4096]{2,1,0:T(2,128)(2,1)} %shard_map.92), calls=%async_computation | async-start | bytes 1048576 | tf_op jit(solution)/shard_map/all_to_all | solution.py:30
  140.6 11.1 %collective-permute-start.1 = (bf16[64,2048]{1,0:T(8,128)(2,1)S(1)}, bf16[64,2048]{1,0:T(8,128)(2,1)S(1)}, u32[]{:S(2)}, u32[]{:S(2)}) collective-permute-start(bf16[64,2048]{1,0:T(8,128)(2,1)S(1)} %get-tuple-element.47.refs_0_), channel_id=1, source_target_pairs={{0,224},{32,0},{64,32},{96,64},{128,96},{160,128},{192,160},{224,1... | collective-permute-start | bytes 786440 | tf_op jit(solution)/shard_map/ppermute | solution.py:26
  146.3 8.6 %collective-permute-start.2 = (bf16[64,2048]{1,0:T(8,128)(2,1)S(1)}, bf16[64,2048]{1,0:T(8,128)(2,1)S(1)}, u32[]{:S(2)}, u32[]{:S(2)}) collective-permute-start(bf16[64,2048]{1,0:T(8,128)(2,1)S(1)} %get-tuple-element.47.refs_0_), channel_id=1, source_target_pairs={{0,32},{32,64},{64,96},{96,128},{128,160},{160,192},{192,224},{224... | collective-permute-start | bytes 786440 | tf_op jit(solution)/shard_map/ppermute | solution.py:26
  154.8 6.4 %collective-permute-start.5 = (bf16[64,2048]{1,0:T(8,128)(2,1)S(1)}, bf16[64,2048]{1,0:T(8,128)(2,1)S(1)}, u32[]{:S(2)}, u32[]{:S(2)}) collective-permute-start(bf16[64,2048]{1,0:T(8,128)(2,1)S(1)} %get-tuple-element.50.refs_0_), channel_id=1, source_target_pairs={{0,224},{32,0},{64,32},{96,64},{128,96},{160,128},{192,160},{224,1... | collective-permute-start | bytes 786440 | tf_op jit(solution)/shard_map/ppermute | solution.py:26
  155.2 7.7 %collective-permute-start.6 = (bf16[64,2048]{1,0:T(8,128)(2,1)S(1)}, bf16[64,2048]{1,0:T(8,128)(2,1)S(1)}, u32[]{:S(2)}, u32[]{:S(2)}) collective-permute-start(bf16[64,2048]{1,0:T(8,128)(2,1)S(1)} %get-tuple-element.50.refs_0_), channel_id=1, source_target_pairs={{0,32},{32,64},{64,96},{96,128},{128,160},{160,192},{192,224},{224... | collective-permute-start | bytes 786440 | tf_op jit(solution)/shard_map/ppermute | solution.py:26
  156.3 10.6 %collective-permute-start.3 = (bf16[64,2048]{1,0:T(8,128)(2,1)S(1)}, bf16[64,2048]{1,0:T(8,128)(2,1)S(1)}, u32[]{:S(2)}, u32[]{:S(2)}) collective-permute-start(bf16[64,2048]{1,0:T(8,128)(2,1)S(1)} %collective-permute-done.1.refs_1_), channel_id=1, source_target_pairs={{0,224},{32,0},{64,32},{96,64},{128,96},{160,128},{192,160},{224,1... | collective-permute-start | bytes 786440 | tf_op jit(solution)/shard_map/ppermute | solution.py:26
  157.8 10.6 %collective-permute-start.4 = (bf16[64,2048]{1,0:T(8,128)(2,1)S(1)}, bf16[64,2048]{1,0:T(8,128)(2,1)S(1)}, u32[]{:S(2)}, u32[]{:S(2)}) collective-permute-start(bf16[64,2048]{1,0:T(8,128)(2,1)S(1)} %collective-permute-done.2.refs_6_), channel_id=1, source_target_pairs={{0,32},{32,64},{64,96},{96,128},{128,160},{160,192},{192,224},{224... | collective-permute-start | bytes 786440 | tf_op jit(solution)/shard_map/ppermute | solution.py:26
  168.5 6.8 %collective-permute-start.10 = (bf16[64,2048]{1,0:T(8,128)(2,1)S(1)}, bf16[64,2048]{1,0:T(8,128)(2,1)S(1)}, u32[]{:S(2)}, u32[]{:S(2)}) collective-permute-start(bf16[64,2048]{1,0:T(8,128)(2,1)S(1)} %collective-permute-done.6.refs_6_), channel_id=1, source_target_pairs={{0,32},{32,64},{64,96},{96,128},{128,160},{160,192},{192,224},{224... | collective-permute-start | bytes 786440 | tf_op jit(solution)/shard_map/ppermute | solution.py:26
  168.5 6.8 %collective-permute-start.9 = (bf16[64,2048]{1,0:T(8,128)(2,1)S(1)}, bf16[64,2048]{1,0:T(8,128)(2,1)S(1)}, u32[]{:S(2)}, u32[]{:S(2)}) collective-permute-start(bf16[64,2048]{1,0:T(8,128)(2,1)S(1)} %collective-permute-done.5.refs_1_), channel_id=1, source_target_pairs={{0,224},{32,0},{64,32},{96,64},{128,96},{160,128},{192,160},{224,1... | collective-permute-start | bytes 786440 | tf_op jit(solution)/shard_map/ppermute | solution.py:26
  171.1 8.7 %collective-permute-start.7 = (bf16[64,2048]{1,0:T(8,128)(2,1)S(1)}, bf16[64,2048]{1,0:T(8,128)(2,1)S(1)}, u32[]{:S(2)}, u32[]{:S(2)}) collective-permute-start(bf16[64,2048]{1,0:T(8,128)(2,1)S(1)} %collective-permute-done.3.refs_2_), channel_id=1, source_target_pairs={{0,224},{32,0},{64,32},{96,64},{128,96},{160,128},{192,160},{224,1... | collective-permute-start | bytes 786440 | tf_op jit(solution)/shard_map/ppermute | solution.py:26
  171.2 9.7 %collective-permute-start.8 = (bf16[64,2048]{1,0:T(8,128)(2,1)S(1)}, bf16[64,2048]{1,0:T(8,128)(2,1)S(1)}, u32[]{:S(2)}, u32[]{:S(2)}) collective-permute-start(bf16[64,2048]{1,0:T(8,128)(2,1)S(1)} %collective-permute-done.4.refs_5_), channel_id=1, source_target_pairs={{0,32},{32,64},{64,96},{96,128},{128,160},{160,192},{192,224},{224... | collective-permute-start | bytes 786440 | tf_op jit(solution)/shard_map/ppermute | solution.py:26
  180.8 11.0 %collective-permute-start.13 = (bf16[64,2048]{1,0:T(8,128)(2,1)S(1)}, bf16[64,2048]{1,0:T(8,128)(2,1)S(1)}, u32[]{:S(2)}, u32[]{:S(2)}) collective-permute-start(bf16[64,2048]{1,0:T(8,128)(2,1)S(1)} %collective-permute-done.9.refs_2_), channel_id=1, source_target_pairs={{0,224},{32,0},{64,32},{96,64},{128,96},{160,128},{192,160},{224,1... | collective-permute-start | bytes 786440 | tf_op jit(solution)/shard_map/ppermute | solution.py:26
  183.3 8.6 %collective-permute-start.14 = (bf16[64,2048]{1,0:T(8,128)(2,1)S(1)}, bf16[64,2048]{1,0:T(8,128)(2,1)S(1)}, u32[]{:S(2)}, u32[]{:S(2)}) collective-permute-start(bf16[64,2048]{1,0:T(8,128)(2,1)S(1)} %collective-permute-done.10.refs_5_), channel_id=1, source_target_pairs={{0,32},{32,64},{64,96},{96,128},{128,160},{160,192},{192,224},{224... | collective-permute-start | bytes 786440 | tf_op jit(solution)/shard_map/ppermute | solution.py:26
  183.3 5.0 %collective-permute-start.11 = (bf16[64,1024]{1,0:T(8,128)(2,1)S(1)}, bf16[64,1024]{1,0:T(8,128)(2,1)S(1)}, u32[]{:S(2)}, u32[]{:S(2)}) collective-permute-start(bf16[64,1024]{1,0:T(8,128)(2,1)S(1)} %slice.98), channel_id=1, source_target_pairs={{0,224},{32,0},{64,32},{96,64},{128,96},{160,128},{192,160},{224,1... | collective-permute-start | bytes 393224 | tf_op jit(solution)/shard_map/ppermute | solution.py:26
  186.0 5.8 %collective-permute-start.12 = (bf16[64,1024]{1,0:T(8,128)(2,1)S(1)}, bf16[64,1024]{1,0:T(8,128)(2,1)S(1)}, u32[]{:S(2)}, u32[]{:S(2)}) collective-permute-start(bf16[64,1024]{1,0:T(8,128)(2,1)S(1)} %slice.99), channel_id=1, source_target_pairs={{0,32},{32,64},{64,96},{96,128},{128,160},{160,192},{192,224},{224... | collective-permute-start | bytes 393224 | tf_op jit(solution)/shard_map/ppermute | solution.py:26
  193.0 13.5 %collective-permute-start.15 = (f32[224,512]{1,0:T(8,128)S(1)}, f32[224,512]{1,0:T(8,128)S(1)}, u32[]{:S(2)}, u32[]{:S(2)}) collective-permute-start(f32[224,512]{1,0:T(8,128)S(1)} %fusion), channel_id=1, source_target_pairs={{0,2},{2,0},{1,3},{3,1},{4,6},{6,4},{5,7},{7,5},{8,10},{10,8},{9,1... | collective-permute-start | bytes 1376264 | tf_op jit(solution)/shard_map/ppermute | solution.py:26
  198.0 5.2 %collective-permute-start.17 = (bf16[64,1024]{1,0:T(8,128)(2,1)S(1)}, bf16[64,1024]{1,0:T(8,128)(2,1)S(1)}, u32[]{:S(2)}, u32[]{:S(2)}) collective-permute-start(bf16[64,1024]{1,0:T(8,128)(2,1)S(1)} %slice.79), channel_id=1, source_target_pairs={{0,224},{32,0},{64,32},{96,64},{128,96},{160,128},{192,160},{224,1... | collective-permute-start | bytes 393224 | tf_op jit(solution)/shard_map/ppermute | solution.py:26
  198.1 6.4 %collective-permute-start.18 = (bf16[64,1024]{1,0:T(8,128)(2,1)S(1)}, bf16[64,1024]{1,0:T(8,128)(2,1)S(1)}, u32[]{:S(2)}, u32[]{:S(2)}) collective-permute-start(bf16[64,1024]{1,0:T(8,128)(2,1)S(1)} %slice.80), channel_id=1, source_target_pairs={{0,32},{32,64},{64,96},{96,128},{128,160},{160,192},{192,224},{224... | collective-permute-start | bytes 393224 | tf_op jit(solution)/shard_map/ppermute | solution.py:26
  207.3 18.6 %collective-permute-start.16 = (f32[224,512]{1,0:T(8,128)S(1)}, f32[224,512]{1,0:T(8,128)S(1)}, u32[]{:S(2)}, u32[]{:S(2)}) collective-permute-start(f32[224,512]{1,0:T(8,128)S(1)} %convolution_add_fusion.sum_ref), channel_id=1, source_target_pairs={{0,1},{1,0},{2,3},{3,2},{4,5},{5,4},{6,7},{7,6},{8,9},{9,8},{10,11... | collective-permute-start | bytes 1376264 | tf_op jit(solution)/shard_map/ppermute | solution.py:26
  210.8 15.1 %collective-permute-start.20 = (f32[112,512]{1,0:T(8,128)S(1)}, f32[112,512]{1,0:T(8,128)S(1)}, u32[]{:S(2)}, u32[]{:S(2)}) collective-permute-start(f32[112,512]{1,0:T(8,128)S(1)} %convolution_add_fusion.1.hid_ref), channel_id=1, source_target_pairs={{0,1},{1,0},{2,3},{3,2},{4,5},{5,4},{6,7},{7,6},{8,9},{9,8},{10,11... | collective-permute-start | bytes 688136 | tf_op jit(solution)/shard_map/ppermute | solution.py:26
  231.1 7.7 %collective-permute-start.23 = (bf16[64,2048]{1,0:T(8,128)(2,1)}, bf16[64,2048]{1,0:T(8,128)(2,1)S(1)}, u32[]{:S(2)}, u32[]{:S(2)}) collective-permute-start(bf16[64,2048]{1,0:T(8,128)(2,1)} %slice.144), channel_id=1, source_target_pairs={{0,224},{32,0},{64,32},{96,64},{128,96},{160,128},{192,160},{224,1... | collective-permute-start | bytes 786440 | tf_op jit(solution)/shard_map/ppermute | solution.py:26
  233.7 8.8 %collective-permute-start.22 = (bf16[64,2048]{1,0:T(8,128)(2,1)}, bf16[64,2048]{1,0:T(8,128)(2,1)S(1)}, u32[]{:S(2)}, u32[]{:S(2)}) collective-permute-start(bf16[64,2048]{1,0:T(8,128)(2,1)} %slice.145), channel_id=1, source_target_pairs={{0,32},{32,64},{64,96},{96,128},{128,160},{160,192},{192,224},{224... | collective-permute-start | bytes 786440 | tf_op jit(solution)/shard_map/ppermute | solution.py:26
  246.6 29.2 %collective-permute-start.31 = (bf16[112,2048]{1,0:T(8,128)(2,1)S(1)}, bf16[112,2048]{1,0:T(8,128)(2,1)S(1)}, u32[]{:S(2)}, u32[]{:S(2)}) collective-permute-start(bf16[112,2048]{1,0:T(8,128)(2,1)S(1)} %convolution_convert_fusion.2), channel_id=1, source_target_pairs={{0,2},{2,0},{1,3},{3,1},{4,6},{6,4},{5,7},{7,5},{8,10},{10,8},{9,1... | collective-permute-start | bytes 1376264 | tf_op jit(solution)/shard_map/ppermute | solution.py:26
  248.0 51.4 %collective-permute-start.30 = (bf16[224,2048]{1,0:T(8,128)(2,1)}, bf16[224,2048]{1,0:T(8,128)(2,1)}, u32[]{:S(2)}, u32[]{:S(2)}) collective-permute-start(bf16[224,2048]{1,0:T(8,128)(2,1)} %convolution_convert_fusion), channel_id=1, source_target_pairs={{0,2},{2,0},{1,3},{3,1},{4,6},{6,4},{5,7},{7,5},{8,10},{10,8},{9,1... | collective-permute-start | bytes 2752520 | tf_op jit(solution)/shard_map/ppermute | solution.py:26
  248.2 12.6 %collective-permute-start.27 = (bf16[64,4096]{1,0:T(8,128)(2,1)S(1)}, bf16[64,4096]{1,0:T(8,128)(2,1)S(1)}, u32[]{:S(2)}, u32[]{:S(2)}) collective-permute-start(bf16[64,4096]{1,0:T(8,128)(2,1)S(1)} %shard_map.103), channel_id=1, source_target_pairs={{0,224},{32,0},{64,32},{96,64},{128,96},{160,128},{192,160},{224,1... | collective-permute-start | bytes 1572872 | tf_op jit(solution)/shard_map/ppermute | solution.py:26
  248.6 13.9 %collective-permute-start.24 = (bf16[64,4096]{1,0:T(8,128)(2,1)S(1)}, bf16[64,4096]{1,0:T(8,128)(2,1)S(1)}, u32[]{:S(2)}, u32[]{:S(2)}) collective-permute-start(bf16[64,4096]{1,0:T(8,128)(2,1)S(1)} %shard_map.100), channel_id=1, source_target_pairs={{0,32},{32,64},{64,96},{96,128},{128,160},{160,192},{192,224},{224... | collective-permute-start | bytes 1572872 | tf_op jit(solution)/shard_map/ppermute | solution.py:26
  260.9 11.5 %collective-permute-start.28 = (bf16[64,4096]{1,0:T(8,128)(2,1)S(1)}, bf16[64,4096]{1,0:T(8,128)(2,1)S(1)}, u32[]{:S(2)}, u32[]{:S(2)}) collective-permute-start(bf16[64,4096]{1,0:T(8,128)(2,1)S(1)} %shard_map.104), channel_id=1, source_target_pairs={{0,224},{32,0},{64,32},{96,64},{128,96},{160,128},{192,160},{224,1... | collective-permute-start | bytes 1572872 | tf_op jit(solution)/shard_map/ppermute | solution.py:26
  262.6 13.0 %collective-permute-start.25 = (bf16[64,4096]{1,0:T(8,128)(2,1)S(1)}, bf16[64,4096]{1,0:T(8,128)(2,1)S(1)}, u32[]{:S(2)}, u32[]{:S(2)}) collective-permute-start(bf16[64,4096]{1,0:T(8,128)(2,1)S(1)} %shard_map.101), channel_id=1, source_target_pairs={{0,32},{32,64},{64,96},{96,128},{128,160},{160,192},{192,224},{224... | collective-permute-start | bytes 1572872 | tf_op jit(solution)/shard_map/ppermute | solution.py:26
  272.5 11.7 %collective-permute-start.29 = (bf16[64,4096]{1,0:T(8,128)(2,1)S(1)}, bf16[64,4096]{1,0:T(8,128)(2,1)S(1)}, u32[]{:S(2)}, u32[]{:S(2)}) collective-permute-start(bf16[64,4096]{1,0:T(8,128)(2,1)S(1)} %shard_map.105), channel_id=1, source_target_pairs={{0,224},{32,0},{64,32},{96,64},{128,96},{160,128},{192,160},{224,1... | collective-permute-start | bytes 1572872 | tf_op jit(solution)/shard_map/ppermute | solution.py:26
  275.7 11.8 %collective-permute-start.26 = (bf16[64,4096]{1,0:T(8,128)(2,1)S(1)}, bf16[64,4096]{1,0:T(8,128)(2,1)S(1)}, u32[]{:S(2)}, u32[]{:S(2)}) collective-permute-start(bf16[64,4096]{1,0:T(8,128)(2,1)S(1)} %shard_map.102), channel_id=1, source_target_pairs={{0,32},{32,64},{64,96},{96,128},{128,160},{160,192},{192,224},{224... | collective-permute-start | bytes 1572872 | tf_op jit(solution)/shard_map/ppermute | solution.py:26
  288.8 22.0 %all-to-all-start.1 = ((bf16[32,2,4096]{2,1,0:T(2,128)(2,1)}), bf16[32,2,4096]{2,1,0:T(2,128)(2,1)S(1)}, u32[]{:S(2)}, u32[]{:S(2)}) async-start(bf16[32,2,4096]{2,1,0:T(2,128)(2,1)} %shard_map.106), calls=%async_computation.1 | async-start | bytes 1048576 | tf_op jit(solution)/shard_map/all_to_all | solution.py:30
  (16 other events, 80.6 us)

commit v3 on v2

v3 whole, which is shorter than its diff:
```python
import functools

import jax
import jax.numpy as jnp
from jax import lax
from jax.experimental import pallas as pl
from jax.experimental.pallas import tpu as pltpu
from jax.sharding import Mesh
from jax.sharding import PartitionSpec as P

AXES = ("z", "y", "x", "core", "tok")
BLK = ("z", "y", "x", "core")
PLANE = ("y", "x")
PAIRS = ("tok", "core")
F32 = jnp.float32
BF16 = jnp.bfloat16
VMEM = pl.BlockSpec(memory_space=pltpu.VMEM)
SMEM = pl.BlockSpec(memory_space=pltpu.SMEM)
PARAMS = pltpu.CompilerParams(vmem_limit_bytes=20 * 1024 * 1024)
LARGE = pltpu.CompilerParams(vmem_limit_bytes=58 * 1024 * 1024)


def shifted(block, axis, distance):
    count = lax.axis_size(axis)
    return lax.ppermute(block, axis, [(i, (i + distance) % count) for i in range(count)])


def exchanged(blocks, axes):
    return lax.all_to_all(blocks, axes, 0, 0, tiled=True)


def by_rows(left, right):
    return lax.dot_general(left, right, (((1,), (1,)), ((), ())), preferred_element_type=F32)


def by_columns(left, right):
    return lax.dot_general(left, right, (((0,), (0,)), ((), ())), preferred_element_type=F32)


def called(kernel, out_shape, *args, specs=None, scratch=(), **kwargs):
    specs = specs or [VMEM] * len(args)
    return pl.pallas_call(
        functools.partial(kernel, **kwargs),
        out_shape=out_shape,
        in_specs=specs,
        out_specs=jax.tree.map(lambda _: VMEM, out_shape),
        scratch_shapes=scratch,
        compiler_params=PARAMS,
    )(*args)


def called_at(kernel, out_shape, places, *args, index=None, scratch=(), params=PARAMS, **kwargs):
    def whole(shape):
        return pl.BlockSpec(shape, lambda *_: (0,) * len(shape))

    specs = [
        whole(arg.shape) if place is None else pl.BlockSpec(*place)
        for arg, place in zip(args, places, strict=True)
    ]
    grid = pltpu.PrefetchScalarGridSpec(
        num_scalar_prefetch=1,
        grid=(1,),
        in_specs=specs,
        out_specs=jax.tree.map(lambda o: whole(o.shape), out_shape),
        scratch_shapes=scratch,
    )
    return pl.pallas_call(
        functools.partial(kernel, **kwargs),
        out_shape=out_shape,
        grid_spec=grid,
        compiler_params=params,
    )(jnp.zeros((1,), jnp.int32) if index is None else index, *args)


def shape_of(shape, kind=BF16):
    return jax.ShapeDtypeStruct(shape, kind)


def deal_kernel(tokens_ref, upstream_ref, out_ref, *, quarters):
    part = tokens_ref.shape[1] // quarters
    for q in range(quarters):
        rows = tokens_ref[:, q * part : (q + 1) * part]
        grads = upstream_ref[:, q * part : (q + 1) * part]
        for j in range(out_ref.shape[0] // quarters):
            out_ref[j * quarters + q, :, :part] = rows
            out_ref[j * quarters + q, :, part:] = grads


def merge_kernel(blocks_ref, out_ref, rows_ref):
    n, pair, _ = blocks_ref.shape
    for j in range(n):
        rows_ref[j * pair : (j + 1) * pair, :] = blocks_ref[j].astype(F32)
    out_ref[...] = rows_ref[...].astype(BF16)


def pack_kernel(_, gate_ref, up_ref, down_ref, out_ref):
    units = gate_ref.shape[0]
    for j, ref in enumerate((gate_ref, up_ref, down_ref)):
        out_ref[j * units : (j + 1) * units, :] = ref[...]


def weights_kernel(_, gate_ref, up_ref, down_ref, got_ref, in_ref, out_ref):
    units = gate_ref.shape[0]
    in_ref[:units, :] = gate_ref[...]
    in_ref[units : 2 * units, :] = up_ref[...]
    in_ref[2 * units :, :] = got_ref[: 2 * units, :]
    out_ref[:units, :] = down_ref[...]
    out_ref[units:, :] = got_ref[2 * units :, :]


def stack_kernel(*refs):
    *block_refs, rows_ref, grads_ref = refs
    part = rows_ref.shape[1]
    k = 0
    for ref in block_refs:
        height, width = ref.shape
        at = slice(k * height, (k + 1) * height)
        if width == 2 * part:
            rows_ref[at, :] = ref[:, :part]
            grads_ref[at, :] = ref[:, part:]
            k += 1
        elif ref is block_refs[-2]:
            rows_ref[at, :] = ref[...]
        else:
            grads_ref[at, :] = ref[...]
            k += 1


def partial_kernel(rows_ref, grads_ref, in_ref, out_ref, own_ref, other_ref):
    units = out_ref.shape[0] // 2
    rows, grads = rows_ref[...], grads_ref[...]
    for j, ref in enumerate((own_ref, other_ref)):
        ref[: 2 * units, :] = by_rows(in_ref[2 * j * units : 2 * (j + 1) * units, :], rows)
        ref[2 * units :, :] = by_rows(out_ref[j * units : (j + 1) * units, :], grads)


def middle_kernel(sum_ref, got_ref, out_ref):
    units = sum_ref.shape[0] // 3
    total = sum_ref[...] + got_ref[...]
    gate_value, up_value = total[:units, :], total[units : 2 * units, :]
    hidden_grad = total[2 * units :, :]
    gate_sigmoid = jax.nn.sigmoid(gate_value)
    swish_gate = gate_value * gate_sigmoid
    gate_grad = hidden_grad * up_value * gate_sigmoid * (1.0 + gate_value * (1.0 - gate_sigmoid))
    out_ref[:units, :] = gate_grad.astype(BF16)
    out_ref[units : 2 * units, :] = (hidden_grad * swish_gate).astype(BF16)
    out_ref[2 * units :, :] = (swish_gate * up_value).astype(BF16)


def pair_kernel(own_ref, got_ref, in_ref, hidden_ref):
    double = in_ref.shape[0] // 2
    in_ref[:double, :] = own_ref[:double, :]
    in_ref[double:, :] = got_ref[:double, :]
    hidden_ref[: double // 2, :] = own_ref[double:, :]
    hidden_ref[double // 2 :, :] = got_ref[double:, :]


def turn_kernel(_, left_ref, right_ref, came_ref, out_ref, *, whole, up):
    width = left_ref.shape[1]
    left, right = left_ref[...], right_ref[...]
    if whole or up:
        left = left + came_ref[:, :width].astype(F32)
    if whole or not up:
        right = right + came_ref[:, came_ref.shape[1] - width :].astype(F32)
    out_ref[:, :width] = left.astype(BF16)
    out_ref[:, width:] = right.astype(BF16)


def close_kernel(_, left_ref, right_ref, came_up_ref, came_down_ref, out_ref, rows_ref):
    n, pair, _ = out_ref.shape
    width = left_ref.shape[1]
    came = came_up_ref[...].astype(F32) + came_down_ref[...].astype(F32)
    rows_ref[:, :width] = left_ref[...] + came[:, :width]
    rows_ref[:, width:] = right_ref[...] + came[:, width:]
    for j in range(n):
        out_ref[j] = rows_ref[j * pair : (j + 1) * pair, :].astype(BF16)


def total_kernel(blocks_ref, mixed_ref, input_ref, *, quarters):
    part = mixed_ref.shape[1] // quarters
    for q in range(quarters):
        total = blocks_ref[q].astype(F32)
        for j in range(1, blocks_ref.shape[0] // quarters):
            total = total + blocks_ref[j * quarters + q].astype(F32)
        total = total.astype(BF16)
        mixed_ref[:, q * part : (q + 1) * part] = total[:, :part]
        input_ref[:, q * part : (q + 1) * part] = total[:, part:]


def ring_reduced(terms, later, height, pair):
    count = lax.axis_size("z")
    half = count // 2

    def added(kernel, out_shape, k, *came, scratch=(), **kwargs):
        found, j = terms[k % count]
        place = ((height, found[0].shape[1]), lambda *_: (j, 0))
        places = [place, place] + [None] * len(came)
        return called_at(kernel, out_shape, places, *found, *came, scratch=scratch, **kwargs)

    found, j = terms[half]
    width = found[0].shape[1]
    up, down = (f[j * height : (j + 1) * height].astype(BF16) for f in found)
    both = shape_of((height, 2 * width))
    for k in range(half - 1, 0, -1):
        up, down = shifted(up, "z", 1), shifted(down, "z", -1)
        if k in later:
            up, down = later[k](up, down)
        up = added(turn_kernel, both, k, up, whole=k < half - 1, up=True)
        down = added(turn_kernel, both, -k, down, whole=k < half - 1, up=False)
    up, down = shifted(up, "z", 1), shifted(down, "z", -1)
    return added(
        close_kernel,
        shape_of((height // pair, pair, 2 * width)),
        0,
        up,
        down,
        scratch=[pltpu.VMEM((height, 2 * width), F32)],
    )


def local(tokens, upstream, gate_weight, up_weight, down_weight):
    core = lax.axis_index("core")
    tok = lax.axis_index("tok")
    n_z = lax.axis_size("z")
    n_plane = lax.axis_size("y") * lax.axis_size("x")
    n_core = lax.axis_size("core")
    quarters = n_core * lax.axis_size("tok")
    pair, width = tokens.shape
    part = width // quarters
    units = gate_weight.shape[0]
    n = pair * quarters
    n_rows = n_plane * n
    own_at = (tok * n_core + core).astype(jnp.int32).reshape(1)
    other_at = (tok * n_core + 1 - core).astype(jnp.int32).reshape(1)

    dealt = called(
        deal_kernel,
        shape_of((n_plane * quarters, pair, 2 * part)),
        tokens,
        upstream,
        quarters=quarters,
    )
    dealt, *weights = lax.optimization_barrier((dealt, gate_weight, up_weight, down_weight))
    column = ((units, part), lambda i, at: (0, at[0]))
    sent = called_at(
        pack_kernel,
        shape_of((3 * units, part)),
        [column] * 3,
        *weights,
        index=other_at,
        params=LARGE,
    )
    in_weights, out_weights = called_at(
        weights_kernel,
        (shape_of((4 * units, part)), shape_of((2 * units, part))),
        [column] * 3 + [None],
        *weights,
        shifted(sent, "core", 1),
        index=own_at,
        params=LARGE,
    )
    dealt = exchanged(dealt, (*PLANE, *PAIRS))
    dealt, in_weights, out_weights = lax.optimization_barrier((dealt, in_weights, out_weights))
    block = called(
        merge_kernel,
        shape_of((n_rows, 2 * part)),
        dealt,
        scratch=[pltpu.VMEM((n_rows, 2 * part), F32)],
    )

    def stacked(*blocks):
        shape = shape_of((half * n_rows, part))
        return called(stack_kernel, (shape, shape), *blocks)

    def partial_sums(rows, grads):
        shape = shape_of((3 * units, rows.shape[0]), F32)
        return called(partial_kernel, (shape, shape), rows, grads, in_weights, out_weights)

    def factors(sums, got):
        own = called(middle_kernel, shape_of(sums.shape), sums, got)
        return called(
            pair_kernel,
            (
                shape_of((4 * units, sums.shape[1])),
                shape_of((2 * units, sums.shape[1])),
            ),
            own,
            shifted(own, "core", 1),
        )

    half = n_z // 2
    ring = {0: block}
    for k in range(1, half):
        ring[k], ring[-k] = shifted(ring[k - 1], "z", -1), shifted(ring[1 - k], "z", 1)
    near_rows, near_grads = stacked(*(ring[k] for k in range(-half // 2, half // 2)))
    own, other = partial_sums(near_rows, near_grads)
    ahead, behind, own, other = lax.optimization_barrier((ring[half - 1], ring[1 - half], own, other))
    left, right = shifted(ahead[:, :part], "z", -1), shifted(behind[:, part:], "z", 1)
    left, right, near_sums = lax.optimization_barrier(
        (left, right, own + shifted(other, "core", 1))
    )
    near_got = shifted(near_sums, "tok", 1)
    far_rows, far_grads = stacked(
        *(ring[k] for k in range(half // 2, half)),
        *(ring[k] for k in range(1 - half, -half // 2)),
        left,
        right,
    )
    own, other = partial_sums(far_rows, far_grads)
    far_sums = own + shifted(other, "core", 1)
    far_in, far_hidden = factors(far_sums, shifted(far_sums, "tok", 1))
    near_in, near_hidden = factors(near_sums, near_got)

    terms = {}

    def set_terms(places, hidden, in_grads):
        found = (by_columns(hidden, out_weights), by_columns(in_grads, in_weights))
        for j, k in enumerate(places):
            terms[k % n_z] = found, j

    far_places = [*range(half // 2, half), *range(1 - half, -half // 2), half]
    set_terms(far_places, far_hidden, far_in)
    grads_out = []

    def near_terms(up, down):
        nonlocal near_in, near_hidden
        up, down, near_in, near_hidden = lax.optimization_barrier(
            (up, down, near_in, near_hidden)
        )
        set_terms(range(-half // 2, half // 2), near_hidden, near_in)
        return up, down

    def weight_product(near, far, near_right, far_right):
        total = jnp.dot(near, near_right, preferred_element_type=F32)
        total = total + jnp.dot(far, far_right, preferred_element_type=F32)
        return total.astype(BF16)

    def others_grads(up, down):
        up, down, a, b, c, d = lax.optimization_barrier(
            (up, down, near_in, far_in, near_hidden, far_hidden)
        )
        in_other = weight_product(a[2 * units :], b[2 * units :], near_rows, far_rows)
        out_other = weight_product(c[units:], d[units:], near_grads, far_grads)
        grads_out.extend([shifted(in_other, "core", 1), shifted(out_other, "core", 1)])
        return up, down

    def own_grads(up, down):
        up, down, a, b, c, d = lax.optimization_barrier(
            (up, down, near_in, far_in, near_hidden, far_hidden)
        )
        grads_out.append(weight_product(a[: 2 * units], b[: 2 * units], near_rows, far_rows))
        grads_out.append(weight_product(c[:units], d[:units], near_grads, far_grads))
        return up, down

    later = {half - 1: near_terms, half - 2: others_grads, half - 3: own_grads}
    summed = ring_reduced(terms, later, n_rows, pair)
    mixed, input_grad = called(
        total_kernel,
        (shape_of((pair, width)), shape_of((pair, width))),
        exchanged(summed, (*PLANE, *PAIRS)),
        quarters=quarters,
    )
    got_in, got_out, in_weight_grad, out_weight_grad = grads_out

    def side_by_side(mine, others):
        left = jnp.where(core == 0, mine, others)
        right = jnp.where(core == 0, others, mine)
        return jnp.concatenate([left, right], axis=1)

    return (
        mixed,
        input_grad,
        side_by_side(in_weight_grad[:units], got_in[:units]),
        side_by_side(in_weight_grad[units:], got_in[units:]),
        side_by_side(out_weight_grad, got_out),
    )


def solution(mesh):
    finer = Mesh(mesh.devices.reshape(8, 4, 2, 2, mesh.shape["tok"]), AXES)
    return jax.shard_map(
        local,
        mesh=finer,
        in_specs=(P(AXES, None), P(AXES, None), P(BLK, None), P(BLK, None), P(BLK, None)),
        out_specs=(P(AXES, None), P(AXES, None), P(BLK, "tok"), P(BLK, "tok"), P(BLK, "tok")),
        check_vma=False,
    )
```

time: 312 us -> 189 us (0.61)
  Pallas kernels: 132 us -> 15.7 us
  starting transfers between devices: 58.8 us -> 51.3 us
  matrix products: 11.7 us -> 5.24 us
  waiting for transfers between devices: 97.8 us -> 104 us
    pallas_call x4 -> x0, Pallas kernels: 128 us -> none  [moved(): pl.pallas_call(kernel, out_shape=out_shape, in_specs=([] if at is None el...]
    all_to_all x2, waiting for transfers between devices: 8.8 us -> 16.9 us  [exchanged(): return lax.all_to_all(blocks, axes, 0, 0, tiled=True)]
    pallas_call x7 -> x9, Pallas kernels: 1.84 us -> 9.66 us  [called_at(): pl.pallas_call(functools.partial(kernel, **kwargs), out_shape=out_shape,...]
    dot_general x8, matrix products: 8.87 us -> 2.87 us  [the longest x4 1.44 us: weight_product(): total = total + jnp.dot(far, far_right, preferred_element_type=F32)]
    all_to_all x2, starting transfers between devices: 16 us -> 11.6 us  [exchanged(): return lax.all_to_all(blocks, axes, 0, 0, tiled=True)]
    pallas_call x5 -> x11, Pallas kernels: 2.09 us -> 6.07 us  [called(): pl.pallas_call(functools.partial(kernel, **kwargs), out_shape=out_shape,...]
    ppermute x32 -> x25, starting transfers between devices: 42.8 us -> 39.7 us  [shifted(): lax.ppermute(block, axis, [(i, (i + distance) % count) for i in range(cou...]
    ppermute x32 -> x25, waiting for transfers between devices: 89 us -> 87.3 us  [shifted(): lax.ppermute(block, axis, [(i, (i + distance) % count) for i in range(cou...]
  transfers between devices with their start and end apart: 34 -> 27, of which waited for: 22 -> 17; matrix products, arithmetic and copies ran while one was open for 3% -> 5% of each run, Pallas kernels for 28% -> 4%
where the time goes in v3:
time: 189 us; the launch traced here: 188 us
  waiting for transfers between devices  104 us (55%)
  starting transfers between devices  51.3 us (27%)
  Pallas kernels  15.7 us (8%)
  local copies, waits for them, and re-layouts  7.92 us (4%)
  matrix products  5.24 us (3%)
  other arithmetic  2.55 us (1%)
    ppermute x25, waiting for transfers between devices, shifted(): lax.ppermute(block, axis, [(i, (i + distance) % count) for i in range(cou...  87.3 us
    ppermute x25, starting transfers between devices, shifted(): lax.ppermute(block, axis, [(i, (i + distance) % count) for i in range(cou...  39.7 us
    all_to_all x2, waiting for transfers between devices, exchanged(): return lax.all_to_all(blocks, axes, 0, 0, tiled=True)  16.9 us
    all_to_all x2, starting transfers between devices, exchanged(): return lax.all_to_all(blocks, axes, 0, 0, tiled=True)  11.6 us
    pallas_call x9, Pallas kernels, called_at(): pl.pallas_call(functools.partial(kernel, **kwargs), out_shape=out_shape,...  9.66 us
    unnamed x34, local copies, waits for them, and re-layouts  6.41 us
    pallas_call x11, Pallas kernels, called(): pl.pallas_call(functools.partial(kernel, **kwargs), out_shape=out_shape,...  6.07 us
  transfers between devices with their start and end apart: 27, of which 17 were waited for; matrix products, arithmetic and copies ran while one was open for 5% of the time, Pallas kernels for 4%

profile of v3, /device:TPU:1, one launch (start us, length us, event | category | flops | bytes accessed | tf_op | source)
XLA Modules:
  0.0 187.9 jit_solution(9268853096632424501)
XLA Ops:
  3.0 2.5 %shard_map.93 = bf16[336,2048]{1,0:T(8,128)(2,1)} custom-call(s32[1]{0:T(128)} %bitcast.1._, bf16[112,8192]{1,0:T(8,128)(2,1)} %gate_ref.1, bf16[112,8192]{1,0:T(8,128)(2,1)} %up_ref.1, bf16[112,8192]{1,0:T(8,128)(2,1)} %down_ref.1), custom_call_target="tpu_custom_call" | custom-call | tf_op jit(solution)/shard_map/pallas_call | solution.py:67
  5.5 3.2 %collective-permute-start = (bf16[336,2048]{1,0:T(8,128)(2,1)}, bf16[336,2048]{1,0:T(8,128)(2,1)S(1)}, u32[]{:S(2)}, u32[]{:S(2)}) collective-permute-start(bf16[336,2048]{1,0:T(8,128)(2,1)} %shard_map.93), channel_id=1, source_target_pairs={{0,2},{2,0},{1,3},{3,1},{4,6},{6,4},{5,7},{7,5},{8,10},{10,8},{9,1... | collective-permute-start | bytes 4128776 | tf_op jit(solution)/shard_map/ppermute | solution.py:25
  8.7 5.5 %all-to-all-start = ((bf16[32,2,4096]{2,1,0:T(2,128)(2,1)}), bf16[32,2,4096]{2,1,0:T(2,128)(2,1)S(1)}, u32[]{:S(2)}, u32[]{:S(2)}) async-start(bf16[32,2,4096]{2,1,0:T(2,128)(2,1)} %shard_map.92), calls=%async_computation | async-start | bytes 1048576 | tf_op jit(solution)/shard_map/all_to_all | solution.py:29
  15.3 3.4 %shard_map.94 = (bf16[448,2048]{1,0:T(8,128)(2,1)}, bf16[224,2048]{1,0:T(8,128)(2,1)}) custom-call(s32[1]{0:T(128)} %bitcast._, bf16[112,8192]{1,0:T(8,128)(2,1)} %gate_ref.1, bf16[112,8192]{1,0:T(8,128)(2,1)} %up_ref.1, bf16[112,8192]{1,0:T(8,128)(2,1)} %down_ref.1, bf16[336,2048]{1,0:T(8,128)(2,1)} %copy-done.16), custom_call_target="tpu_custom_call" | custom-call | tf_op jit(solution)/shard_map/pallas_call | solution.py:67
  18.8 6.9 %all-to-all-done.blocks_ref = bf16[32,2,4096]{2,1,0:T(2,128)(2,1)S(1)} async-done(((bf16[32,2,4096]{2,1,0:T(2,128)(2,1)}), bf16[32,2,4096]{2,1,0:T(2,128)(2,1)S(1)}, u32[]{:S(2)}, u32[]{:S(2)}) %all-to-all-start) | async-done | bytes 524320 | tf_op jit(solution)/shard_map/all_to_all | solution.py:29
  26.0 1.7 collective-permute-start.4
  27.7 4.0 %collective-permute-start.1 = (bf16[64,4096]{1,0:T(8,128)(2,1)S(1)}, bf16[64,4096]{1,0:T(8,128)(2,1)S(1)}, u32[]{:S(2)}, u32[]{:S(2)}) collective-permute-start(bf16[64,4096]{1,0:T(8,128)(2,1)S(1)} %shard_map.95.refs_2_), channel_id=1, source_target_pairs={{0,224},{32,0},{64,32},{96,64},{128,96},{160,128},{192,160},{224,1... | collective-permute-start | bytes 1572872 | tf_op jit(solution)/shard_map/ppermute | solution.py:25
  31.7 12.2 %collective-permute-done.4.refs_1_ = bf16[64,4096]{1,0:T(8,128)(2,1)S(1)} collective-permute-done((bf16[64,4096]{1,0:T(8,128)(2,1)S(1)}, bf16[64,4096]{1,0:T(8,128)(2,1)S(1)}, u32[]{:S(2)}, u32[]{:S(2)}) %collective-permute-start.4) | collective-permute-done | bytes 524320 | tf_op jit(solution)/shard_map/ppermute | solution.py:25
  43.9 2.7 %collective-permute-start.2 = (bf16[64,4096]{1,0:T(8,128)(2,1)S(1)}, bf16[64,4096]{1,0:T(8,128)(2,1)S(1)}, u32[]{:S(2)}, u32[]{:S(2)}) collective-permute-start(bf16[64,4096]{1,0:T(8,128)(2,1)S(1)} %collective-permute-done.1.refs_3_), channel_id=1, source_target_pairs={{0,224},{32,0},{64,32},{96,64},{128,96},{160,128},{192,160},{224,1... | collective-permute-start | bytes 1572872 | tf_op jit(solution)/shard_map/ppermute | solution.py:25
  46.6 11.4 %collective-permute-done.5.refs_0_ = bf16[64,4096]{1,0:T(8,128)(2,1)S(1)} collective-permute-done((bf16[64,4096]{1,0:T(8,128)(2,1)S(1)}, bf16[64,4096]{1,0:T(8,128)(2,1)S(1)}, u32[]{:S(2)}, u32[]{:S(2)}) %collective-permute-start.5) | collective-permute-done | bytes 524320 | tf_op jit(solution)/shard_map/ppermute | solution.py:25
  58.0 2.7 %collective-permute-start.3 = (bf16[64,4096]{1,0:T(8,128)(2,1)S(1)}, bf16[64,4096]{1,0:T(8,128)(2,1)S(1)}, u32[]{:S(2)}, u32[]{:S(2)}) collective-permute-start(bf16[64,4096]{1,0:T(8,128)(2,1)S(1)} %collective-permute-done.2.refs_0_), channel_id=1, source_target_pairs={{0,224},{32,0},{64,32},{96,64},{128,96},{160,128},{192,160},{224,1... | collective-permute-start | bytes 1572872 | tf_op jit(solution)/shard_map/ppermute | solution.py:25
  62.3 8.9 %collective-permute-done.6.refs_2_ = bf16[64,4096]{1,0:T(8,128)(2,1)S(1)} collective-permute-done((bf16[64,4096]{1,0:T(8,128)(2,1)S(1)}, bf16[64,4096]{1,0:T(8,128)(2,1)S(1)}, u32[]{:S(2)}, u32[]{:S(2)}) %collective-permute-start.6) | collective-permute-done | bytes 524320 | tf_op jit(solution)/shard_map/ppermute | solution.py:25
  71.2 2.4 %collective-permute-start.9 = (f32[336,256]{1,0:T(8,128)S(1)}, f32[336,256]{1,0:T(8,128)S(1)}, u32[]{:S(2)}, u32[]{:S(2)}) collective-permute-start(f32[336,256]{1,0:T(8,128)S(1)} %get-tuple-element.67), channel_id=1, source_target_pairs={{0,2},{2,0},{1,3},{3,1},{4,6},{6,4},{5,7},{7,5},{8,10},{10,8},{9,1... | collective-permute-start | bytes 1032200 | tf_op jit(solution)/shard_map/ppermute | solution.py:25
  73.7 2.8 %collective-permute-start.7 = (bf16[64,2048]{1,0:T(8,128)(2,1)S(1)}, bf16[64,2048]{1,0:T(8,128)(2,1)S(1)}, u32[]{:S(2)}, u32[]{:S(2)}) collective-permute-start(bf16[64,2048]{1,0:T(8,128)(2,1)S(1)} %slice.50), channel_id=1, source_target_pairs={{0,224},{32,0},{64,32},{96,64},{128,96},{160,128},{192,160},{224,1... | collective-permute-start | bytes 786440 | tf_op jit(solution)/shard_map/ppermute | solution.py:25
  76.5 6.3 %collective-permute-done.8.refs_4_ = bf16[64,2048]{1,0:T(8,128)(2,1)S(1)} collective-permute-done((bf16[64,2048]{1,0:T(8,128)(2,1)S(1)}, bf16[64,2048]{1,0:T(8,128)(2,1)S(1)}, u32[]{:S(2)}, u32[]{:S(2)}) %collective-permute-start.8) | collective-permute-done | bytes 262176 | tf_op jit(solution)/shard_map/ppermute | solution.py:25
  87.7 9.8 %collective-permute-done.11.got_ref = f32[336,256]{1,0:T(8,128)S(1)} collective-permute-done((f32[336,256]{1,0:T(8,128)S(1)}, f32[336,256]{1,0:T(8,128)S(1)}, u32[]{:S(2)}, u32[]{:S(2)}) %collective-permute-start.11) | collective-permute-done | bytes 344096 | tf_op jit(solution)/shard_map/ppermute | solution.py:25
  97.6 1.5 collective-permute-start.12
  101.3 1.7 collective-permute-start.13
  107.3 2.9 %collective-permute-done.15.got_ref = f32[336,256]{1,0:T(8,128)S(1)} collective-permute-done((f32[336,256]{1,0:T(8,128)S(1)}, f32[336,256]{1,0:T(8,128)S(1)}, u32[]{:S(2)}, u32[]{:S(2)}) %collective-permute-start.15) | collective-permute-done | bytes 344096 | tf_op jit(solution)/shard_map/ppermute | solution.py:25
  113.4 1.6 copy-done.1
  117.1 3.0 %collective-permute-start.18 = (bf16[64,4096]{1,0:T(8,128)(2,1)S(1)}, bf16[64,4096]{1,0:T(8,128)(2,1)S(1)}, u32[]{:S(2)}, u32[]{:S(2)}) collective-permute-start(bf16[64,4096]{1,0:T(8,128)(2,1)S(1)} %shard_map.105), channel_id=1, source_target_pairs={{0,224},{32,0},{64,32},{96,64},{128,96},{160,128},{192,160},{224,1... | collective-permute-start | bytes 1572872 | tf_op jit(solution)/shard_map/ppermute | solution.py:25
  121.3 8.8 %collective-permute-done.18.came_ref = bf16[64,4096]{1,0:T(8,128)(2,1)S(1)} collective-permute-done((bf16[64,4096]{1,0:T(8,128)(2,1)S(1)}, bf16[64,4096]{1,0:T(8,128)(2,1)S(1)}, u32[]{:S(2)}, u32[]{:S(2)}) %collective-permute-start.18) | collective-permute-done | bytes 524320 | tf_op jit(solution)/shard_map/ppermute | solution.py:25
  130.1 3.1 %collective-permute-done.17.came_ref = bf16[64,4096]{1,0:T(8,128)(2,1)S(1)} collective-permute-done((bf16[64,4096]{1,0:T(8,128)(2,1)S(1)}, bf16[64,4096]{1,0:T(8,128)(2,1)S(1)}, u32[]{:S(2)}, u32[]{:S(2)}) %collective-permute-start.17) | collective-permute-done | bytes 524320 | tf_op jit(solution)/shard_map/ppermute | solution.py:25
  134.9 2.5 %collective-permute-start.24 = (bf16[112,2048]{1,0:T(8,128)(2,1)S(1)}, bf16[112,2048]{1,0:T(8,128)(2,1)S(1)}, u32[]{:S(2)}, u32[]{:S(2)}) collective-permute-start(bf16[112,2048]{1,0:T(8,128)(2,1)S(1)} %fusion.3), channel_id=1, source_target_pairs={{0,2},{2,0},{1,3},{3,1},{4,6},{6,4},{5,7},{7,5},{8,10},{10,8},{9,1... | collective-permute-start | bytes 1376264 | tf_op jit(solution)/shard_map/ppermute | solution.py:25
  137.4 2.2 %collective-permute-start.20 = (bf16[64,4096]{1,0:T(8,128)(2,1)S(1)}, bf16[64,4096]{1,0:T(8,128)(2,1)S(1)}, u32[]{:S(2)}, u32[]{:S(2)}) collective-permute-start(bf16[64,4096]{1,0:T(8,128)(2,1)S(1)} %shard_map.107), channel_id=1, source_target_pairs={{0,224},{32,0},{64,32},{96,64},{128,96},{160,128},{192,160},{224,1... | collective-permute-start | bytes 1572872 | tf_op jit(solution)/shard_map/ppermute | solution.py:25
  140.9 4.7 %collective-permute-done.19.came_ref = bf16[64,4096]{1,0:T(8,128)(2,1)S(1)} collective-permute-done((bf16[64,4096]{1,0:T(8,128)(2,1)S(1)}, bf16[64,4096]{1,0:T(8,128)(2,1)S(1)}, u32[]{:S(2)}, u32[]{:S(2)}) %collective-permute-start.19) | collective-permute-done | bytes 524320 | tf_op jit(solution)/shard_map/ppermute | solution.py:25
  145.6 5.4 %collective-permute-done.20.came_ref = bf16[64,4096]{1,0:T(8,128)(2,1)S(1)} collective-permute-done((bf16[64,4096]{1,0:T(8,128)(2,1)S(1)}, bf16[64,4096]{1,0:T(8,128)(2,1)S(1)}, u32[]{:S(2)}, u32[]{:S(2)}) %collective-permute-start.20) | collective-permute-done | bytes 524320 | tf_op jit(solution)/shard_map/ppermute | solution.py:25
  151.2 3.4 %collective-permute-start.22 = (bf16[64,4096]{1,0:T(8,128)(2,1)S(1)}, bf16[64,4096]{1,0:T(8,128)(2,1)S(1)}, u32[]{:S(2)}, u32[]{:S(2)}) collective-permute-start(bf16[64,4096]{1,0:T(8,128)(2,1)S(1)} %shard_map.109), channel_id=1, source_target_pairs={{0,224},{32,0},{64,32},{96,64},{128,96},{160,128},{192,160},{224,1... | collective-permute-start | bytes 1572872 | tf_op jit(solution)/shard_map/ppermute | solution.py:25
  157.1 8.0 %collective-permute-done.22.came_down_ref = bf16[64,4096]{1,0:T(8,128)(2,1)S(1)} collective-permute-done((bf16[64,4096]{1,0:T(8,128)(2,1)S(1)}, bf16[64,4096]{1,0:T(8,128)(2,1)S(1)}, u32[]{:S(2)}, u32[]{:S(2)}) %collective-permute-start.22) | collective-permute-done | bytes 524320 | tf_op jit(solution)/shard_map/ppermute | solution.py:25
  165.1 3.1 %collective-permute-done.21.came_up_ref = bf16[64,4096]{1,0:T(8,128)(2,1)S(1)} collective-permute-done((bf16[64,4096]{1,0:T(8,128)(2,1)S(1)}, bf16[64,4096]{1,0:T(8,128)(2,1)S(1)}, u32[]{:S(2)}, u32[]{:S(2)}) %collective-permute-start.21) | collective-permute-done | bytes 524320 | tf_op jit(solution)/shard_map/ppermute | solution.py:25
  169.6 6.2 %all-to-all-start.1 = ((bf16[32,2,4096]{2,1,0:T(2,128)(2,1)}), bf16[32,2,4096]{2,1,0:T(2,128)(2,1)S(1)}, u32[]{:S(2)}, u32[]{:S(2)}) async-start(bf16[32,2,4096]{2,1,0:T(2,128)(2,1)} %shard_map.110), calls=%async_computation.1 | async-start | bytes 1048576 | tf_op jit(solution)/shard_map/all_to_all | solution.py:29
  177.2 10.0 %all-to-all-done.1.blocks_ref = bf16[32,2,4096]{2,1,0:T(2,128)(2,1)S(1)} async-done(((bf16[32,2,4096]{2,1,0:T(2,128)(2,1)}), bf16[32,2,4096]{2,1,0:T(2,128)(2,1)S(1)}, u32[]{:S(2)}, u32[]{:S(2)}) %all-to-all-start.1) | async-done | bytes 524320 | tf_op jit(solution)/shard_map/all_to_all | solution.py:29
  (97 shorter events, 32.4 us)
Async XLA Ops:
  5.5 8.7 %collective-permute-start = (bf16[336,2048]{1,0:T(8,128)(2,1)}, bf16[336,2048]{1,0:T(8,128)(2,1)S(1)}, u32[]{:S(2)}, u32[]{:S(2)}) collective-permute-start(bf16[336,2048]{1,0:T(8,128)(2,1)} %shard_map.93), channel_id=1, source_target_pairs={{0,2},{2,0},{1,3},{3,1},{4,6},{6,4},{5,7},{7,5},{8,10},{10,8},{9,1... | collective-permute-start | bytes 4128776 | tf_op jit(solution)/shard_map/ppermute | solution.py:25
  8.7 16.9 %all-to-all-start = ((bf16[32,2,4096]{2,1,0:T(2,128)(2,1)}), bf16[32,2,4096]{2,1,0:T(2,128)(2,1)S(1)}, u32[]{:S(2)}, u32[]{:S(2)}) async-start(bf16[32,2,4096]{2,1,0:T(2,128)(2,1)} %shard_map.92), calls=%async_computation | async-start | bytes 1048576 | tf_op jit(solution)/shard_map/all_to_all | solution.py:29
  18.8 42.1 %copy-start.2 = (bf16[448,2048]{1,0:T(8,128)(2,1)S(1)}, bf16[448,2048]{1,0:T(8,128)(2,1)}, u32[]{:S(2)}) copy-start(bf16[448,2048]{1,0:T(8,128)(2,1)} %get-tuple-element.60.in_ref) | copy-start | bytes 5505028
  18.8 42.1 %copy-start.5 = (bf16[224,2048]{1,0:T(8,128)(2,1)S(1)}, bf16[224,2048]{1,0:T(8,128)(2,1)}, u32[]{:S(2)}) copy-start(bf16[224,2048]{1,0:T(8,128)(2,1)} %get-tuple-element.61.out_ref) | copy-start | bytes 2752516
  26.0 17.9 %collective-permute-start.4 = (bf16[64,4096]{1,0:T(8,128)(2,1)S(1)}, bf16[64,4096]{1,0:T(8,128)(2,1)S(1)}, u32[]{:S(2)}, u32[]{:S(2)}) collective-permute-start(bf16[64,4096]{1,0:T(8,128)(2,1)S(1)} %shard_map.95.refs_2_), channel_id=1, source_target_pairs={{0,32},{32,64},{64,96},{96,128},{128,160},{160,192},{192,224},{224... | collective-permute-start | bytes 1572872 | tf_op jit(solution)/shard_map/ppermute | solution.py:25
  27.7 16.2 %collective-permute-start.1 = (bf16[64,4096]{1,0:T(8,128)(2,1)S(1)}, bf16[64,4096]{1,0:T(8,128)(2,1)S(1)}, u32[]{:S(2)}, u32[]{:S(2)}) collective-permute-start(bf16[64,4096]{1,0:T(8,128)(2,1)S(1)} %shard_map.95.refs_2_), channel_id=1, source_target_pairs={{0,224},{32,0},{64,32},{96,64},{128,96},{160,128},{192,160},{224,1... | collective-permute-start | bytes 1572872 | tf_op jit(solution)/shard_map/ppermute | solution.py:25
  43.9 14.1 %collective-permute-start.5 = (bf16[64,4096]{1,0:T(8,128)(2,1)S(1)}, bf16[64,4096]{1,0:T(8,128)(2,1)S(1)}, u32[]{:S(2)}, u32[]{:S(2)}) collective-permute-start(bf16[64,4096]{1,0:T(8,128)(2,1)S(1)} %collective-permute-done.4.refs_1_), channel_id=1, source_target_pairs={{0,32},{32,64},{64,96},{96,128},{128,160},{160,192},{192,224},{224... | collective-permute-start | bytes 1572872 | tf_op jit(solution)/shard_map/ppermute | solution.py:25
  43.9 14.1 %collective-permute-start.2 = (bf16[64,4096]{1,0:T(8,128)(2,1)S(1)}, bf16[64,4096]{1,0:T(8,128)(2,1)S(1)}, u32[]{:S(2)}, u32[]{:S(2)}) collective-permute-start(bf16[64,4096]{1,0:T(8,128)(2,1)S(1)} %collective-permute-done.1.refs_3_), channel_id=1, source_target_pairs={{0,224},{32,0},{64,32},{96,64},{128,96},{160,128},{192,160},{224,1... | collective-permute-start | bytes 1572872 | tf_op jit(solution)/shard_map/ppermute | solution.py:25
  58.0 13.2 %collective-permute-start.6 = (bf16[64,4096]{1,0:T(8,128)(2,1)S(1)}, bf16[64,4096]{1,0:T(8,128)(2,1)S(1)}, u32[]{:S(2)}, u32[]{:S(2)}) collective-permute-start(bf16[64,4096]{1,0:T(8,128)(2,1)S(1)} %collective-permute-done.5.refs_0_), channel_id=1, source_target_pairs={{0,32},{32,64},{64,96},{96,128},{128,160},{160,192},{192,224},{224... | collective-permute-start | bytes 1572872 | tf_op jit(solution)/shard_map/ppermute | solution.py:25
  58.0 13.2 %collective-permute-start.3 = (bf16[64,4096]{1,0:T(8,128)(2,1)S(1)}, bf16[64,4096]{1,0:T(8,128)(2,1)S(1)}, u32[]{:S(2)}, u32[]{:S(2)}) collective-permute-start(bf16[64,4096]{1,0:T(8,128)(2,1)S(1)} %collective-permute-done.2.refs_0_), channel_id=1, source_target_pairs={{0,224},{32,0},{64,32},{96,64},{128,96},{160,128},{192,160},{224,1... | collective-permute-start | bytes 1572872 | tf_op jit(solution)/shard_map/ppermute | solution.py:25
  71.2 5.3 %collective-permute-start.9 = (f32[336,256]{1,0:T(8,128)S(1)}, f32[336,256]{1,0:T(8,128)S(1)}, u32[]{:S(2)}, u32[]{:S(2)}) collective-permute-start(f32[336,256]{1,0:T(8,128)S(1)} %get-tuple-element.67), channel_id=1, source_target_pairs={{0,2},{2,0},{1,3},{3,1},{4,6},{6,4},{5,7},{7,5},{8,10},{10,8},{9,1... | collective-permute-start | bytes 1032200 | tf_op jit(solution)/shard_map/ppermute | solution.py:25
  73.6 9.2 %collective-permute-start.8 = (bf16[64,2048]{1,0:T(8,128)(2,1)S(1)}, bf16[64,2048]{1,0:T(8,128)(2,1)S(1)}, u32[]{:S(2)}, u32[]{:S(2)}) collective-permute-start(bf16[64,2048]{1,0:T(8,128)(2,1)S(1)} %slice.51), channel_id=1, source_target_pairs={{0,32},{32,64},{64,96},{96,128},{128,160},{160,192},{192,224},{224... | collective-permute-start | bytes 786440 | tf_op jit(solution)/shard_map/ppermute | solution.py:25
  73.7 9.1 %collective-permute-start.7 = (bf16[64,2048]{1,0:T(8,128)(2,1)S(1)}, bf16[64,2048]{1,0:T(8,128)(2,1)S(1)}, u32[]{:S(2)}, u32[]{:S(2)}) collective-permute-start(bf16[64,2048]{1,0:T(8,128)(2,1)S(1)} %slice.50), channel_id=1, source_target_pairs={{0,224},{32,0},{64,32},{96,64},{128,96},{160,128},{192,160},{224,1... | collective-permute-start | bytes 786440 | tf_op jit(solution)/shard_map/ppermute | solution.py:25
  84.4 2.1 %collective-permute-start.10 = (f32[336,256]{1,0:T(8,128)S(1)}, f32[336,256]{1,0:T(8,128)S(1)}, u32[]{:S(2)}, u32[]{:S(2)}) collective-permute-start(f32[336,256]{1,0:T(8,128)S(1)} %get-tuple-element.73), channel_id=1, source_target_pairs={{0,2},{2,0},{1,3},{3,1},{4,6},{6,4},{5,7},{7,5},{8,10},{10,8},{9,1... | collective-permute-start | bytes 1032200 | tf_op jit(solution)/shard_map/ppermute | solution.py:25
  86.6 10.9 %collective-permute-start.11 = (f32[336,256]{1,0:T(8,128)S(1)}, f32[336,256]{1,0:T(8,128)S(1)}, u32[]{:S(2)}, u32[]{:S(2)}) collective-permute-start(f32[336,256]{1,0:T(8,128)S(1)} %add.27.sum_ref), channel_id=1, source_target_pairs={{0,1},{1,0},{2,3},{3,2},{4,5},{5,4},{6,7},{7,6},{8,9},{9,8},{10,11... | collective-permute-start | bytes 1032200 | tf_op jit(solution)/shard_map/ppermute | solution.py:25
  97.6 2.5 %collective-permute-start.12 = (bf16[336,256]{1,0:T(8,128)(2,1)S(1)}, bf16[336,256]{1,0:T(8,128)(2,1)S(1)}, u32[]{:S(2)}, u32[]{:S(2)}) collective-permute-start(bf16[336,256]{1,0:T(8,128)(2,1)S(1)} %shard_map.100.own_ref), channel_id=1, source_target_pairs={{0,2},{2,0},{1,3},{3,1},{4,6},{6,4},{5,7},{7,5},{8,10},{10,8},{9,1... | collective-permute-start | bytes 516104 | tf_op jit(solution)/shard_map/ppermute | solution.py:25
  99.1 11.1 %collective-permute-start.15 = (f32[336,256]{1,0:T(8,128)S(1)}, f32[336,256]{1,0:T(8,128)S(1)}, u32[]{:S(2)}, u32[]{:S(2)}) collective-permute-start(f32[336,256]{1,0:T(8,128)S(1)} %add.26.sum_ref), channel_id=1, source_target_pairs={{0,1},{1,0},{2,3},{3,2},{4,5},{5,4},{6,7},{7,6},{8,9},{9,8},{10,11... | collective-permute-start | bytes 1032200 | tf_op jit(solution)/shard_map/ppermute | solution.py:25
  101.3 12.0 %collective-permute-start.13 = (bf16[64,2048]{1,0:T(8,128)(2,1)}, bf16[64,2048]{1,0:T(8,128)(2,1)}, u32[]{:S(2)}, u32[]{:S(2)}) collective-permute-start(bf16[64,2048]{1,0:T(8,128)(2,1)} %slice.99), channel_id=1, source_target_pairs={{0,32},{32,64},{64,96},{96,128},{128,160},{160,192},{192,224},{224... | collective-permute-start | bytes 786440 | tf_op jit(solution)/shard_map/ppermute | solution.py:25
  105.9 7.5 %collective-permute-start.14 = (bf16[64,2048]{1,0:T(8,128)(2,1)}, bf16[64,2048]{1,0:T(8,128)(2,1)}, u32[]{:S(2)}, u32[]{:S(2)}) collective-permute-start(bf16[64,2048]{1,0:T(8,128)(2,1)} %slice.98), channel_id=1, source_target_pairs={{0,224},{32,0},{64,32},{96,64},{128,96},{160,128},{192,160},{224,1... | collective-permute-start | bytes 786440 | tf_op jit(solution)/shard_map/ppermute | solution.py:25
  110.3 2.1 %collective-permute-start.16 = (bf16[336,256]{1,0:T(8,128)(2,1)S(1)}, bf16[336,256]{1,0:T(8,128)(2,1)}, u32[]{:S(2)}, u32[]{:S(2)}) collective-permute-start(bf16[336,256]{1,0:T(8,128)(2,1)S(1)} %shard_map.102.own_ref), channel_id=1, source_target_pairs={{0,2},{2,0},{1,3},{3,1},{4,6},{6,4},{5,7},{7,5},{8,10},{10,8},{9,1... | collective-permute-start | bytes 516104 | tf_op jit(solution)/shard_map/ppermute | solution.py:25
  117.0 3.5 %copy-start.4 = (bf16[448,2048]{1,0:T(8,128)(2,1)S(1)}, bf16[448,2048]{1,0:T(8,128)(2,1)}, u32[]{:S(2)}) copy-start(bf16[448,2048]{1,0:T(8,128)(2,1)} %get-tuple-element.60.in_ref) | copy-start | bytes 5505028
  117.1 13.0 %collective-permute-start.18 = (bf16[64,4096]{1,0:T(8,128)(2,1)S(1)}, bf16[64,4096]{1,0:T(8,128)(2,1)S(1)}, u32[]{:S(2)}, u32[]{:S(2)}) collective-permute-start(bf16[64,4096]{1,0:T(8,128)(2,1)S(1)} %shard_map.105), channel_id=1, source_target_pairs={{0,224},{32,0},{64,32},{96,64},{128,96},{160,128},{192,160},{224,1... | collective-permute-start | bytes 1572872 | tf_op jit(solution)/shard_map/ppermute | solution.py:25
  120.1 13.2 %collective-permute-start.17 = (bf16[64,4096]{1,0:T(8,128)(2,1)S(1)}, bf16[64,4096]{1,0:T(8,128)(2,1)S(1)}, u32[]{:S(2)}, u32[]{:S(2)}) collective-permute-start(bf16[64,4096]{1,0:T(8,128)(2,1)S(1)} %shard_map.104), channel_id=1, source_target_pairs={{0,32},{32,64},{64,96},{96,128},{128,160},{160,192},{192,224},{224... | collective-permute-start | bytes 1572872 | tf_op jit(solution)/shard_map/ppermute | solution.py:25
  121.3 12.1 %copy-start.9 = (bf16[256,2048]{1,0:T(8,128)(2,1)S(1)}, bf16[256,2048]{1,0:T(8,128)(2,1)}, u32[]{:S(2)}) copy-start(bf16[256,2048]{1,0:T(8,128)(2,1)} %copy-done.8) | copy-start | bytes 3145732
  133.3 12.3 %collective-permute-start.19 = (bf16[64,4096]{1,0:T(8,128)(2,1)S(1)}, bf16[64,4096]{1,0:T(8,128)(2,1)S(1)}, u32[]{:S(2)}, u32[]{:S(2)}) collective-permute-start(bf16[64,4096]{1,0:T(8,128)(2,1)S(1)} %shard_map.106), channel_id=1, source_target_pairs={{0,32},{32,64},{64,96},{96,128},{128,160},{160,192},{192,224},{224... | collective-permute-start | bytes 1572872 | tf_op jit(solution)/shard_map/ppermute | solution.py:25
  134.8 4.8 %copy-start.7 = (bf16[256,2048]{1,0:T(8,128)(2,1)S(1)}, bf16[256,2048]{1,0:T(8,128)(2,1)}, u32[]{:S(2)}) copy-start(bf16[256,2048]{1,0:T(8,128)(2,1)} %copy-done.6) | copy-start | bytes 3145732
  134.9 21.0 %collective-permute-start.24 = (bf16[112,2048]{1,0:T(8,128)(2,1)S(1)}, bf16[112,2048]{1,0:T(8,128)(2,1)S(1)}, u32[]{:S(2)}, u32[]{:S(2)}) collective-permute-start(bf16[112,2048]{1,0:T(8,128)(2,1)S(1)} %fusion.3), channel_id=1, source_target_pairs={{0,2},{2,0},{1,3},{3,1},{4,6},{6,4},{5,7},{7,5},{8,10},{10,8},{9,1... | collective-permute-start | bytes 1376264 | tf_op jit(solution)/shard_map/ppermute | solution.py:25
  137.4 13.6 %collective-permute-start.20 = (bf16[64,4096]{1,0:T(8,128)(2,1)S(1)}, bf16[64,4096]{1,0:T(8,128)(2,1)S(1)}, u32[]{:S(2)}, u32[]{:S(2)}) collective-permute-start(bf16[64,4096]{1,0:T(8,128)(2,1)S(1)} %shard_map.107), channel_id=1, source_target_pairs={{0,224},{32,0},{64,32},{96,64},{128,96},{160,128},{192,160},{224,1... | collective-permute-start | bytes 1572872 | tf_op jit(solution)/shard_map/ppermute | solution.py:25
  140.5 35.3 %collective-permute-start.23 = (bf16[224,2048]{1,0:T(8,128)(2,1)S(1)}, bf16[224,2048]{1,0:T(8,128)(2,1)S(1)}, u32[]{:S(2)}, u32[]{:S(2)}) collective-permute-start(bf16[224,2048]{1,0:T(8,128)(2,1)S(1)} %fusion.1), channel_id=1, source_target_pairs={{0,2},{2,0},{1,3},{3,1},{4,6},{6,4},{5,7},{7,5},{8,10},{10,8},{9,1... | collective-permute-start | bytes 2752520 | tf_op jit(solution)/shard_map/ppermute | solution.py:25
  151.2 13.9 %collective-permute-start.22 = (bf16[64,4096]{1,0:T(8,128)(2,1)S(1)}, bf16[64,4096]{1,0:T(8,128)(2,1)S(1)}, u32[]{:S(2)}, u32[]{:S(2)}) collective-permute-start(bf16[64,4096]{1,0:T(8,128)(2,1)S(1)} %shard_map.109), channel_id=1, source_target_pairs={{0,224},{32,0},{64,32},{96,64},{128,96},{160,128},{192,160},{224,1... | collective-permute-start | bytes 1572872 | tf_op jit(solution)/shard_map/ppermute | solution.py:25
  154.7 13.5 %collective-permute-start.21 = (bf16[64,4096]{1,0:T(8,128)(2,1)S(1)}, bf16[64,4096]{1,0:T(8,128)(2,1)S(1)}, u32[]{:S(2)}, u32[]{:S(2)}) collective-permute-start(bf16[64,4096]{1,0:T(8,128)(2,1)S(1)} %shard_map.108), channel_id=1, source_target_pairs={{0,32},{32,64},{64,96},{96,128},{128,160},{160,192},{192,224},{224... | collective-permute-start | bytes 1572872 | tf_op jit(solution)/shard_map/ppermute | solution.py:25
  169.6 17.6 %all-to-all-start.1 = ((bf16[32,2,4096]{2,1,0:T(2,128)(2,1)}), bf16[32,2,4096]{2,1,0:T(2,128)(2,1)S(1)}, u32[]{:S(2)}, u32[]{:S(2)}) async-start(bf16[32,2,4096]{2,1,0:T(2,128)(2,1)} %shard_map.110), calls=%async_computation.1 | async-start | bytes 1048576 | tf_op jit(solution)/shard_map/all_to_all | solution.py:29
  (12 other events, 18.1 us)

commit v4 on v3

--- a/solution.py
+++ b/solution.py
@@ -155,23 +155,15 @@
     hidden_ref[double // 2 :, :] = got_ref[double:, :]
 
 
-def turn_kernel(_, left_ref, right_ref, came_ref, out_ref, *, whole, up):
-    width = left_ref.shape[1]
-    left, right = left_ref[...], right_ref[...]
-    if whole or up:
-        left = left + came_ref[:, :width].astype(F32)
-    if whole or not up:
-        right = right + came_ref[:, came_ref.shape[1] - width :].astype(F32)
-    out_ref[:, :width] = left.astype(BF16)
-    out_ref[:, width:] = right.astype(BF16)
-
-
-def close_kernel(_, left_ref, right_ref, came_up_ref, came_down_ref, out_ref, rows_ref):
+def turn_kernel(_, term_ref, came_ref, out_ref):
+    out_ref[...] = (term_ref[...] + came_ref[...].astype(F32)).astype(BF16)
+
+
+def close_kernel(_, a0_ref, b0_ref, a1_ref, a2_ref, b1_ref, b2_ref, out_ref, rows_ref):
     n, pair, _ = out_ref.shape
-    width = left_ref.shape[1]
-    came = came_up_ref[...].astype(F32) + came_down_ref[...].astype(F32)
-    rows_ref[:, :width] = left_ref[...] + came[:, :width]
-    rows_ref[:, width:] = right_ref[...] + came[:, width:]
+    width = a0_ref.shape[1]
+    rows_ref[:, :width] = a0_ref[...] + a1_ref[...].astype(F32) + a2_ref[...].astype(F32)
+    rows_ref[:, width:] = b0_ref[...] + b1_ref[...].astype(F32) + b2_ref[...].astype(F32)
     for j in range(n):
         out_ref[j] = rows_ref[j * pair : (j + 1) * pair, :].astype(BF16)
 
@@ -191,29 +183,42 @@
     count = lax.axis_size("z")
     half = count // 2
 
-    def added(kernel, out_shape, k, *came, scratch=(), **kwargs):
+    def at(k):
         found, j = terms[k % count]
         place = ((height, found[0].shape[1]), lambda *_: (j, 0))
-        places = [place, place] + [None] * len(came)
-        return called_at(kernel, out_shape, places, *found, *came, scratch=scratch, **kwargs)
-
-    found, j = terms[half]
-    width = found[0].shape[1]
-    up, down = (f[j * height : (j + 1) * height].astype(BF16) for f in found)
-    both = shape_of((height, 2 * width))
+        return found, place
+
+    def own_term(ring, k):
+        found, j = terms[k % count]
+        return found[ring][j * height : (j + 1) * height].astype(BF16)
+
+    def turned(ring, k, came):
+        if came is None:
+            return own_term(ring, k)
+        found, place = at(k)
+        out = shape_of((height, found[ring].shape[1]))
+        return called_at(turn_kernel, out, [place, None], found[ring], came)
+
+    def sent(block, distance):
+        return None if block is None else shifted(block, "z", distance)
+
+    width = terms[half][0][0].shape[1]
+    rings = [[own_term(0, half), None], [None, own_term(1, half)]]
     for k in range(half - 1, 0, -1):
-        up, down = shifted(up, "z", 1), shifted(down, "z", -1)
+        for j, (up, down) in enumerate(rings):
+            rings[j] = [sent(up, 1), sent(down, -1)]
         if k in later:
-            up, down = later[k](up, down)
-        up = added(turn_kernel, both, k, up, whole=k < half - 1, up=True)
-        down = added(turn_kernel, both, -k, down, whole=k < half - 1, up=False)
-    up, down = shifted(up, "z", 1), shifted(down, "z", -1)
-    return added(
+            rings[0][0], rings[0][1] = later[k](*rings[0])
+        for j, (up, down) in enumerate(rings):
+            rings[j] = [turned(j, k, up), turned(j, -k, down)]
+    came = [c for up, down in rings for c in (shifted(up, "z", 1), shifted(down, "z", -1))]
+    found, place = at(0)
+    return called_at(
         close_kernel,
         shape_of((height // pair, pair, 2 * width)),
-        0,
-        up,
-        down,
+        [place, place] + [None] * len(came),
+        *found,
+        *came,
         scratch=[pltpu.VMEM((height, 2 * width), F32)],
     )
 
@@ -294,12 +299,11 @@
         ring[k], ring[-k] = shifted(ring[k - 1], "z", -1), shifted(ring[1 - k], "z", 1)
     near_rows, near_grads = stacked(*(ring[k] for k in range(-half // 2, half // 2)))
     own, other = partial_sums(near_rows, near_grads)
-    ahead, behind, own, other = lax.optimization_barrier((ring[half - 1], ring[1 - half], own, other))
+    near_sums = own + shifted(other, "core", 1)
+    ahead, behind, near_sums = lax.optimization_barrier((ring[half - 1], ring[1 - half], near_sums))
     left, right = shifted(ahead[:, :part], "z", -1), shifted(behind[:, part:], "z", 1)
-    left, right, near_sums = lax.optimization_barrier(
-        (left, right, own + shifted(other, "core", 1))
-    )
     near_got = shifted(near_sums, "tok", 1)
+    left, right, near_got = lax.optimization_barrier((left, right, near_got))
     far_rows, far_grads = stacked(
         *(ring[k] for k in range(half // 2, half)),
         *(ring[k] for k in range(1 - half, -half // 2)),
@@ -308,8 +312,10 @@
     )
     own, other = partial_sums(far_rows, far_grads)
     far_sums = own + shifted(other, "core", 1)
-    far_in, far_hidden = factors(far_sums, shifted(far_sums, "tok", 1))
+    far_got = shifted(far_sums, "tok", 1)
     near_in, near_hidden = factors(near_sums, near_got)
+    far_got, near_in, near_hidden = lax.optimization_barrier((far_got, near_in, near_hidden))
+    far_in, far_hidden = factors(far_sums, far_got)
 
     terms = {}
 
@@ -344,23 +350,25 @@
         grads_out.extend([shifted(in_other, "core", 1), shifted(out_other, "core", 1)])
         return up, down
 
-    def own_grads(up, down):
-        up, down, a, b, c, d = lax.optimization_barrier(
-            (up, down, near_in, far_in, near_hidden, far_hidden)
+    later = {half - 1: near_terms, half - 2: others_grads}
+    summed, a, b, c, d = lax.optimization_barrier(
+        (
+            ring_reduced(terms, later, n_rows, pair),
+            near_in,
+            far_in,
+            near_hidden,
+            far_hidden,
         )
-        grads_out.append(weight_product(a[: 2 * units], b[: 2 * units], near_rows, far_rows))
-        grads_out.append(weight_product(c[:units], d[:units], near_grads, far_grads))
-        return up, down
-
-    later = {half - 1: near_terms, half - 2: others_grads, half - 3: own_grads}
-    summed = ring_reduced(terms, later, n_rows, pair)
+    )
+    in_weight_grad = weight_product(a[: 2 * units], b[: 2 * units], near_rows, far_rows)
+    out_weight_grad = weight_product(c[:units], d[:units], near_grads, far_grads)
     mixed, input_grad = called(
         total_kernel,
         (shape_of((pair, width)), shape_of((pair, width))),
         exchanged(summed, (*PLANE, *PAIRS)),
         quarters=quarters,
     )
-    got_in, got_out, in_weight_grad, out_weight_grad = grads_out
+    got_in, got_out = grads_out
 
     def side_by_side(mine, others):
         left = jnp.where(core == 0, mine, others)

time: 189 us -> 174 us (0.921)
  waiting for transfers between devices: 104 us -> 70.4 us
  starting transfers between devices: 51.3 us -> 63.6 us
  matrix products: 5.24 us -> 10.6 us
    ppermute x25 -> x31, waiting for transfers between devices: 87.3 us -> 59.4 us  [shifted(): lax.ppermute(block, axis, [(i, (i + distance) % count) for i in range(cou...]
    ppermute x25 -> x31, starting transfers between devices: 39.7 us -> 52.9 us  [shifted(): lax.ppermute(block, axis, [(i, (i + distance) % count) for i in range(cou...]
    all_to_all x2, waiting for transfers between devices: 16.9 us -> 11 us  [exchanged(): return lax.all_to_all(blocks, axes, 0, 0, tiled=True)]
    dot_general x4, matrix products: 1.44 us -> 4.16 us  [weight_product(): total = total + jnp.dot(far, far_right, preferred_element_type=F32)]
    dot_general x4, matrix products: 2.37 us -> 5.04 us  [by_columns(): lax.dot_general(left, right, (((0,), (0,)), ((), ())), preferred_element_...]
    pallas_call x9 -> x13, Pallas kernels: 9.66 us -> 8.93 us  [called_at(): pl.pallas_call(functools.partial(kernel, **kwargs), out_shape=out_shape,...]
    unnamed x34 -> x48, local copies, waits for them, and re-layouts: 6.41 us -> 6.44 us
  transfers between devices with their start and end apart: 27 -> 33, of which waited for: 17 -> 19; matrix products, arithmetic and copies ran while one was open for 5% -> 8% of each run, Pallas kernels for 4% -> 5%
where the time goes in v4:
time: 174 us; the launch traced here: 173 us
  waiting for transfers between devices  70.4 us (40%)
  starting transfers between devices  63.6 us (37%)
  Pallas kernels  15.1 us (9%)
  matrix products  10.6 us (6%)
  local copies, waits for them, and re-layouts  8.13 us (5%)
  other arithmetic  3.75 us (2%)
    ppermute x31, waiting for transfers between devices, shifted(): lax.ppermute(block, axis, [(i, (i + distance) % count) for i in range(cou...  59.4 us
    ppermute x31, starting transfers between devices, shifted(): lax.ppermute(block, axis, [(i, (i + distance) % count) for i in range(cou...  52.9 us
    all_to_all x2, waiting for transfers between devices, exchanged(): return lax.all_to_all(blocks, axes, 0, 0, tiled=True)  11 us
    all_to_all x2, starting transfers between devices, exchanged(): return lax.all_to_all(blocks, axes, 0, 0, tiled=True)  10.8 us
    pallas_call x13, Pallas kernels, called_at(): pl.pallas_call(functools.partial(kernel, **kwargs), out_shape=out_shape,...  8.93 us
    unnamed x48, local copies, waits for them, and re-layouts  6.44 us
    pallas_call x11, Pallas kernels, called(): pl.pallas_call(functools.partial(kernel, **kwargs), out_shape=out_shape,...  6.19 us
    dot_general x4, matrix products, by_columns(): lax.dot_general(left, right, (((0,), (0,)), ((), ())), preferred_element_...  5.04 us
  transfers between devices with their start and end apart: 33, of which 19 were waited for; matrix products, arithmetic and copies ran while one was open for 8% of the time, Pallas kernels for 5%

profile of v4, /device:TPU:1, one launch (start us, length us, event | category | flops | bytes accessed | tf_op | source)
XLA Modules:
  0.0 172.8 jit_solution(10514271830567498400)
XLA Ops:
  3.0 2.5 %shard_map.93 = bf16[336,2048]{1,0:T(8,128)(2,1)} custom-call(s32[1]{0:T(128)} %bitcast.1._, bf16[112,8192]{1,0:T(8,128)(2,1)} %gate_ref.1, bf16[112,8192]{1,0:T(8,128)(2,1)} %up_ref.1, bf16[112,8192]{1,0:T(8,128)(2,1)} %down_ref.1), custom_call_target="tpu_custom_call" | custom-call | tf_op jit(solution)/shard_map/pallas_call | solution.py:67
  5.5 3.2 %collective-permute-start = (bf16[336,2048]{1,0:T(8,128)(2,1)}, bf16[336,2048]{1,0:T(8,128)(2,1)S(1)}, u32[]{:S(2)}, u32[]{:S(2)}) collective-permute-start(bf16[336,2048]{1,0:T(8,128)(2,1)} %shard_map.93), channel_id=1, source_target_pairs={{0,2},{2,0},{1,3},{3,1},{4,6},{6,4},{5,7},{7,5},{8,10},{10,8},{9,1... | collective-permute-start | bytes 4128776 | tf_op jit(solution)/shard_map/ppermute | solution.py:25
  8.7 5.5 %all-to-all-start = ((bf16[32,2,4096]{2,1,0:T(2,128)(2,1)}), bf16[32,2,4096]{2,1,0:T(2,128)(2,1)S(1)}, u32[]{:S(2)}, u32[]{:S(2)}) async-start(bf16[32,2,4096]{2,1,0:T(2,128)(2,1)} %shard_map.92), calls=%async_computation | async-start | bytes 1048576 | tf_op jit(solution)/shard_map/all_to_all | solution.py:29
  15.3 3.4 %shard_map.94 = (bf16[448,2048]{1,0:T(8,128)(2,1)}, bf16[224,2048]{1,0:T(8,128)(2,1)}) custom-call(s32[1]{0:T(128)} %bitcast._, bf16[112,8192]{1,0:T(8,128)(2,1)} %gate_ref.1, bf16[112,8192]{1,0:T(8,128)(2,1)} %up_ref.1, bf16[112,8192]{1,0:T(8,128)(2,1)} %down_ref.1, bf16[336,2048]{1,0:T(8,128)(2,1)} %copy-done.23), custom_call_target="tpu_custom_call" | custom-call | tf_op jit(solution)/shard_map/pallas_call | solution.py:67
  18.7 6.9 %all-to-all-done.blocks_ref = bf16[32,2,4096]{2,1,0:T(2,128)(2,1)S(1)} async-done(((bf16[32,2,4096]{2,1,0:T(2,128)(2,1)}), bf16[32,2,4096]{2,1,0:T(2,128)(2,1)S(1)}, u32[]{:S(2)}, u32[]{:S(2)}) %all-to-all-start) | async-done | bytes 524320 | tf_op jit(solution)/shard_map/all_to_all | solution.py:29
  26.0 5.7 %collective-permute-start.1 = (bf16[64,4096]{1,0:T(8,128)(2,1)S(1)}, bf16[64,4096]{1,0:T(8,128)(2,1)S(1)}, u32[]{:S(2)}, u32[]{:S(2)}) collective-permute-start(bf16[64,4096]{1,0:T(8,128)(2,1)S(1)} %shard_map.95.refs_2_), channel_id=1, source_target_pairs={{0,224},{32,0},{64,32},{96,64},{128,96},{160,128},{192,160},{224,1... | collective-permute-start | bytes 1572872 | tf_op jit(solution)/shard_map/ppermute | solution.py:25
  31.6 11.3 %collective-permute-done.1.refs_3_ = bf16[64,4096]{1,0:T(8,128)(2,1)S(1)} collective-permute-done((bf16[64,4096]{1,0:T(8,128)(2,1)S(1)}, bf16[64,4096]{1,0:T(8,128)(2,1)S(1)}, u32[]{:S(2)}, u32[]{:S(2)}) %collective-permute-start.1) | collective-permute-done | bytes 524320 | tf_op jit(solution)/shard_map/ppermute | solution.py:25
  43.0 3.4 %collective-permute-start.2 = (bf16[64,4096]{1,0:T(8,128)(2,1)S(1)}, bf16[64,4096]{1,0:T(8,128)(2,1)S(1)}, u32[]{:S(2)}, u32[]{:S(2)}) collective-permute-start(bf16[64,4096]{1,0:T(8,128)(2,1)S(1)} %collective-permute-done.1.refs_3_), channel_id=1, source_target_pairs={{0,224},{32,0},{64,32},{96,64},{128,96},{160,128},{192,160},{224,1... | collective-permute-start | bytes 1572872 | tf_op jit(solution)/shard_map/ppermute | solution.py:25
  46.4 10.4 %collective-permute-done.2.refs_0_ = bf16[64,4096]{1,0:T(8,128)(2,1)S(1)} collective-permute-done((bf16[64,4096]{1,0:T(8,128)(2,1)S(1)}, bf16[64,4096]{1,0:T(8,128)(2,1)S(1)}, u32[]{:S(2)}, u32[]{:S(2)}) %collective-permute-start.2) | collective-permute-done | bytes 524320 | tf_op jit(solution)/shard_map/ppermute | solution.py:25
  56.8 3.4 %collective-permute-start.3 = (bf16[64,4096]{1,0:T(8,128)(2,1)S(1)}, bf16[64,4096]{1,0:T(8,128)(2,1)S(1)}, u32[]{:S(2)}, u32[]{:S(2)}) collective-permute-start(bf16[64,4096]{1,0:T(8,128)(2,1)S(1)} %collective-permute-done.2.refs_0_), channel_id=1, source_target_pairs={{0,224},{32,0},{64,32},{96,64},{128,96},{160,128},{192,160},{224,1... | collective-permute-start | bytes 1572872 | tf_op jit(solution)/shard_map/ppermute | solution.py:25
  61.9 2.1 %collective-permute-start.7 = (f32[336,256]{1,0:T(8,128)S(1)}, f32[336,256]{1,0:T(8,128)S(1)}, u32[]{:S(2)}, u32[]{:S(2)}) collective-permute-start(f32[336,256]{1,0:T(8,128)S(1)} %get-tuple-element.63), channel_id=1, source_target_pairs={{0,2},{2,0},{1,3},{3,1},{4,6},{6,4},{5,7},{7,5},{8,10},{10,8},{9,1... | collective-permute-start | bytes 1032200 | tf_op jit(solution)/shard_map/ppermute | solution.py:25
  65.2 4.5 %collective-permute-done.3.refs_1_ = bf16[64,4096]{1,0:T(8,128)(2,1)S(1)} collective-permute-done((bf16[64,4096]{1,0:T(8,128)(2,1)S(1)}, bf16[64,4096]{1,0:T(8,128)(2,1)S(1)}, u32[]{:S(2)}, u32[]{:S(2)}) %collective-permute-start.3) | collective-permute-done | bytes 524320 | tf_op jit(solution)/shard_map/ppermute | solution.py:25
  69.8 3.1 %collective-permute-done.6.refs_2_ = bf16[64,4096]{1,0:T(8,128)(2,1)S(1)} collective-permute-done((bf16[64,4096]{1,0:T(8,128)(2,1)S(1)}, bf16[64,4096]{1,0:T(8,128)(2,1)S(1)}, u32[]{:S(2)}, u32[]{:S(2)}) %collective-permute-start.6) | collective-permute-done | bytes 524320 | tf_op jit(solution)/shard_map/ppermute | solution.py:25
  75.3 3.7 %collective-permute-done.8.refs_3_ = bf16[64,2048]{1,0:T(8,128)(2,1)S(1)} collective-permute-done((bf16[64,2048]{1,0:T(8,128)(2,1)S(1)}, bf16[64,2048]{1,0:T(8,128)(2,1)S(1)}, u32[]{:S(2)}, u32[]{:S(2)}) %collective-permute-start.8) | collective-permute-done | bytes 262176 | tf_op jit(solution)/shard_map/ppermute | solution.py:25
  78.9 1.9 %collective-permute-done.9.refs_4_ = bf16[64,2048]{1,0:T(8,128)(2,1)S(1)} collective-permute-done((bf16[64,2048]{1,0:T(8,128)(2,1)S(1)}, bf16[64,2048]{1,0:T(8,128)(2,1)S(1)}, u32[]{:S(2)}, u32[]{:S(2)}) %collective-permute-start.9) | collective-permute-done | bytes 262176 | tf_op jit(solution)/shard_map/ppermute | solution.py:25
  82.7 4.1 %collective-permute-start.11 = (f32[336,256]{1,0:T(8,128)S(1)}, f32[336,256]{1,0:T(8,128)S(1)}, u32[]{:S(2)}, u32[]{:S(2)}) collective-permute-start(f32[336,256]{1,0:T(8,128)S(1)} %get-tuple-element.72), channel_id=1, source_target_pairs={{0,2},{2,0},{1,3},{3,1},{4,6},{6,4},{5,7},{7,5},{8,10},{10,8},{9,1... | collective-permute-start | bytes 1032200 | tf_op jit(solution)/shard_map/ppermute | solution.py:25
  88.0 2.3 %collective-permute-start.12 = (f32[336,256]{1,0:T(8,128)S(1)}, f32[336,256]{1,0:T(8,128)S(1)}, u32[]{:S(2)}, u32[]{:S(2)}) collective-permute-start(f32[336,256]{1,0:T(8,128)S(1)} %add.27.sum_ref), channel_id=1, source_target_pairs={{0,1},{1,0},{2,3},{3,2},{4,5},{5,4},{6,7},{7,6},{8,9},{9,8},{10,11... | collective-permute-start | bytes 1032200 | tf_op jit(solution)/shard_map/ppermute | solution.py:25
  92.3 6.8 %collective-permute-done.12.got_ref = f32[336,256]{1,0:T(8,128)S(1)} collective-permute-done((f32[336,256]{1,0:T(8,128)S(1)}, f32[336,256]{1,0:T(8,128)S(1)}, u32[]{:S(2)}, u32[]{:S(2)}) %collective-permute-start.12) | collective-permute-done | bytes 344096 | tf_op jit(solution)/shard_map/ppermute | solution.py:25
  104.4 2.1 %fusion.19 = (bf16[256,2048]{1,0:T(8,128)(2,1)S(1)}, f32[256,2048]{1,0:T(8,128)}) fusion(bf16[448,256]{1,0:T(8,128)(2,1)S(1)} %get-tuple-element.90, bf16[448,2048]{1,0:T(8,128)(2,1)S(1)} %copy-done), kind=kOutput, calls=%fused_computation.32 | convolution fusion | flops 470286336 | bytes 5210112 | tf_op jit(solution)/shard_map/dot_general | solution.py:37
  107.3 2.7 %collective-permute-start.17 = (bf16[64,2048]{1,0:T(8,128)(2,1)}, bf16[64,2048]{1,0:T(8,128)(2,1)S(1)}, u32[]{:S(2)}, u32[]{:S(2)}) collective-permute-start(bf16[64,2048]{1,0:T(8,128)(2,1)} %get-tuple-element.103), channel_id=1, source_target_pairs={{0,224},{32,0},{64,32},{96,64},{128,96},{160,128},{192,160},{224,1... | collective-permute-start | bytes 786440 | tf_op jit(solution)/shard_map/ppermute | solution.py:25
  111.2 2.0 %collective-permute-done.15.came_ref = bf16[64,2048]{1,0:T(8,128)(2,1)} collective-permute-done((bf16[64,2048]{1,0:T(8,128)(2,1)}, bf16[64,2048]{1,0:T(8,128)(2,1)}, u32[]{:S(2)}, u32[]{:S(2)}) %collective-permute-start.15) | collective-permute-done | bytes 262176 | tf_op jit(solution)/shard_map/ppermute | solution.py:25
  116.1 2.8 %collective-permute-done.22.came_ref = bf16[64,2048]{1,0:T(8,128)(2,1)} collective-permute-done((bf16[64,2048]{1,0:T(8,128)(2,1)}, bf16[64,2048]{1,0:T(8,128)(2,1)}, u32[]{:S(2)}, u32[]{:S(2)}) %collective-permute-start.22) | collective-permute-done | bytes 262176 | tf_op jit(solution)/shard_map/ppermute | solution.py:25
  120.8 3.3 %collective-permute-start.26 = (bf16[64,2048]{1,0:T(8,128)(2,1)S(1)}, bf16[64,2048]{1,0:T(8,128)(2,1)S(1)}, u32[]{:S(2)}, u32[]{:S(2)}) collective-permute-start(bf16[64,2048]{1,0:T(8,128)(2,1)S(1)} %shard_map.111), channel_id=1, source_target_pairs={{0,224},{32,0},{64,32},{96,64},{128,96},{160,128},{192,160},{224,1... | collective-permute-start | bytes 786440 | tf_op jit(solution)/shard_map/ppermute | solution.py:25
  124.8 2.7 %collective-permute-start.20 = (bf16[64,2048]{1,0:T(8,128)(2,1)S(1)}, bf16[64,2048]{1,0:T(8,128)(2,1)S(1)}, u32[]{:S(2)}, u32[]{:S(2)}) collective-permute-start(bf16[64,2048]{1,0:T(8,128)(2,1)S(1)} %shard_map.107), channel_id=1, source_target_pairs={{0,224},{32,0},{64,32},{96,64},{128,96},{160,128},{192,160},{224,1... | collective-permute-start | bytes 786440 | tf_op jit(solution)/shard_map/ppermute | solution.py:25
  127.5 2.0 %collective-permute-done.23.came_ref = bf16[64,2048]{1,0:T(8,128)(2,1)S(1)} collective-permute-done((bf16[64,2048]{1,0:T(8,128)(2,1)S(1)}, bf16[64,2048]{1,0:T(8,128)(2,1)S(1)}, u32[]{:S(2)}, u32[]{:S(2)}) %collective-permute-start.23) | collective-permute-done | bytes 262176 | tf_op jit(solution)/shard_map/ppermute | solution.py:25
  129.8 2.9 %collective-permute-start.27 = (bf16[64,2048]{1,0:T(8,128)(2,1)S(1)}, bf16[64,2048]{1,0:T(8,128)(2,1)S(1)}, u32[]{:S(2)}, u32[]{:S(2)}) collective-permute-start(bf16[64,2048]{1,0:T(8,128)(2,1)S(1)} %shard_map.112), channel_id=1, source_target_pairs={{0,224},{32,0},{64,32},{96,64},{128,96},{160,128},{192,160},{224,1... | collective-permute-start | bytes 786440 | tf_op jit(solution)/shard_map/ppermute | solution.py:25
  134.1 4.3 %collective-permute-start.30 = (bf16[112,2048]{1,0:T(8,128)(2,1)}, bf16[112,2048]{1,0:T(8,128)(2,1)}, u32[]{:S(2)}, u32[]{:S(2)}) collective-permute-start(bf16[112,2048]{1,0:T(8,128)(2,1)} %fusion.3), channel_id=1, source_target_pairs={{0,2},{2,0},{1,3},{3,1},{4,6},{6,4},{5,7},{7,5},{8,10},{10,8},{9,1... | collective-permute-start | bytes 1376264 | tf_op jit(solution)/shard_map/ppermute | solution.py:25
  139.1 2.7 %collective-permute-start.21 = (bf16[64,2048]{1,0:T(8,128)(2,1)S(1)}, bf16[64,2048]{1,0:T(8,128)(2,1)S(1)}, u32[]{:S(2)}, u32[]{:S(2)}) collective-permute-start(bf16[64,2048]{1,0:T(8,128)(2,1)S(1)} %shard_map.108), channel_id=1, source_target_pairs={{0,224},{32,0},{64,32},{96,64},{128,96},{160,128},{192,160},{224,1... | collective-permute-start | bytes 786440 | tf_op jit(solution)/shard_map/ppermute | solution.py:25
  144.1 2.8 %collective-permute-start.29 = (bf16[224,2048]{1,0:T(8,128)(2,1)}, bf16[224,2048]{1,0:T(8,128)(2,1)}, u32[]{:S(2)}, u32[]{:S(2)}) collective-permute-start(bf16[224,2048]{1,0:T(8,128)(2,1)} %fusion.1), channel_id=1, source_target_pairs={{0,2},{2,0},{1,3},{3,1},{4,6},{6,4},{5,7},{7,5},{8,10},{10,8},{9,1... | collective-permute-start | bytes 2752520 | tf_op jit(solution)/shard_map/ppermute | solution.py:25
  148.2 4.7 %collective-permute-done.28.b2_ref = bf16[64,2048]{1,0:T(8,128)(2,1)S(1)} collective-permute-done((bf16[64,2048]{1,0:T(8,128)(2,1)S(1)}, bf16[64,2048]{1,0:T(8,128)(2,1)S(1)}, u32[]{:S(2)}, u32[]{:S(2)}) %collective-permute-start.28) | collective-permute-done | bytes 262176 | tf_op jit(solution)/shard_map/ppermute | solution.py:25
  154.1 5.3 %all-to-all-start.1 = ((bf16[32,2,4096]{2,1,0:T(2,128)(2,1)}), bf16[32,2,4096]{2,1,0:T(2,128)(2,1)}, u32[]{:S(2)}, u32[]{:S(2)}) async-start(bf16[32,2,4096]{2,1,0:T(2,128)(2,1)} %copy-done.14), calls=%async_computation.1 | async-start | bytes 1048576 | tf_op jit(solution)/shard_map/all_to_all | solution.py:29
  167.0 4.0 %all-to-all-done.1.blocks_ref = bf16[32,2,4096]{2,1,0:T(2,128)(2,1)} async-done(((bf16[32,2,4096]{2,1,0:T(2,128)(2,1)}), bf16[32,2,4096]{2,1,0:T(2,128)(2,1)}, u32[]{:S(2)}, u32[]{:S(2)}) %all-to-all-start.1) | async-done | bytes 524320 | tf_op jit(solution)/shard_map/all_to_all | solution.py:29
  (127 shorter events, 42.9 us)
Async XLA Ops:
  5.5 8.7 %collective-permute-start = (bf16[336,2048]{1,0:T(8,128)(2,1)}, bf16[336,2048]{1,0:T(8,128)(2,1)S(1)}, u32[]{:S(2)}, u32[]{:S(2)}) collective-permute-start(bf16[336,2048]{1,0:T(8,128)(2,1)} %shard_map.93), channel_id=1, source_target_pairs={{0,2},{2,0},{1,3},{3,1},{4,6},{6,4},{5,7},{7,5},{8,10},{10,8},{9,1... | collective-permute-start | bytes 4128776 | tf_op jit(solution)/shard_map/ppermute | solution.py:25
  8.7 16.9 %all-to-all-start = ((bf16[32,2,4096]{2,1,0:T(2,128)(2,1)}), bf16[32,2,4096]{2,1,0:T(2,128)(2,1)S(1)}, u32[]{:S(2)}, u32[]{:S(2)}) async-start(bf16[32,2,4096]{2,1,0:T(2,128)(2,1)} %shard_map.92), calls=%async_computation | async-start | bytes 1048576 | tf_op jit(solution)/shard_map/all_to_all | solution.py:29
  26.0 17.0 %collective-permute-start.1 = (bf16[64,4096]{1,0:T(8,128)(2,1)S(1)}, bf16[64,4096]{1,0:T(8,128)(2,1)S(1)}, u32[]{:S(2)}, u32[]{:S(2)}) collective-permute-start(bf16[64,4096]{1,0:T(8,128)(2,1)S(1)} %shard_map.95.refs_2_), channel_id=1, source_target_pairs={{0,224},{32,0},{64,32},{96,64},{128,96},{160,128},{192,160},{224,1... | collective-permute-start | bytes 1572872 | tf_op jit(solution)/shard_map/ppermute | solution.py:25
  31.6 14.8 %collective-permute-start.4 = (bf16[64,4096]{1,0:T(8,128)(2,1)S(1)}, bf16[64,4096]{1,0:T(8,128)(2,1)S(1)}, u32[]{:S(2)}, u32[]{:S(2)}) collective-permute-start(bf16[64,4096]{1,0:T(8,128)(2,1)S(1)} %shard_map.95.refs_2_), channel_id=1, source_target_pairs={{0,32},{32,64},{64,96},{96,128},{128,160},{160,192},{192,224},{224... | collective-permute-start | bytes 1572872 | tf_op jit(solution)/shard_map/ppermute | solution.py:25
  43.0 13.9 %collective-permute-start.2 = (bf16[64,4096]{1,0:T(8,128)(2,1)S(1)}, bf16[64,4096]{1,0:T(8,128)(2,1)S(1)}, u32[]{:S(2)}, u32[]{:S(2)}) collective-permute-start(bf16[64,4096]{1,0:T(8,128)(2,1)S(1)} %collective-permute-done.1.refs_3_), channel_id=1, source_target_pairs={{0,224},{32,0},{64,32},{96,64},{128,96},{160,128},{192,160},{224,1... | collective-permute-start | bytes 1572872 | tf_op jit(solution)/shard_map/ppermute | solution.py:25
  46.4 13.9 %collective-permute-start.5 = (bf16[64,4096]{1,0:T(8,128)(2,1)S(1)}, bf16[64,4096]{1,0:T(8,128)(2,1)S(1)}, u32[]{:S(2)}, u32[]{:S(2)}) collective-permute-start(bf16[64,4096]{1,0:T(8,128)(2,1)S(1)} %collective-permute-done.4.refs_1_), channel_id=1, source_target_pairs={{0,32},{32,64},{64,96},{96,128},{128,160},{160,192},{192,224},{224... | collective-permute-start | bytes 1572872 | tf_op jit(solution)/shard_map/ppermute | solution.py:25
  56.8 12.9 %collective-permute-start.3 = (bf16[64,4096]{1,0:T(8,128)(2,1)S(1)}, bf16[64,4096]{1,0:T(8,128)(2,1)S(1)}, u32[]{:S(2)}, u32[]{:S(2)}) collective-permute-start(bf16[64,4096]{1,0:T(8,128)(2,1)S(1)} %collective-permute-done.2.refs_0_), channel_id=1, source_target_pairs={{0,224},{32,0},{64,32},{96,64},{128,96},{160,128},{192,160},{224,1... | collective-permute-start | bytes 1572872 | tf_op jit(solution)/shard_map/ppermute | solution.py:25
  60.3 12.7 %collective-permute-start.6 = (bf16[64,4096]{1,0:T(8,128)(2,1)S(1)}, bf16[64,4096]{1,0:T(8,128)(2,1)S(1)}, u32[]{:S(2)}, u32[]{:S(2)}) collective-permute-start(bf16[64,4096]{1,0:T(8,128)(2,1)S(1)} %collective-permute-done.5.refs_0_), channel_id=1, source_target_pairs={{0,32},{32,64},{64,96},{96,128},{128,160},{160,192},{192,224},{224... | collective-permute-start | bytes 1572872 | tf_op jit(solution)/shard_map/ppermute | solution.py:25
  61.9 3.3 %collective-permute-start.7 = (f32[336,256]{1,0:T(8,128)S(1)}, f32[336,256]{1,0:T(8,128)S(1)}, u32[]{:S(2)}, u32[]{:S(2)}) collective-permute-start(f32[336,256]{1,0:T(8,128)S(1)} %get-tuple-element.63), channel_id=1, source_target_pairs={{0,2},{2,0},{1,3},{3,1},{4,6},{6,4},{5,7},{7,5},{8,10},{10,8},{9,1... | collective-permute-start | bytes 1032200 | tf_op jit(solution)/shard_map/ppermute | solution.py:25
  72.9 8.2 %collective-permute-start.10 = (f32[336,256]{1,0:T(8,128)S(1)}, f32[336,256]{1,0:T(8,128)S(1)}, u32[]{:S(2)}, u32[]{:S(2)}) collective-permute-start(f32[336,256]{1,0:T(8,128)S(1)} %add.26.sum_ref), channel_id=1, source_target_pairs={{0,1},{1,0},{2,3},{3,2},{4,5},{5,4},{6,7},{7,6},{8,9},{9,8},{10,11... | collective-permute-start | bytes 1032200 | tf_op jit(solution)/shard_map/ppermute | solution.py:25
  73.6 5.3 %collective-permute-start.8 = (bf16[64,2048]{1,0:T(8,128)(2,1)S(1)}, bf16[64,2048]{1,0:T(8,128)(2,1)S(1)}, u32[]{:S(2)}, u32[]{:S(2)}) collective-permute-start(bf16[64,2048]{1,0:T(8,128)(2,1)S(1)} %slice.58), channel_id=1, source_target_pairs={{0,224},{32,0},{64,32},{96,64},{128,96},{160,128},{192,160},{224,1... | collective-permute-start | bytes 786440 | tf_op jit(solution)/shard_map/ppermute | solution.py:25
  74.0 6.8 %collective-permute-start.9 = (bf16[64,2048]{1,0:T(8,128)(2,1)S(1)}, bf16[64,2048]{1,0:T(8,128)(2,1)S(1)}, u32[]{:S(2)}, u32[]{:S(2)}) collective-permute-start(bf16[64,2048]{1,0:T(8,128)(2,1)S(1)} %slice.59), channel_id=1, source_target_pairs={{0,32},{32,64},{64,96},{96,128},{128,160},{160,192},{192,224},{224... | collective-permute-start | bytes 786440 | tf_op jit(solution)/shard_map/ppermute | solution.py:25
  82.7 5.3 %collective-permute-start.11 = (f32[336,256]{1,0:T(8,128)S(1)}, f32[336,256]{1,0:T(8,128)S(1)}, u32[]{:S(2)}, u32[]{:S(2)}) collective-permute-start(f32[336,256]{1,0:T(8,128)S(1)} %get-tuple-element.72), channel_id=1, source_target_pairs={{0,2},{2,0},{1,3},{3,1},{4,6},{6,4},{5,7},{7,5},{8,10},{10,8},{9,1... | collective-permute-start | bytes 1032200 | tf_op jit(solution)/shard_map/ppermute | solution.py:25
  88.0 11.0 %collective-permute-start.12 = (f32[336,256]{1,0:T(8,128)S(1)}, f32[336,256]{1,0:T(8,128)S(1)}, u32[]{:S(2)}, u32[]{:S(2)}) collective-permute-start(f32[336,256]{1,0:T(8,128)S(1)} %add.27.sum_ref), channel_id=1, source_target_pairs={{0,1},{1,0},{2,3},{3,2},{4,5},{5,4},{6,7},{7,6},{8,9},{9,8},{10,11... | collective-permute-start | bytes 1032200 | tf_op jit(solution)/shard_map/ppermute | solution.py:25
  99.2 2.3 %collective-permute-start.14 = (bf16[336,256]{1,0:T(8,128)(2,1)S(1)}, bf16[336,256]{1,0:T(8,128)(2,1)S(1)}, u32[]{:S(2)}, u32[]{:S(2)}) collective-permute-start(bf16[336,256]{1,0:T(8,128)(2,1)S(1)} %shard_map.102.own_ref), channel_id=1, source_target_pairs={{0,2},{2,0},{1,3},{3,1},{4,6},{6,4},{5,7},{7,5},{8,10},{10,8},{9,1... | collective-permute-start | bytes 516104 | tf_op jit(solution)/shard_map/ppermute | solution.py:25
  104.2 9.1 %collective-permute-start.15 = (bf16[64,2048]{1,0:T(8,128)(2,1)}, bf16[64,2048]{1,0:T(8,128)(2,1)}, u32[]{:S(2)}, u32[]{:S(2)}) collective-permute-start(bf16[64,2048]{1,0:T(8,128)(2,1)} %get-tuple-element.104), channel_id=1, source_target_pairs={{0,32},{32,64},{64,96},{96,128},{128,160},{160,192},{192,224},{224... | collective-permute-start | bytes 786440 | tf_op jit(solution)/shard_map/ppermute | solution.py:25
  107.3 11.5 %collective-permute-start.22 = (bf16[64,2048]{1,0:T(8,128)(2,1)}, bf16[64,2048]{1,0:T(8,128)(2,1)}, u32[]{:S(2)}, u32[]{:S(2)}) collective-permute-start(bf16[64,2048]{1,0:T(8,128)(2,1)} %get-tuple-element.102), channel_id=1, source_target_pairs={{0,32},{32,64},{64,96},{96,128},{128,160},{160,192},{192,224},{224... | collective-permute-start | bytes 786440 | tf_op jit(solution)/shard_map/ppermute | solution.py:25
  107.3 17.2 %collective-permute-start.17 = (bf16[64,2048]{1,0:T(8,128)(2,1)}, bf16[64,2048]{1,0:T(8,128)(2,1)S(1)}, u32[]{:S(2)}, u32[]{:S(2)}) collective-permute-start(bf16[64,2048]{1,0:T(8,128)(2,1)} %get-tuple-element.103), channel_id=1, source_target_pairs={{0,224},{32,0},{64,32},{96,64},{128,96},{160,128},{192,160},{224,1... | collective-permute-start | bytes 786440 | tf_op jit(solution)/shard_map/ppermute | solution.py:25
  110.0 10.7 %collective-permute-start.25 = (bf16[64,2048]{1,0:T(8,128)(2,1)}, bf16[64,2048]{1,0:T(8,128)(2,1)S(1)}, u32[]{:S(2)}, u32[]{:S(2)}) collective-permute-start(bf16[64,2048]{1,0:T(8,128)(2,1)} %get-tuple-element.101), channel_id=1, source_target_pairs={{0,224},{32,0},{64,32},{96,64},{128,96},{160,128},{192,160},{224,1... | collective-permute-start | bytes 786440 | tf_op jit(solution)/shard_map/ppermute | solution.py:25
  116.0 8.5 %collective-permute-start.16 = (bf16[64,2048]{1,0:T(8,128)(2,1)S(1)}, bf16[64,2048]{1,0:T(8,128)(2,1)S(1)}, u32[]{:S(2)}, u32[]{:S(2)}) collective-permute-start(bf16[64,2048]{1,0:T(8,128)(2,1)S(1)} %shard_map.104), channel_id=1, source_target_pairs={{0,32},{32,64},{64,96},{96,128},{128,160},{160,192},{192,224},{224... | collective-permute-start | bytes 786440 | tf_op jit(solution)/shard_map/ppermute | solution.py:25
  119.9 9.7 %collective-permute-start.23 = (bf16[64,2048]{1,0:T(8,128)(2,1)S(1)}, bf16[64,2048]{1,0:T(8,128)(2,1)S(1)}, u32[]{:S(2)}, u32[]{:S(2)}) collective-permute-start(bf16[64,2048]{1,0:T(8,128)(2,1)S(1)} %shard_map.109), channel_id=1, source_target_pairs={{0,32},{32,64},{64,96},{96,128},{128,160},{160,192},{192,224},{224... | collective-permute-start | bytes 786440 | tf_op jit(solution)/shard_map/ppermute | solution.py:25
  120.8 8.9 %collective-permute-start.26 = (bf16[64,2048]{1,0:T(8,128)(2,1)S(1)}, bf16[64,2048]{1,0:T(8,128)(2,1)S(1)}, u32[]{:S(2)}, u32[]{:S(2)}) collective-permute-start(bf16[64,2048]{1,0:T(8,128)(2,1)S(1)} %shard_map.111), channel_id=1, source_target_pairs={{0,224},{32,0},{64,32},{96,64},{128,96},{160,128},{192,160},{224,1... | collective-permute-start | bytes 786440 | tf_op jit(solution)/shard_map/ppermute | solution.py:25
  124.6 14.3 %collective-permute-start.18 = (bf16[64,2048]{1,0:T(8,128)(2,1)S(1)}, bf16[64,2048]{1,0:T(8,128)(2,1)S(1)}, u32[]{:S(2)}, u32[]{:S(2)}) collective-permute-start(bf16[64,2048]{1,0:T(8,128)(2,1)S(1)} %shard_map.105), channel_id=1, source_target_pairs={{0,32},{32,64},{64,96},{96,128},{128,160},{160,192},{192,224},{224... | collective-permute-start | bytes 786440 | tf_op jit(solution)/shard_map/ppermute | solution.py:25
  124.8 14.3 %collective-permute-start.20 = (bf16[64,2048]{1,0:T(8,128)(2,1)S(1)}, bf16[64,2048]{1,0:T(8,128)(2,1)S(1)}, u32[]{:S(2)}, u32[]{:S(2)}) collective-permute-start(bf16[64,2048]{1,0:T(8,128)(2,1)S(1)} %shard_map.107), channel_id=1, source_target_pairs={{0,224},{32,0},{64,32},{96,64},{128,96},{160,128},{192,160},{224,1... | collective-permute-start | bytes 786440 | tf_op jit(solution)/shard_map/ppermute | solution.py:25
  129.6 14.5 %collective-permute-start.24 = (bf16[64,2048]{1,0:T(8,128)(2,1)S(1)}, bf16[64,2048]{1,0:T(8,128)(2,1)S(1)}, u32[]{:S(2)}, u32[]{:S(2)}) collective-permute-start(bf16[64,2048]{1,0:T(8,128)(2,1)S(1)} %shard_map.110), channel_id=1, source_target_pairs={{0,32},{32,64},{64,96},{96,128},{128,160},{160,192},{192,224},{224... | collective-permute-start | bytes 786440 | tf_op jit(solution)/shard_map/ppermute | solution.py:25
  129.8 12.1 %collective-permute-start.27 = (bf16[64,2048]{1,0:T(8,128)(2,1)S(1)}, bf16[64,2048]{1,0:T(8,128)(2,1)S(1)}, u32[]{:S(2)}, u32[]{:S(2)}) collective-permute-start(bf16[64,2048]{1,0:T(8,128)(2,1)S(1)} %shard_map.112), channel_id=1, source_target_pairs={{0,224},{32,0},{64,32},{96,64},{128,96},{160,128},{192,160},{224,1... | collective-permute-start | bytes 786440 | tf_op jit(solution)/shard_map/ppermute | solution.py:25
  134.1 25.6 %collective-permute-start.30 = (bf16[112,2048]{1,0:T(8,128)(2,1)}, bf16[112,2048]{1,0:T(8,128)(2,1)}, u32[]{:S(2)}, u32[]{:S(2)}) collective-permute-start(bf16[112,2048]{1,0:T(8,128)(2,1)} %fusion.3), channel_id=1, source_target_pairs={{0,2},{2,0},{1,3},{3,1},{4,6},{6,4},{5,7},{7,5},{8,10},{10,8},{9,1... | collective-permute-start | bytes 1376264 | tf_op jit(solution)/shard_map/ppermute | solution.py:25
  138.9 9.2 %collective-permute-start.19 = (bf16[64,2048]{1,0:T(8,128)(2,1)S(1)}, bf16[64,2048]{1,0:T(8,128)(2,1)S(1)}, u32[]{:S(2)}, u32[]{:S(2)}) collective-permute-start(bf16[64,2048]{1,0:T(8,128)(2,1)S(1)} %shard_map.106), channel_id=1, source_target_pairs={{0,32},{32,64},{64,96},{96,128},{128,160},{160,192},{192,224},{224... | collective-permute-start | bytes 786440 | tf_op jit(solution)/shard_map/ppermute | solution.py:25
  139.1 9.0 %collective-permute-start.21 = (bf16[64,2048]{1,0:T(8,128)(2,1)S(1)}, bf16[64,2048]{1,0:T(8,128)(2,1)S(1)}, u32[]{:S(2)}, u32[]{:S(2)}) collective-permute-start(bf16[64,2048]{1,0:T(8,128)(2,1)S(1)} %shard_map.108), channel_id=1, source_target_pairs={{0,224},{32,0},{64,32},{96,64},{128,96},{160,128},{192,160},{224,1... | collective-permute-start | bytes 786440 | tf_op jit(solution)/shard_map/ppermute | solution.py:25
  141.9 11.0 %collective-permute-start.28 = (bf16[64,2048]{1,0:T(8,128)(2,1)S(1)}, bf16[64,2048]{1,0:T(8,128)(2,1)S(1)}, u32[]{:S(2)}, u32[]{:S(2)}) collective-permute-start(bf16[64,2048]{1,0:T(8,128)(2,1)S(1)} %shard_map.113), channel_id=1, source_target_pairs={{0,224},{32,0},{64,32},{96,64},{128,96},{160,128},{192,160},{224,1... | collective-permute-start | bytes 786440 | tf_op jit(solution)/shard_map/ppermute | solution.py:25
  144.1 20.2 %collective-permute-start.29 = (bf16[224,2048]{1,0:T(8,128)(2,1)}, bf16[224,2048]{1,0:T(8,128)(2,1)}, u32[]{:S(2)}, u32[]{:S(2)}) collective-permute-start(bf16[224,2048]{1,0:T(8,128)(2,1)} %fusion.1), channel_id=1, source_target_pairs={{0,2},{2,0},{1,3},{3,1},{4,6},{6,4},{5,7},{7,5},{8,10},{10,8},{9,1... | collective-permute-start | bytes 2752520 | tf_op jit(solution)/shard_map/ppermute | solution.py:25
  154.1 16.9 %all-to-all-start.1 = ((bf16[32,2,4096]{2,1,0:T(2,128)(2,1)}), bf16[32,2,4096]{2,1,0:T(2,128)(2,1)}, u32[]{:S(2)}, u32[]{:S(2)}) async-start(bf16[32,2,4096]{2,1,0:T(2,128)(2,1)} %copy-done.14), calls=%async_computation.1 | async-start | bytes 1048576 | tf_op jit(solution)/shard_map/all_to_all | solution.py:29
  (25 other events, 137.9 us)

commit v5 on v4

--- a/solution.py
+++ b/solution.py
@@ -76,6 +76,15 @@
     return jax.ShapeDtypeStruct(shape, kind)
 
 
+def copy_rows(dst, src, at, start, count):
+    def some(i, carry):
+        to = pl.ds(pl.multiple_of(at + i * 16, 16), 16)
+        dst[to, :] = src[pl.ds(pl.multiple_of(start + i * 16, 16), 16), :]
+        return carry
+
+    lax.fori_loop(0, count // 16, some, 0)
+
+
 def deal_kernel(tokens_ref, upstream_ref, out_ref, *, quarters):
     part = tokens_ref.shape[1] // quarters
     for q in range(quarters):
@@ -86,44 +95,33 @@
             out_ref[j * quarters + q, :, part:] = grads
 
 
-def merge_kernel(blocks_ref, out_ref, rows_ref):
+def merge_kernel(blocks_ref, left_ref, right_ref, rows_ref):
     n, pair, _ = blocks_ref.shape
     for j in range(n):
         rows_ref[j * pair : (j + 1) * pair, :] = blocks_ref[j].astype(F32)
-    out_ref[...] = rows_ref[...].astype(BF16)
+    left_ref[...] = rows_ref[:, : left_ref.shape[1]].astype(BF16)
+    right_ref[...] = rows_ref[:, left_ref.shape[1] :].astype(BF16)
 
 
 def pack_kernel(_, gate_ref, up_ref, down_ref, out_ref):
     units = gate_ref.shape[0]
     for j, ref in enumerate((gate_ref, up_ref, down_ref)):
-        out_ref[j * units : (j + 1) * units, :] = ref[...]
+        copy_rows(out_ref, ref, j * units, 0, units)
 
 
 def weights_kernel(_, gate_ref, up_ref, down_ref, got_ref, in_ref, out_ref):
     units = gate_ref.shape[0]
-    in_ref[:units, :] = gate_ref[...]
-    in_ref[units : 2 * units, :] = up_ref[...]
-    in_ref[2 * units :, :] = got_ref[: 2 * units, :]
-    out_ref[:units, :] = down_ref[...]
-    out_ref[units:, :] = got_ref[2 * units :, :]
+    copy_rows(in_ref, gate_ref, 0, 0, units)
+    copy_rows(in_ref, up_ref, units, 0, units)
+    copy_rows(in_ref, got_ref, 2 * units, 0, 2 * units)
+    copy_rows(out_ref, down_ref, 0, 0, units)
+    copy_rows(out_ref, got_ref, units, 2 * units, units)
 
 
 def stack_kernel(*refs):
-    *block_refs, rows_ref, grads_ref = refs
-    part = rows_ref.shape[1]
-    k = 0
-    for ref in block_refs:
-        height, width = ref.shape
-        at = slice(k * height, (k + 1) * height)
-        if width == 2 * part:
-            rows_ref[at, :] = ref[:, :part]
-            grads_ref[at, :] = ref[:, part:]
-            k += 1
-        elif ref is block_refs[-2]:
-            rows_ref[at, :] = ref[...]
-        else:
-            grads_ref[at, :] = ref[...]
-            k += 1
+    *block_refs, out_ref = refs
+    for k, ref in enumerate(block_refs):
+        copy_rows(out_ref, ref, k * ref.shape[0], 0, ref.shape[0])
 
 
 def partial_kernel(rows_ref, grads_ref, in_ref, out_ref, own_ref, other_ref):
@@ -156,7 +154,12 @@
 
 
 def turn_kernel(_, term_ref, came_ref, out_ref):
-    out_ref[...] = (term_ref[...] + came_ref[...].astype(F32)).astype(BF16)
+    def some(i, carry):
+        at = pl.ds(pl.multiple_of(i * 16, 16), 16)
+        out_ref[at, :] = (term_ref[at, :] + came_ref[at, :].astype(F32)).astype(BF16)
+        return carry
+
+    lax.fori_loop(0, term_ref.shape[0] // 16, some, 0)
 
 
 def close_kernel(_, a0_ref, b0_ref, a1_ref, a2_ref, b1_ref, b2_ref, out_ref, rows_ref):
@@ -266,16 +269,15 @@
     )
     dealt = exchanged(dealt, (*PLANE, *PAIRS))
     dealt, in_weights, out_weights = lax.optimization_barrier((dealt, in_weights, out_weights))
-    block = called(
+    blocks = called(
         merge_kernel,
-        shape_of((n_rows, 2 * part)),
+        (shape_of((n_rows, part)), shape_of((n_rows, part))),
         dealt,
         scratch=[pltpu.VMEM((n_rows, 2 * part), F32)],
     )
 
     def stacked(*blocks):
-        shape = shape_of((half * n_rows, part))
-        return called(stack_kernel, (shape, shape), *blocks)
+        return called(stack_kernel, shape_of((half * n_rows, part)), *blocks)
 
     def partial_sums(rows, grads):
         shape = shape_of((3 * units, rows.shape[0]), F32)
@@ -294,21 +296,28 @@
         )
 
     half = n_z // 2
-    ring = {0: block}
+    rings = [{0: block} for block in blocks]
     for k in range(1, half):
-        ring[k], ring[-k] = shifted(ring[k - 1], "z", -1), shifted(ring[1 - k], "z", 1)
-    near_rows, near_grads = stacked(*(ring[k] for k in range(-half // 2, half // 2)))
+        for ring in rings:
+            ring[k], ring[-k] = shifted(ring[k - 1], "z", -1), shifted(ring[1 - k], "z", 1)
+    near_rows, near_grads = (
+        stacked(*(ring[k] for k in range(-half // 2, half // 2))) for ring in rings
+    )
     own, other = partial_sums(near_rows, near_grads)
     near_sums = own + shifted(other, "core", 1)
-    ahead, behind, near_sums = lax.optimization_barrier((ring[half - 1], ring[1 - half], near_sums))
-    left, right = shifted(ahead[:, :part], "z", -1), shifted(behind[:, part:], "z", 1)
+    ahead, behind = rings[0][half - 1], rings[1][1 - half]
+    behind, near_sums = lax.optimization_barrier((behind, near_sums))
     near_got = shifted(near_sums, "tok", 1)
-    left, right, near_got = lax.optimization_barrier((left, right, near_got))
-    far_rows, far_grads = stacked(
-        *(ring[k] for k in range(half // 2, half)),
-        *(ring[k] for k in range(1 - half, -half // 2)),
-        left,
-        right,
+    *ends, near_got = lax.optimization_barrier(
+        (shifted(ahead, "z", -1), shifted(behind, "z", 1), near_got)
+    )
+    far_rows, far_grads = (
+        stacked(
+            *(ring[k] for k in range(half // 2, half)),
+            *(ring[k] for k in range(1 - half, -half // 2)),
+            end,
+        )
+        for ring, end in zip(rings, ends, strict=True)
     )
     own, other = partial_sums(far_rows, far_grads)
     far_sums = own + shifted(other, "core", 1)

time: 174 us -> 172 us (0.989)
    pallas_call x11 -> x13, Pallas kernels: 6.19 us -> 5.3 us  [called(): pl.pallas_call(functools.partial(kernel, **kwargs), out_shape=out_shape,...]
    ppermute x31 -> x37, starting transfers between devices: 52.9 us -> 52.3 us  [shifted(): lax.ppermute(block, axis, [(i, (i + distance) % count) for i in range(cou...]
    unnamed x48 -> x38, local copies, waits for them, and re-layouts: 6.44 us -> 5.94 us
    ppermute x31 -> x37, waiting for transfers between devices: 59.4 us -> 59.2 us  [shifted(): lax.ppermute(block, axis, [(i, (i + distance) % count) for i in range(cou...]
  transfers between devices with their start and end apart: 33 -> 39, of which waited for: 19 -> 22; matrix products, arithmetic and copies ran while one was open for 8% -> 8% of each run, Pallas kernels for 5% -> 5%
where the time goes in v5:
time: 172 us; the launch traced here: 171 us
  waiting for transfers between devices  69.6 us (40%)
  starting transfers between devices  63.2 us (37%)
  Pallas kernels  15.3 us (9%)
  matrix products  10.6 us (6%)
  local copies, waits for them, and re-layouts  7.63 us (4%)
  other arithmetic  3.72 us (2%)
    ppermute x37, waiting for transfers between devices, shifted(): lax.ppermute(block, axis, [(i, (i + distance) % count) for i in range(cou...  59.2 us
    ppermute x37, starting transfers between devices, shifted(): lax.ppermute(block, axis, [(i, (i + distance) % count) for i in range(cou...  52.3 us
    all_to_all x2, starting transfers between devices, exchanged(): return lax.all_to_all(blocks, axes, 0, 0, tiled=True)  11 us
    all_to_all x2, waiting for transfers between devices, exchanged(): return lax.all_to_all(blocks, axes, 0, 0, tiled=True)  10.4 us
    pallas_call x13, Pallas kernels, called_at(): pl.pallas_call(functools.partial(kernel, **kwargs), out_shape=out_shape,...  10.1 us
    unnamed x38, local copies, waits for them, and re-layouts  5.94 us
    pallas_call x13, Pallas kernels, called(): pl.pallas_call(functools.partial(kernel, **kwargs), out_shape=out_shape,...  5.3 us
    dot_general x4, matrix products, by_columns(): lax.dot_general(left, right, (((0,), (0,)), ((), ())), preferred_element_...  5.04 us
  transfers between devices with their start and end apart: 39, of which 22 were waited for; matrix products, arithmetic and copies ran while one was open for 8% of the time, Pallas kernels for 5%

profile of v5, /device:TPU:1, one launch (start us, length us, event | category | flops | bytes accessed | tf_op | source)
XLA Modules:
  0.0 171.3 jit_solution(11877214315671222252)
XLA Ops:
  3.0 2.6 %shard_map.93 = bf16[336,2048]{1,0:T(8,128)(2,1)} custom-call(s32[1]{0:T(128)} %bitcast.1._, bf16[112,8192]{1,0:T(8,128)(2,1)} %gate_ref.1, bf16[112,8192]{1,0:T(8,128)(2,1)} %up_ref.1, bf16[112,8192]{1,0:T(8,128)(2,1)} %down_ref.1), custom_call_target="tpu_custom_call" | custom-call | tf_op jit(solution)/shard_map/pallas_call | solution.py:67
  5.5 3.2 %collective-permute-start = (bf16[336,2048]{1,0:T(8,128)(2,1)}, bf16[336,2048]{1,0:T(8,128)(2,1)S(1)}, u32[]{:S(2)}, u32[]{:S(2)}) collective-permute-start(bf16[336,2048]{1,0:T(8,128)(2,1)} %shard_map.93), channel_id=1, source_target_pairs={{0,2},{2,0},{1,3},{3,1},{4,6},{6,4},{5,7},{7,5},{8,10},{10,8},{9,1... | collective-permute-start | bytes 4128776 | tf_op jit(solution)/shard_map/ppermute | solution.py:25
  8.8 5.5 %all-to-all-start = ((bf16[32,2,4096]{2,1,0:T(2,128)(2,1)}), bf16[32,2,4096]{2,1,0:T(2,128)(2,1)S(1)}, u32[]{:S(2)}, u32[]{:S(2)}) async-start(bf16[32,2,4096]{2,1,0:T(2,128)(2,1)} %shard_map.92), calls=%async_computation | async-start | bytes 1048576 | tf_op jit(solution)/shard_map/all_to_all | solution.py:29
  15.4 3.6 %shard_map.94 = (bf16[448,2048]{1,0:T(8,128)(2,1)}, bf16[224,2048]{1,0:T(8,128)(2,1)}) custom-call(s32[1]{0:T(128)} %bitcast._, bf16[112,8192]{1,0:T(8,128)(2,1)} %gate_ref.1, bf16[112,8192]{1,0:T(8,128)(2,1)} %up_ref.1, bf16[112,8192]{1,0:T(8,128)(2,1)} %down_ref.1, bf16[336,2048]{1,0:T(8,128)(2,1)} %copy-done.18), custom_call_target="tpu_custom_call" | custom-call | tf_op jit(solution)/shard_map/pallas_call | solution.py:67
  19.0 6.7 %all-to-all-done.blocks_ref = bf16[32,2,4096]{2,1,0:T(2,128)(2,1)S(1)} async-done(((bf16[32,2,4096]{2,1,0:T(2,128)(2,1)}), bf16[32,2,4096]{2,1,0:T(2,128)(2,1)S(1)}, u32[]{:S(2)}, u32[]{:S(2)}) %all-to-all-start) | async-done | bytes 524320 | tf_op jit(solution)/shard_map/all_to_all | solution.py:29
  29.4 2.5 %collective-permute-start.1 = (bf16[64,2048]{1,0:T(8,128)(2,1)S(1)}, bf16[64,2048]{1,0:T(8,128)(2,1)S(1)}, u32[]{:S(2)}, u32[]{:S(2)}) collective-permute-start(bf16[64,2048]{1,0:T(8,128)(2,1)S(1)} %get-tuple-element.55.refs_2_), channel_id=1, source_target_pairs={{0,224},{32,0},{64,32},{96,64},{128,96},{160,128},{192,160},{224,1... | collective-permute-start | bytes 786440 | tf_op jit(solution)/shard_map/ppermute | solution.py:25
  31.9 6.5 %collective-permute-done.4.refs_1_ = bf16[64,2048]{1,0:T(8,128)(2,1)S(1)} collective-permute-done((bf16[64,2048]{1,0:T(8,128)(2,1)S(1)}, bf16[64,2048]{1,0:T(8,128)(2,1)S(1)}, u32[]{:S(2)}, u32[]{:S(2)}) %collective-permute-start.4) | collective-permute-done | bytes 262176 | tf_op jit(solution)/shard_map/ppermute | solution.py:25
  38.4 2.7 %collective-permute-start.11 = (bf16[64,2048]{1,0:T(8,128)(2,1)S(1)}, bf16[64,2048]{1,0:T(8,128)(2,1)S(1)}, u32[]{:S(2)}, u32[]{:S(2)}) collective-permute-start(bf16[64,2048]{1,0:T(8,128)(2,1)S(1)} %get-tuple-element.56.refs_2_), channel_id=1, source_target_pairs={{0,224},{32,0},{64,32},{96,64},{128,96},{160,128},{192,160},{224,1... | collective-permute-start | bytes 786440 | tf_op jit(solution)/shard_map/ppermute | solution.py:25
  41.0 2.9 %collective-permute-done.8.refs_1_ = bf16[64,2048]{1,0:T(8,128)(2,1)S(1)} collective-permute-done((bf16[64,2048]{1,0:T(8,128)(2,1)S(1)}, bf16[64,2048]{1,0:T(8,128)(2,1)S(1)}, u32[]{:S(2)}, u32[]{:S(2)}) %collective-permute-start.8) | collective-permute-done | bytes 262176 | tf_op jit(solution)/shard_map/ppermute | solution.py:25
  44.0 2.7 %collective-permute-start.2 = (bf16[64,2048]{1,0:T(8,128)(2,1)S(1)}, bf16[64,2048]{1,0:T(8,128)(2,1)S(1)}, u32[]{:S(2)}, u32[]{:S(2)}) collective-permute-start(bf16[64,2048]{1,0:T(8,128)(2,1)S(1)} %collective-permute-done.1.refs_3_), channel_id=1, source_target_pairs={{0,224},{32,0},{64,32},{96,64},{128,96},{160,128},{192,160},{224,1... | collective-permute-start | bytes 786440 | tf_op jit(solution)/shard_map/ppermute | solution.py:25
  46.7 2.9 %collective-permute-done.5.refs_0_ = bf16[64,2048]{1,0:T(8,128)(2,1)S(1)} collective-permute-done((bf16[64,2048]{1,0:T(8,128)(2,1)S(1)}, bf16[64,2048]{1,0:T(8,128)(2,1)S(1)}, u32[]{:S(2)}, u32[]{:S(2)}) %collective-permute-start.5) | collective-permute-done | bytes 262176 | tf_op jit(solution)/shard_map/ppermute | solution.py:25
  49.7 5.5 %collective-permute-done.9.refs_0_ = bf16[64,2048]{1,0:T(8,128)(2,1)S(1)} collective-permute-done((bf16[64,2048]{1,0:T(8,128)(2,1)S(1)}, bf16[64,2048]{1,0:T(8,128)(2,1)S(1)}, u32[]{:S(2)}, u32[]{:S(2)}) %collective-permute-start.9) | collective-permute-done | bytes 262176 | tf_op jit(solution)/shard_map/ppermute | solution.py:25
  57.5 2.7 %collective-permute-start.3 = (bf16[64,2048]{1,0:T(8,128)(2,1)S(1)}, bf16[64,2048]{1,0:T(8,128)(2,1)S(1)}, u32[]{:S(2)}, u32[]{:S(2)}) collective-permute-start(bf16[64,2048]{1,0:T(8,128)(2,1)S(1)} %collective-permute-done.2.refs_0_), channel_id=1, source_target_pairs={{0,224},{32,0},{64,32},{96,64},{128,96},{160,128},{192,160},{224,1... | collective-permute-start | bytes 786440 | tf_op jit(solution)/shard_map/ppermute | solution.py:25
  60.5 6.1 %collective-permute-done.10.refs_2_ = bf16[64,2048]{1,0:T(8,128)(2,1)S(1)} collective-permute-done((bf16[64,2048]{1,0:T(8,128)(2,1)S(1)}, bf16[64,2048]{1,0:T(8,128)(2,1)S(1)}, u32[]{:S(2)}, u32[]{:S(2)}) %collective-permute-start.10) | collective-permute-done | bytes 262176 | tf_op jit(solution)/shard_map/ppermute | solution.py:25
  69.3 1.8 %collective-permute-done.15.refs_0_ = bf16[64,2048]{1,0:T(8,128)(2,1)S(1)} collective-permute-done((bf16[64,2048]{1,0:T(8,128)(2,1)S(1)}, bf16[64,2048]{1,0:T(8,128)(2,1)S(1)}, u32[]{:S(2)}, u32[]{:S(2)}) %collective-permute-start.15) | collective-permute-done | bytes 262176 | tf_op jit(solution)/shard_map/ppermute | solution.py:25
  71.1 3.4 %collective-permute-start.16 = (bf16[64,2048]{1,0:T(8,128)(2,1)S(1)}, bf16[64,2048]{1,0:T(8,128)(2,1)S(1)}, u32[]{:S(2)}, u32[]{:S(2)}) collective-permute-start(bf16[64,2048]{1,0:T(8,128)(2,1)S(1)} %collective-permute-done.15.refs_0_), channel_id=1, source_target_pairs={{0,224},{32,0},{64,32},{96,64},{128,96},{160,128},{192,160},{224,1... | collective-permute-start | bytes 786440 | tf_op jit(solution)/shard_map/ppermute | solution.py:25
  74.5 2.2 %collective-permute-done.7.refs_3_ = bf16[64,2048]{1,0:T(8,128)(2,1)S(1)} collective-permute-done((bf16[64,2048]{1,0:T(8,128)(2,1)S(1)}, bf16[64,2048]{1,0:T(8,128)(2,1)S(1)}, u32[]{:S(2)}, u32[]{:S(2)}) %collective-permute-start.7) | collective-permute-done | bytes 262176 | tf_op jit(solution)/shard_map/ppermute | solution.py:25
  76.7 4.5 %collective-permute-done.6.refs_2_ = bf16[64,2048]{1,0:T(8,128)(2,1)S(1)} collective-permute-done((bf16[64,2048]{1,0:T(8,128)(2,1)S(1)}, bf16[64,2048]{1,0:T(8,128)(2,1)S(1)}, u32[]{:S(2)}, u32[]{:S(2)}) %collective-permute-start.6) | collective-permute-done | bytes 262176 | tf_op jit(solution)/shard_map/ppermute | solution.py:25
  83.9 2.3 %collective-permute-start.17 = (f32[336,256]{1,0:T(8,128)S(1)}, f32[336,256]{1,0:T(8,128)S(1)}, u32[]{:S(2)}, u32[]{:S(2)}) collective-permute-start(f32[336,256]{1,0:T(8,128)S(1)} %get-tuple-element.66), channel_id=1, source_target_pairs={{0,2},{2,0},{1,3},{3,1},{4,6},{6,4},{5,7},{7,5},{8,10},{10,8},{9,1... | collective-permute-start | bytes 1032200 | tf_op jit(solution)/shard_map/ppermute | solution.py:25
  90.8 7.7 %collective-permute-done.18.got_ref = f32[336,256]{1,0:T(8,128)S(1)} collective-permute-done((f32[336,256]{1,0:T(8,128)S(1)}, f32[336,256]{1,0:T(8,128)S(1)}, u32[]{:S(2)}, u32[]{:S(2)}) %collective-permute-start.18) | collective-permute-done | bytes 344096 | tf_op jit(solution)/shard_map/ppermute | solution.py:25
  103.5 2.1 %fusion.19 = (bf16[256,2048]{1,0:T(8,128)(2,1)S(1)}, f32[256,2048]{1,0:T(8,128)}) fusion(bf16[448,256]{1,0:T(8,128)(2,1)S(1)} %get-tuple-element.84, bf16[448,2048]{1,0:T(8,128)(2,1)S(1)} %copy-done), kind=kOutput, calls=%fused_computation.32 | convolution fusion | flops 470286336 | bytes 5210112 | tf_op jit(solution)/shard_map/dot_general | solution.py:37
  106.4 1.8 %collective-permute-start.28 = (bf16[64,2048]{1,0:T(8,128)(2,1)}, bf16[64,2048]{1,0:T(8,128)(2,1)}, u32[]{:S(2)}, u32[]{:S(2)}) collective-permute-start(bf16[64,2048]{1,0:T(8,128)(2,1)} %get-tuple-element.96), channel_id=1, source_target_pairs={{0,32},{32,64},{64,96},{96,128},{128,160},{160,192},{192,224},{224... | collective-permute-start | bytes 786440 | tf_op jit(solution)/shard_map/ppermute | solution.py:25
  110.5 2.0 %collective-permute-done.21.came_ref = bf16[64,2048]{1,0:T(8,128)(2,1)} collective-permute-done((bf16[64,2048]{1,0:T(8,128)(2,1)}, bf16[64,2048]{1,0:T(8,128)(2,1)}, u32[]{:S(2)}, u32[]{:S(2)}) %collective-permute-start.21) | collective-permute-done | bytes 262176 | tf_op jit(solution)/shard_map/ppermute | solution.py:25
  115.4 2.8 %collective-permute-done.28.came_ref = bf16[64,2048]{1,0:T(8,128)(2,1)} collective-permute-done((bf16[64,2048]{1,0:T(8,128)(2,1)}, bf16[64,2048]{1,0:T(8,128)(2,1)}, u32[]{:S(2)}, u32[]{:S(2)}) %collective-permute-start.28) | collective-permute-done | bytes 262176 | tf_op jit(solution)/shard_map/ppermute | solution.py:25
  120.0 2.5 %collective-permute-done.31.came_ref = bf16[64,2048]{1,0:T(8,128)(2,1)S(1)} collective-permute-done((bf16[64,2048]{1,0:T(8,128)(2,1)}, bf16[64,2048]{1,0:T(8,128)(2,1)S(1)}, u32[]{:S(2)}, u32[]{:S(2)}) %collective-permute-start.31) | collective-permute-done | bytes 262176 | tf_op jit(solution)/shard_map/ppermute | solution.py:25
  129.2 2.6 %collective-permute-start.33 = (bf16[64,2048]{1,0:T(8,128)(2,1)S(1)}, bf16[64,2048]{1,0:T(8,128)(2,1)S(1)}, u32[]{:S(2)}, u32[]{:S(2)}) collective-permute-start(bf16[64,2048]{1,0:T(8,128)(2,1)S(1)} %shard_map.114), channel_id=1, source_target_pairs={{0,224},{32,0},{64,32},{96,64},{128,96},{160,128},{192,160},{224,1... | collective-permute-start | bytes 786440 | tf_op jit(solution)/shard_map/ppermute | solution.py:25
  133.2 4.3 %collective-permute-start.36 = (bf16[112,2048]{1,0:T(8,128)(2,1)}, bf16[112,2048]{1,0:T(8,128)(2,1)}, u32[]{:S(2)}, u32[]{:S(2)}) collective-permute-start(bf16[112,2048]{1,0:T(8,128)(2,1)} %fusion.3), channel_id=1, source_target_pairs={{0,2},{2,0},{1,3},{3,1},{4,6},{6,4},{5,7},{7,5},{8,10},{10,8},{9,1... | collective-permute-start | bytes 1376264 | tf_op jit(solution)/shard_map/ppermute | solution.py:25
  138.3 2.7 %collective-permute-start.27 = (bf16[64,2048]{1,0:T(8,128)(2,1)S(1)}, bf16[64,2048]{1,0:T(8,128)(2,1)S(1)}, u32[]{:S(2)}, u32[]{:S(2)}) collective-permute-start(bf16[64,2048]{1,0:T(8,128)(2,1)S(1)} %shard_map.110), channel_id=1, source_target_pairs={{0,224},{32,0},{64,32},{96,64},{128,96},{160,128},{192,160},{224,1... | collective-permute-start | bytes 786440 | tf_op jit(solution)/shard_map/ppermute | solution.py:25
  143.9 2.7 %collective-permute-start.35 = (bf16[224,2048]{1,0:T(8,128)(2,1)}, bf16[224,2048]{1,0:T(8,128)(2,1)}, u32[]{:S(2)}, u32[]{:S(2)}) collective-permute-start(bf16[224,2048]{1,0:T(8,128)(2,1)} %fusion.1), channel_id=1, source_target_pairs={{0,2},{2,0},{1,3},{3,1},{4,6},{6,4},{5,7},{7,5},{8,10},{10,8},{9,1... | collective-permute-start | bytes 2752520 | tf_op jit(solution)/shard_map/ppermute | solution.py:25
  147.1 5.3 %collective-permute-done.34.b2_ref = bf16[64,2048]{1,0:T(8,128)(2,1)S(1)} collective-permute-done((bf16[64,2048]{1,0:T(8,128)(2,1)S(1)}, bf16[64,2048]{1,0:T(8,128)(2,1)S(1)}, u32[]{:S(2)}, u32[]{:S(2)}) %collective-permute-start.34) | collective-permute-done | bytes 262176 | tf_op jit(solution)/shard_map/ppermute | solution.py:25
  153.6 5.5 %all-to-all-start.1 = ((bf16[32,2,4096]{2,1,0:T(2,128)(2,1)}), bf16[32,2,4096]{2,1,0:T(2,128)(2,1)S(1)}, u32[]{:S(2)}, u32[]{:S(2)}) async-start(bf16[32,2,4096]{2,1,0:T(2,128)(2,1)} %shard_map.116), calls=%async_computation.1 | async-start | bytes 1048576 | tf_op jit(solution)/shard_map/all_to_all | solution.py:29
  166.9 3.6 %all-to-all-done.1.blocks_ref = bf16[32,2,4096]{2,1,0:T(2,128)(2,1)S(1)} async-done(((bf16[32,2,4096]{2,1,0:T(2,128)(2,1)}), bf16[32,2,4096]{2,1,0:T(2,128)(2,1)S(1)}, u32[]{:S(2)}, u32[]{:S(2)}) %all-to-all-start.1) | async-done | bytes 524320 | tf_op jit(solution)/shard_map/all_to_all | solution.py:29
  (129 shorter events, 54.2 us)
Async XLA Ops:
  8.8 16.9 %all-to-all-start = ((bf16[32,2,4096]{2,1,0:T(2,128)(2,1)}), bf16[32,2,4096]{2,1,0:T(2,128)(2,1)S(1)}, u32[]{:S(2)}, u32[]{:S(2)}) async-start(bf16[32,2,4096]{2,1,0:T(2,128)(2,1)} %shard_map.92), calls=%async_computation | async-start | bytes 1048576 | tf_op jit(solution)/shard_map/all_to_all | solution.py:29
  26.0 12.3 %collective-permute-start.4 = (bf16[64,2048]{1,0:T(8,128)(2,1)S(1)}, bf16[64,2048]{1,0:T(8,128)(2,1)S(1)}, u32[]{:S(2)}, u32[]{:S(2)}) collective-permute-start(bf16[64,2048]{1,0:T(8,128)(2,1)S(1)} %get-tuple-element.55.refs_2_), channel_id=1, source_target_pairs={{0,32},{32,64},{64,96},{96,128},{128,160},{160,192},{192,224},{224... | collective-permute-start | bytes 786440 | tf_op jit(solution)/shard_map/ppermute | solution.py:25
  27.8 16.2 %collective-permute-start.8 = (bf16[64,2048]{1,0:T(8,128)(2,1)S(1)}, bf16[64,2048]{1,0:T(8,128)(2,1)S(1)}, u32[]{:S(2)}, u32[]{:S(2)}) collective-permute-start(bf16[64,2048]{1,0:T(8,128)(2,1)S(1)} %get-tuple-element.56.refs_2_), channel_id=1, source_target_pairs={{0,32},{32,64},{64,96},{96,128},{128,160},{160,192},{192,224},{224... | collective-permute-start | bytes 786440 | tf_op jit(solution)/shard_map/ppermute | solution.py:25
  29.4 14.6 %collective-permute-start.1 = (bf16[64,2048]{1,0:T(8,128)(2,1)S(1)}, bf16[64,2048]{1,0:T(8,128)(2,1)S(1)}, u32[]{:S(2)}, u32[]{:S(2)}) collective-permute-start(bf16[64,2048]{1,0:T(8,128)(2,1)S(1)} %get-tuple-element.55.refs_2_), channel_id=1, source_target_pairs={{0,224},{32,0},{64,32},{96,64},{128,96},{160,128},{192,160},{224,1... | collective-permute-start | bytes 786440 | tf_op jit(solution)/shard_map/ppermute | solution.py:25
  38.4 11.2 %collective-permute-start.5 = (bf16[64,2048]{1,0:T(8,128)(2,1)S(1)}, bf16[64,2048]{1,0:T(8,128)(2,1)S(1)}, u32[]{:S(2)}, u32[]{:S(2)}) collective-permute-start(bf16[64,2048]{1,0:T(8,128)(2,1)S(1)} %collective-permute-done.4.refs_1_), channel_id=1, source_target_pairs={{0,32},{32,64},{64,96},{96,128},{128,160},{160,192},{192,224},{224... | collective-permute-start | bytes 786440 | tf_op jit(solution)/shard_map/ppermute | solution.py:25
  38.4 11.4 %collective-permute-start.11 = (bf16[64,2048]{1,0:T(8,128)(2,1)S(1)}, bf16[64,2048]{1,0:T(8,128)(2,1)S(1)}, u32[]{:S(2)}, u32[]{:S(2)}) collective-permute-start(bf16[64,2048]{1,0:T(8,128)(2,1)S(1)} %get-tuple-element.56.refs_2_), channel_id=1, source_target_pairs={{0,224},{32,0},{64,32},{96,64},{128,96},{160,128},{192,160},{224,1... | collective-permute-start | bytes 786440 | tf_op jit(solution)/shard_map/ppermute | solution.py:25
  44.0 11.2 %collective-permute-start.9 = (bf16[64,2048]{1,0:T(8,128)(2,1)S(1)}, bf16[64,2048]{1,0:T(8,128)(2,1)S(1)}, u32[]{:S(2)}, u32[]{:S(2)}) collective-permute-start(bf16[64,2048]{1,0:T(8,128)(2,1)S(1)} %collective-permute-done.8.refs_1_), channel_id=1, source_target_pairs={{0,32},{32,64},{64,96},{96,128},{128,160},{160,192},{192,224},{224... | collective-permute-start | bytes 786440 | tf_op jit(solution)/shard_map/ppermute | solution.py:25
  44.0 13.5 %collective-permute-start.2 = (bf16[64,2048]{1,0:T(8,128)(2,1)S(1)}, bf16[64,2048]{1,0:T(8,128)(2,1)S(1)}, u32[]{:S(2)}, u32[]{:S(2)}) collective-permute-start(bf16[64,2048]{1,0:T(8,128)(2,1)S(1)} %collective-permute-done.1.refs_3_), channel_id=1, source_target_pairs={{0,224},{32,0},{64,32},{96,64},{128,96},{160,128},{192,160},{224,1... | collective-permute-start | bytes 786440 | tf_op jit(solution)/shard_map/ppermute | solution.py:25
  57.4 9.1 %collective-permute-start.10 = (bf16[64,2048]{1,0:T(8,128)(2,1)S(1)}, bf16[64,2048]{1,0:T(8,128)(2,1)S(1)}, u32[]{:S(2)}, u32[]{:S(2)}) collective-permute-start(bf16[64,2048]{1,0:T(8,128)(2,1)S(1)} %collective-permute-done.9.refs_0_), channel_id=1, source_target_pairs={{0,32},{32,64},{64,96},{96,128},{128,160},{160,192},{192,224},{224... | collective-permute-start | bytes 786440 | tf_op jit(solution)/shard_map/ppermute | solution.py:25
  57.5 10.3 %collective-permute-start.3 = (bf16[64,2048]{1,0:T(8,128)(2,1)S(1)}, bf16[64,2048]{1,0:T(8,128)(2,1)S(1)}, u32[]{:S(2)}, u32[]{:S(2)}) collective-permute-start(bf16[64,2048]{1,0:T(8,128)(2,1)S(1)} %collective-permute-done.2.refs_0_), channel_id=1, source_target_pairs={{0,224},{32,0},{64,32},{96,64},{128,96},{160,128},{192,160},{224,1... | collective-permute-start | bytes 786440 | tf_op jit(solution)/shard_map/ppermute | solution.py:25
  60.1 11.0 %collective-permute-start.15 = (bf16[64,2048]{1,0:T(8,128)(2,1)S(1)}, bf16[64,2048]{1,0:T(8,128)(2,1)S(1)}, u32[]{:S(2)}, u32[]{:S(2)}) collective-permute-start(bf16[64,2048]{1,0:T(8,128)(2,1)S(1)} %collective-permute-done.11.refs_3_), channel_id=1, source_target_pairs={{0,224},{32,0},{64,32},{96,64},{128,96},{160,128},{192,160},{224,1... | collective-permute-start | bytes 786440 | tf_op jit(solution)/shard_map/ppermute | solution.py:25
  66.5 10.2 %collective-permute-start.14 = (f32[336,256]{1,0:T(8,128)S(1)}, f32[336,256]{1,0:T(8,128)S(1)}, u32[]{:S(2)}, u32[]{:S(2)}) collective-permute-start(f32[336,256]{1,0:T(8,128)S(1)} %add.26.sum_ref), channel_id=1, source_target_pairs={{0,1},{1,0},{2,3},{3,2},{4,5},{5,4},{6,7},{7,6},{8,9},{9,8},{10,11... | collective-permute-start | bytes 1032200 | tf_op jit(solution)/shard_map/ppermute | solution.py:25
  67.8 8.9 %collective-permute-start.7 = (bf16[64,2048]{1,0:T(8,128)(2,1)S(1)}, bf16[64,2048]{1,0:T(8,128)(2,1)S(1)}, u32[]{:S(2)}, u32[]{:S(2)}) collective-permute-start(bf16[64,2048]{1,0:T(8,128)(2,1)S(1)} %collective-permute-done.3.refs_1_), channel_id=1, source_target_pairs={{0,224},{32,0},{64,32},{96,64},{128,96},{160,128},{192,160},{224,1... | collective-permute-start | bytes 786440 | tf_op jit(solution)/shard_map/ppermute | solution.py:25
  69.2 12.0 %collective-permute-start.6 = (bf16[64,2048]{1,0:T(8,128)(2,1)S(1)}, bf16[64,2048]{1,0:T(8,128)(2,1)S(1)}, u32[]{:S(2)}, u32[]{:S(2)}) collective-permute-start(bf16[64,2048]{1,0:T(8,128)(2,1)S(1)} %collective-permute-done.5.refs_0_), channel_id=1, source_target_pairs={{0,32},{32,64},{64,96},{96,128},{128,160},{160,192},{192,224},{224... | collective-permute-start | bytes 786440 | tf_op jit(solution)/shard_map/ppermute | solution.py:25
  71.1 11.2 %collective-permute-start.16 = (bf16[64,2048]{1,0:T(8,128)(2,1)S(1)}, bf16[64,2048]{1,0:T(8,128)(2,1)S(1)}, u32[]{:S(2)}, u32[]{:S(2)}) collective-permute-start(bf16[64,2048]{1,0:T(8,128)(2,1)S(1)} %collective-permute-done.15.refs_0_), channel_id=1, source_target_pairs={{0,224},{32,0},{64,32},{96,64},{128,96},{160,128},{192,160},{224,1... | collective-permute-start | bytes 786440 | tf_op jit(solution)/shard_map/ppermute | solution.py:25
  87.5 10.9 %collective-permute-start.18 = (f32[336,256]{1,0:T(8,128)S(1)}, f32[336,256]{1,0:T(8,128)S(1)}, u32[]{:S(2)}, u32[]{:S(2)}) collective-permute-start(f32[336,256]{1,0:T(8,128)S(1)} %add.27.sum_ref), channel_id=1, source_target_pairs={{0,1},{1,0},{2,3},{3,2},{4,5},{5,4},{6,7},{7,6},{8,9},{9,8},{10,11... | collective-permute-start | bytes 1032200 | tf_op jit(solution)/shard_map/ppermute | solution.py:25
  103.5 9.1 %collective-permute-start.21 = (bf16[64,2048]{1,0:T(8,128)(2,1)}, bf16[64,2048]{1,0:T(8,128)(2,1)}, u32[]{:S(2)}, u32[]{:S(2)}) collective-permute-start(bf16[64,2048]{1,0:T(8,128)(2,1)} %get-tuple-element.98), channel_id=1, source_target_pairs={{0,32},{32,64},{64,96},{96,128},{128,160},{160,192},{192,224},{224... | collective-permute-start | bytes 786440 | tf_op jit(solution)/shard_map/ppermute | solution.py:25
  106.4 11.7 %collective-permute-start.28 = (bf16[64,2048]{1,0:T(8,128)(2,1)}, bf16[64,2048]{1,0:T(8,128)(2,1)}, u32[]{:S(2)}, u32[]{:S(2)}) collective-permute-start(bf16[64,2048]{1,0:T(8,128)(2,1)} %get-tuple-element.96), channel_id=1, source_target_pairs={{0,32},{32,64},{64,96},{96,128},{128,160},{160,192},{192,224},{224... | collective-permute-start | bytes 786440 | tf_op jit(solution)/shard_map/ppermute | solution.py:25
  108.2 15.9 %collective-permute-start.23 = (bf16[64,2048]{1,0:T(8,128)(2,1)}, bf16[64,2048]{1,0:T(8,128)(2,1)S(1)}, u32[]{:S(2)}, u32[]{:S(2)}) collective-permute-start(bf16[64,2048]{1,0:T(8,128)(2,1)} %get-tuple-element.97), channel_id=1, source_target_pairs={{0,224},{32,0},{64,32},{96,64},{128,96},{160,128},{192,160},{224,1... | collective-permute-start | bytes 786440 | tf_op jit(solution)/shard_map/ppermute | solution.py:25
  109.1 13.4 %collective-permute-start.31 = (bf16[64,2048]{1,0:T(8,128)(2,1)}, bf16[64,2048]{1,0:T(8,128)(2,1)S(1)}, u32[]{:S(2)}, u32[]{:S(2)}) collective-permute-start(bf16[64,2048]{1,0:T(8,128)(2,1)} %get-tuple-element.95), channel_id=1, source_target_pairs={{0,224},{32,0},{64,32},{96,64},{128,96},{160,128},{192,160},{224,1... | collective-permute-start | bytes 786440 | tf_op jit(solution)/shard_map/ppermute | solution.py:25
  115.3 8.9 %collective-permute-start.22 = (bf16[64,2048]{1,0:T(8,128)(2,1)S(1)}, bf16[64,2048]{1,0:T(8,128)(2,1)S(1)}, u32[]{:S(2)}, u32[]{:S(2)}) collective-permute-start(bf16[64,2048]{1,0:T(8,128)(2,1)S(1)} %shard_map.106), channel_id=1, source_target_pairs={{0,32},{32,64},{64,96},{96,128},{128,160},{160,192},{192,224},{224... | collective-permute-start | bytes 786440 | tf_op jit(solution)/shard_map/ppermute | solution.py:25
  119.2 9.7 %collective-permute-start.29 = (bf16[64,2048]{1,0:T(8,128)(2,1)S(1)}, bf16[64,2048]{1,0:T(8,128)(2,1)S(1)}, u32[]{:S(2)}, u32[]{:S(2)}) collective-permute-start(bf16[64,2048]{1,0:T(8,128)(2,1)S(1)} %shard_map.111), channel_id=1, source_target_pairs={{0,32},{32,64},{64,96},{96,128},{128,160},{160,192},{192,224},{224... | collective-permute-start | bytes 786440 | tf_op jit(solution)/shard_map/ppermute | solution.py:25
  124.3 13.7 %collective-permute-start.24 = (bf16[64,2048]{1,0:T(8,128)(2,1)S(1)}, bf16[64,2048]{1,0:T(8,128)(2,1)S(1)}, u32[]{:S(2)}, u32[]{:S(2)}) collective-permute-start(bf16[64,2048]{1,0:T(8,128)(2,1)S(1)} %shard_map.107), channel_id=1, source_target_pairs={{0,32},{32,64},{64,96},{96,128},{128,160},{160,192},{192,224},{224... | collective-permute-start | bytes 786440 | tf_op jit(solution)/shard_map/ppermute | solution.py:25
  125.5 12.7 %collective-permute-start.26 = (bf16[64,2048]{1,0:T(8,128)(2,1)S(1)}, bf16[64,2048]{1,0:T(8,128)(2,1)S(1)}, u32[]{:S(2)}, u32[]{:S(2)}) collective-permute-start(bf16[64,2048]{1,0:T(8,128)(2,1)S(1)} %shard_map.109), channel_id=1, source_target_pairs={{0,224},{32,0},{64,32},{96,64},{128,96},{160,128},{192,160},{224,1... | collective-permute-start | bytes 786440 | tf_op jit(solution)/shard_map/ppermute | solution.py:25
  128.9 15.0 %collective-permute-start.30 = (bf16[64,2048]{1,0:T(8,128)(2,1)S(1)}, bf16[64,2048]{1,0:T(8,128)(2,1)S(1)}, u32[]{:S(2)}, u32[]{:S(2)}) collective-permute-start(bf16[64,2048]{1,0:T(8,128)(2,1)S(1)} %shard_map.112), channel_id=1, source_target_pairs={{0,32},{32,64},{64,96},{96,128},{128,160},{160,192},{192,224},{224... | collective-permute-start | bytes 786440 | tf_op jit(solution)/shard_map/ppermute | solution.py:25
  129.2 11.8 %collective-permute-start.33 = (bf16[64,2048]{1,0:T(8,128)(2,1)S(1)}, bf16[64,2048]{1,0:T(8,128)(2,1)S(1)}, u32[]{:S(2)}, u32[]{:S(2)}) collective-permute-start(bf16[64,2048]{1,0:T(8,128)(2,1)S(1)} %shard_map.114), channel_id=1, source_target_pairs={{0,224},{32,0},{64,32},{96,64},{128,96},{160,128},{192,160},{224,1... | collective-permute-start | bytes 786440 | tf_op jit(solution)/shard_map/ppermute | solution.py:25
  133.2 26.2 %collective-permute-start.36 = (bf16[112,2048]{1,0:T(8,128)(2,1)}, bf16[112,2048]{1,0:T(8,128)(2,1)}, u32[]{:S(2)}, u32[]{:S(2)}) collective-permute-start(bf16[112,2048]{1,0:T(8,128)(2,1)} %fusion.3), channel_id=1, source_target_pairs={{0,2},{2,0},{1,3},{3,1},{4,6},{6,4},{5,7},{7,5},{8,10},{10,8},{9,1... | collective-permute-start | bytes 1376264 | tf_op jit(solution)/shard_map/ppermute | solution.py:25
  138.1 9.0 %collective-permute-start.25 = (bf16[64,2048]{1,0:T(8,128)(2,1)S(1)}, bf16[64,2048]{1,0:T(8,128)(2,1)S(1)}, u32[]{:S(2)}, u32[]{:S(2)}) collective-permute-start(bf16[64,2048]{1,0:T(8,128)(2,1)S(1)} %shard_map.108), channel_id=1, source_target_pairs={{0,32},{32,64},{64,96},{96,128},{128,160},{160,192},{192,224},{224... | collective-permute-start | bytes 786440 | tf_op jit(solution)/shard_map/ppermute | solution.py:25
  138.3 8.8 %collective-permute-start.27 = (bf16[64,2048]{1,0:T(8,128)(2,1)S(1)}, bf16[64,2048]{1,0:T(8,128)(2,1)S(1)}, u32[]{:S(2)}, u32[]{:S(2)}) collective-permute-start(bf16[64,2048]{1,0:T(8,128)(2,1)S(1)} %shard_map.110), channel_id=1, source_target_pairs={{0,224},{32,0},{64,32},{96,64},{128,96},{160,128},{192,160},{224,1... | collective-permute-start | bytes 786440 | tf_op jit(solution)/shard_map/ppermute | solution.py:25
  141.1 11.3 %collective-permute-start.34 = (bf16[64,2048]{1,0:T(8,128)(2,1)S(1)}, bf16[64,2048]{1,0:T(8,128)(2,1)S(1)}, u32[]{:S(2)}, u32[]{:S(2)}) collective-permute-start(bf16[64,2048]{1,0:T(8,128)(2,1)S(1)} %shard_map.115), channel_id=1, source_target_pairs={{0,224},{32,0},{64,32},{96,64},{128,96},{160,128},{192,160},{224,1... | collective-permute-start | bytes 786440 | tf_op jit(solution)/shard_map/ppermute | solution.py:25
  143.9 20.4 %collective-permute-start.35 = (bf16[224,2048]{1,0:T(8,128)(2,1)}, bf16[224,2048]{1,0:T(8,128)(2,1)}, u32[]{:S(2)}, u32[]{:S(2)}) collective-permute-start(bf16[224,2048]{1,0:T(8,128)(2,1)} %fusion.1), channel_id=1, source_target_pairs={{0,2},{2,0},{1,3},{3,1},{4,6},{6,4},{5,7},{7,5},{8,10},{10,8},{9,1... | collective-permute-start | bytes 2752520 | tf_op jit(solution)/shard_map/ppermute | solution.py:25
  153.6 17.0 %all-to-all-start.1 = ((bf16[32,2,4096]{2,1,0:T(2,128)(2,1)}), bf16[32,2,4096]{2,1,0:T(2,128)(2,1)S(1)}, u32[]{:S(2)}, u32[]{:S(2)}) async-start(bf16[32,2,4096]{2,1,0:T(2,128)(2,1)} %shard_map.116), calls=%async_computation.1 | async-start | bytes 1048576 | tf_op jit(solution)/shard_map/all_to_all | solution.py:29
  (26 other events, 126.5 us)

commit v6 on v5

--- a/solution.py
+++ b/solution.py
@@ -306,7 +306,7 @@
     own, other = partial_sums(near_rows, near_grads)
     near_sums = own + shifted(other, "core", 1)
     ahead, behind = rings[0][half - 1], rings[1][1 - half]
-    behind, near_sums = lax.optimization_barrier((behind, near_sums))
+    ahead, near_sums = lax.optimization_barrier((ahead, near_sums))
     near_got = shifted(near_sums, "tok", 1)
     *ends, near_got = lax.optimization_barrier(
         (shifted(ahead, "z", -1), shifted(behind, "z", 1), near_got)

time: 172 us -> 170 us (0.988)
  waiting for transfers between devices: 69.6 us -> 66.5 us
    ppermute x37, waiting for transfers between devices: 59.2 us -> 56.2 us  [shifted(): lax.ppermute(block, axis, [(i, (i + distance) % count) for i in range(cou...]
    ppermute x37, starting transfers between devices: 52.3 us -> 54.1 us  [shifted(): lax.ppermute(block, axis, [(i, (i + distance) % count) for i in range(cou...]
  transfers between devices with their start and end apart: 39 -> 39, of which waited for: 22 -> 23; matrix products, arithmetic and copies ran while one was open for 8% -> 8% of each run, Pallas kernels for 5% -> 5%
where the time goes in v6:
time: 170 us; the launch traced here: 169 us
  waiting for transfers between devices  66.5 us (39%)
  starting transfers between devices  64.3 us (38%)
  Pallas kernels  15.4 us (9%)
  matrix products  10.6 us (6%)
  local copies, waits for them, and re-layouts  7.63 us (4%)
  other arithmetic  3.72 us (2%)
    ppermute x37, waiting for transfers between devices, shifted(): lax.ppermute(block, axis, [(i, (i + distance) % count) for i in range(cou...  56.2 us
    ppermute x37, starting transfers between devices, shifted(): lax.ppermute(block, axis, [(i, (i + distance) % count) for i in range(cou...  54.1 us
    all_to_all x2, waiting for transfers between devices, exchanged(): return lax.all_to_all(blocks, axes, 0, 0, tiled=True)  10.4 us
    all_to_all x2, starting transfers between devices, exchanged(): return lax.all_to_all(blocks, axes, 0, 0, tiled=True)  10.2 us
    pallas_call x13, Pallas kernels, called_at(): pl.pallas_call(functools.partial(kernel, **kwargs), out_shape=out_shape,...  10.1 us
    unnamed x38, local copies, waits for them, and re-layouts  5.94 us
    pallas_call x13, Pallas kernels, called(): pl.pallas_call(functools.partial(kernel, **kwargs), out_shape=out_shape,...  5.3 us
    dot_general x4, matrix products, by_columns(): lax.dot_general(left, right, (((0,), (0,)), ((), ())), preferred_element_...  5.04 us
  transfers between devices with their start and end apart: 39, of which 23 were waited for; matrix products, arithmetic and copies ran while one was open for 8% of the time, Pallas kernels for 5%

profile of v6, /device:TPU:1, one launch (start us, length us, event | category | flops | bytes accessed | tf_op | source)
XLA Modules:
  0.0 169.3 jit_solution(15993945025040166448)
XLA Ops:
  3.0 2.6 %shard_map.93 = bf16[336,2048]{1,0:T(8,128)(2,1)} custom-call(s32[1]{0:T(128)} %bitcast.1._, bf16[112,8192]{1,0:T(8,128)(2,1)} %gate_ref.1, bf16[112,8192]{1,0:T(8,128)(2,1)} %up_ref.1, bf16[112,8192]{1,0:T(8,128)(2,1)} %down_ref.1), custom_call_target="tpu_custom_call" | custom-call | tf_op jit(solution)/shard_map/pallas_call | solution.py:67
  5.5 3.2 %collective-permute-start = (bf16[336,2048]{1,0:T(8,128)(2,1)}, bf16[336,2048]{1,0:T(8,128)(2,1)S(1)}, u32[]{:S(2)}, u32[]{:S(2)}) collective-permute-start(bf16[336,2048]{1,0:T(8,128)(2,1)} %shard_map.93), channel_id=1, source_target_pairs={{0,2},{2,0},{1,3},{3,1},{4,6},{6,4},{5,7},{7,5},{8,10},{10,8},{9,1... | collective-permute-start | bytes 4128776 | tf_op jit(solution)/shard_map/ppermute | solution.py:25
  8.8 5.5 %all-to-all-start = ((bf16[32,2,4096]{2,1,0:T(2,128)(2,1)}), bf16[32,2,4096]{2,1,0:T(2,128)(2,1)S(1)}, u32[]{:S(2)}, u32[]{:S(2)}) async-start(bf16[32,2,4096]{2,1,0:T(2,128)(2,1)} %shard_map.92), calls=%async_computation | async-start | bytes 1048576 | tf_op jit(solution)/shard_map/all_to_all | solution.py:29
  15.4 3.6 %shard_map.94 = (bf16[448,2048]{1,0:T(8,128)(2,1)}, bf16[224,2048]{1,0:T(8,128)(2,1)}) custom-call(s32[1]{0:T(128)} %bitcast._, bf16[112,8192]{1,0:T(8,128)(2,1)} %gate_ref.1, bf16[112,8192]{1,0:T(8,128)(2,1)} %up_ref.1, bf16[112,8192]{1,0:T(8,128)(2,1)} %down_ref.1, bf16[336,2048]{1,0:T(8,128)(2,1)} %copy-done.18), custom_call_target="tpu_custom_call" | custom-call | tf_op jit(solution)/shard_map/pallas_call | solution.py:67
  19.0 6.7 %all-to-all-done.blocks_ref = bf16[32,2,4096]{2,1,0:T(2,128)(2,1)S(1)} async-done(((bf16[32,2,4096]{2,1,0:T(2,128)(2,1)}), bf16[32,2,4096]{2,1,0:T(2,128)(2,1)S(1)}, u32[]{:S(2)}, u32[]{:S(2)}) %all-to-all-start) | async-done | bytes 524320 | tf_op jit(solution)/shard_map/all_to_all | solution.py:29
  29.4 2.5 %collective-permute-start.1 = (bf16[64,2048]{1,0:T(8,128)(2,1)S(1)}, bf16[64,2048]{1,0:T(8,128)(2,1)S(1)}, u32[]{:S(2)}, u32[]{:S(2)}) collective-permute-start(bf16[64,2048]{1,0:T(8,128)(2,1)S(1)} %get-tuple-element.55.refs_2_), channel_id=1, source_target_pairs={{0,224},{32,0},{64,32},{96,64},{128,96},{160,128},{192,160},{224,1... | collective-permute-start | bytes 786440 | tf_op jit(solution)/shard_map/ppermute | solution.py:25
  31.9 6.5 %collective-permute-done.4.refs_1_ = bf16[64,2048]{1,0:T(8,128)(2,1)S(1)} collective-permute-done((bf16[64,2048]{1,0:T(8,128)(2,1)S(1)}, bf16[64,2048]{1,0:T(8,128)(2,1)S(1)}, u32[]{:S(2)}, u32[]{:S(2)}) %collective-permute-start.4) | collective-permute-done | bytes 262176 | tf_op jit(solution)/shard_map/ppermute | solution.py:25
  38.4 2.7 %collective-permute-start.9 = (bf16[64,2048]{1,0:T(8,128)(2,1)S(1)}, bf16[64,2048]{1,0:T(8,128)(2,1)S(1)}, u32[]{:S(2)}, u32[]{:S(2)}) collective-permute-start(bf16[64,2048]{1,0:T(8,128)(2,1)S(1)} %get-tuple-element.56.refs_2_), channel_id=1, source_target_pairs={{0,224},{32,0},{64,32},{96,64},{128,96},{160,128},{192,160},{224,1... | collective-permute-start | bytes 786440 | tf_op jit(solution)/shard_map/ppermute | solution.py:25
  41.0 2.9 %collective-permute-done.7.refs_1_ = bf16[64,2048]{1,0:T(8,128)(2,1)S(1)} collective-permute-done((bf16[64,2048]{1,0:T(8,128)(2,1)S(1)}, bf16[64,2048]{1,0:T(8,128)(2,1)S(1)}, u32[]{:S(2)}, u32[]{:S(2)}) %collective-permute-start.7) | collective-permute-done | bytes 262176 | tf_op jit(solution)/shard_map/ppermute | solution.py:25
  44.0 2.7 %collective-permute-start.2 = (bf16[64,2048]{1,0:T(8,128)(2,1)S(1)}, bf16[64,2048]{1,0:T(8,128)(2,1)S(1)}, u32[]{:S(2)}, u32[]{:S(2)}) collective-permute-start(bf16[64,2048]{1,0:T(8,128)(2,1)S(1)} %collective-permute-done.1.refs_3_), channel_id=1, source_target_pairs={{0,224},{32,0},{64,32},{96,64},{128,96},{160,128},{192,160},{224,1... | collective-permute-start | bytes 786440 | tf_op jit(solution)/shard_map/ppermute | solution.py:25
  46.7 2.9 %collective-permute-done.5.refs_0_ = bf16[64,2048]{1,0:T(8,128)(2,1)S(1)} collective-permute-done((bf16[64,2048]{1,0:T(8,128)(2,1)S(1)}, bf16[64,2048]{1,0:T(8,128)(2,1)S(1)}, u32[]{:S(2)}, u32[]{:S(2)}) %collective-permute-start.5) | collective-permute-done | bytes 262176 | tf_op jit(solution)/shard_map/ppermute | solution.py:25
  49.7 5.5 %collective-permute-done.8.refs_0_ = bf16[64,2048]{1,0:T(8,128)(2,1)S(1)} collective-permute-done((bf16[64,2048]{1,0:T(8,128)(2,1)S(1)}, bf16[64,2048]{1,0:T(8,128)(2,1)S(1)}, u32[]{:S(2)}, u32[]{:S(2)}) %collective-permute-start.8) | collective-permute-done | bytes 262176 | tf_op jit(solution)/shard_map/ppermute | solution.py:25
  58.9 2.7 %collective-permute-start.15 = (bf16[64,2048]{1,0:T(8,128)(2,1)S(1)}, bf16[64,2048]{1,0:T(8,128)(2,1)S(1)}, u32[]{:S(2)}, u32[]{:S(2)}) collective-permute-start(bf16[64,2048]{1,0:T(8,128)(2,1)S(1)} %collective-permute-done.9.refs_3_), channel_id=1, source_target_pairs={{0,224},{32,0},{64,32},{96,64},{128,96},{160,128},{192,160},{224,1... | collective-permute-start | bytes 786440 | tf_op jit(solution)/shard_map/ppermute | solution.py:25
  61.7 3.7 %collective-permute-done.3.refs_1_ = bf16[64,2048]{1,0:T(8,128)(2,1)S(1)} collective-permute-done((bf16[64,2048]{1,0:T(8,128)(2,1)S(1)}, bf16[64,2048]{1,0:T(8,128)(2,1)S(1)}, u32[]{:S(2)}, u32[]{:S(2)}) %collective-permute-start.3) | collective-permute-done | bytes 262176 | tf_op jit(solution)/shard_map/ppermute | solution.py:25
  67.7 2.7 %collective-permute-start.11 = (bf16[64,2048]{1,0:T(8,128)(2,1)S(1)}, bf16[64,2048]{1,0:T(8,128)(2,1)S(1)}, u32[]{:S(2)}, u32[]{:S(2)}) collective-permute-start(bf16[64,2048]{1,0:T(8,128)(2,1)S(1)} %collective-permute-done.3.refs_1_), channel_id=1, source_target_pairs={{0,224},{32,0},{64,32},{96,64},{128,96},{160,128},{192,160},{224,1... | collective-permute-start | bytes 786440 | tf_op jit(solution)/shard_map/ppermute | solution.py:25
  70.9 2.7 %collective-permute-start.16 = (bf16[64,2048]{1,0:T(8,128)(2,1)S(1)}, bf16[64,2048]{1,0:T(8,128)(2,1)S(1)}, u32[]{:S(2)}, u32[]{:S(2)}) collective-permute-start(bf16[64,2048]{1,0:T(8,128)(2,1)S(1)} %collective-permute-done.15.refs_0_), channel_id=1, source_target_pairs={{0,224},{32,0},{64,32},{96,64},{128,96},{160,128},{192,160},{224,1... | collective-permute-start | bytes 786440 | tf_op jit(solution)/shard_map/ppermute | solution.py:25
  73.6 1.9 %collective-permute-done.13.refs_3_ = bf16[64,2048]{1,0:T(8,128)(2,1)S(1)} collective-permute-done((bf16[64,2048]{1,0:T(8,128)(2,1)S(1)}, bf16[64,2048]{1,0:T(8,128)(2,1)S(1)}, u32[]{:S(2)}, u32[]{:S(2)}) %collective-permute-start.13) | collective-permute-done | bytes 262176 | tf_op jit(solution)/shard_map/ppermute | solution.py:25
  76.3 4.8 %collective-permute-done.6.refs_2_ = bf16[64,2048]{1,0:T(8,128)(2,1)S(1)} collective-permute-done((bf16[64,2048]{1,0:T(8,128)(2,1)S(1)}, bf16[64,2048]{1,0:T(8,128)(2,1)S(1)}, u32[]{:S(2)}, u32[]{:S(2)}) %collective-permute-start.6) | collective-permute-done | bytes 262176 | tf_op jit(solution)/shard_map/ppermute | solution.py:25
  89.5 7.6 %collective-permute-done.18.got_ref = f32[336,256]{1,0:T(8,128)S(1)} collective-permute-done((f32[336,256]{1,0:T(8,128)S(1)}, f32[336,256]{1,0:T(8,128)S(1)}, u32[]{:S(2)}, u32[]{:S(2)}) %collective-permute-start.18) | collective-permute-done | bytes 344096 | tf_op jit(solution)/shard_map/ppermute | solution.py:25
  99.6 1.8 %fusion.18 = (bf16[256,2048]{1,0:T(8,128)(2,1)S(1)}, f32[256,2048]{1,0:T(8,128)}) fusion(bf16[224,256]{1,0:T(8,128)(2,1)S(1)} %get-tuple-element.88, bf16[224,2048]{1,0:T(8,128)(2,1)S(1)} %copy-done.12), kind=kOutput, calls=%fused_computation.31 | convolution fusion | flops 235405312 | bytes 4177920 | tf_op jit(solution)/shard_map/dot_general | solution.py:37
  102.2 2.1 %fusion.19 = (bf16[256,2048]{1,0:T(8,128)(2,1)S(1)}, f32[256,2048]{1,0:T(8,128)}) fusion(bf16[448,256]{1,0:T(8,128)(2,1)S(1)} %get-tuple-element.84, bf16[448,2048]{1,0:T(8,128)(2,1)S(1)} %copy-done), kind=kOutput, calls=%fused_computation.32 | convolution fusion | flops 470286336 | bytes 5210112 | tf_op jit(solution)/shard_map/dot_general | solution.py:37
  109.3 2.0 %collective-permute-done.21.came_ref = bf16[64,2048]{1,0:T(8,128)(2,1)} collective-permute-done((bf16[64,2048]{1,0:T(8,128)(2,1)}, bf16[64,2048]{1,0:T(8,128)(2,1)}, u32[]{:S(2)}, u32[]{:S(2)}) %collective-permute-start.21) | collective-permute-done | bytes 262176 | tf_op jit(solution)/shard_map/ppermute | solution.py:25
  114.1 2.8 %collective-permute-done.28.came_ref = bf16[64,2048]{1,0:T(8,128)(2,1)} collective-permute-done((bf16[64,2048]{1,0:T(8,128)(2,1)}, bf16[64,2048]{1,0:T(8,128)(2,1)}, u32[]{:S(2)}, u32[]{:S(2)}) %collective-permute-start.28) | collective-permute-done | bytes 262176 | tf_op jit(solution)/shard_map/ppermute | solution.py:25
  120.4 2.0 %collective-permute-start.32 = (bf16[64,2048]{1,0:T(8,128)(2,1)S(1)}, bf16[64,2048]{1,0:T(8,128)(2,1)S(1)}, u32[]{:S(2)}, u32[]{:S(2)}) collective-permute-start(bf16[64,2048]{1,0:T(8,128)(2,1)S(1)} %shard_map.113), channel_id=1, source_target_pairs={{0,224},{32,0},{64,32},{96,64},{128,96},{160,128},{192,160},{224,1... | collective-permute-start | bytes 786440 | tf_op jit(solution)/shard_map/ppermute | solution.py:25
  123.4 2.6 %collective-permute-start.26 = (bf16[64,2048]{1,0:T(8,128)(2,1)S(1)}, bf16[64,2048]{1,0:T(8,128)(2,1)S(1)}, u32[]{:S(2)}, u32[]{:S(2)}) collective-permute-start(bf16[64,2048]{1,0:T(8,128)(2,1)S(1)} %shard_map.109), channel_id=1, source_target_pairs={{0,224},{32,0},{64,32},{96,64},{128,96},{160,128},{192,160},{224,1... | collective-permute-start | bytes 786440 | tf_op jit(solution)/shard_map/ppermute | solution.py:25
  127.9 2.7 %collective-permute-start.33 = (bf16[64,2048]{1,0:T(8,128)(2,1)S(1)}, bf16[64,2048]{1,0:T(8,128)(2,1)S(1)}, u32[]{:S(2)}, u32[]{:S(2)}) collective-permute-start(bf16[64,2048]{1,0:T(8,128)(2,1)S(1)} %shard_map.114), channel_id=1, source_target_pairs={{0,224},{32,0},{64,32},{96,64},{128,96},{160,128},{192,160},{224,1... | collective-permute-start | bytes 786440 | tf_op jit(solution)/shard_map/ppermute | solution.py:25
  132.0 4.3 %collective-permute-start.36 = (bf16[112,2048]{1,0:T(8,128)(2,1)}, bf16[112,2048]{1,0:T(8,128)(2,1)}, u32[]{:S(2)}, u32[]{:S(2)}) collective-permute-start(bf16[112,2048]{1,0:T(8,128)(2,1)} %fusion.3), channel_id=1, source_target_pairs={{0,2},{2,0},{1,3},{3,1},{4,6},{6,4},{5,7},{7,5},{8,10},{10,8},{9,1... | collective-permute-start | bytes 1376264 | tf_op jit(solution)/shard_map/ppermute | solution.py:25
  137.0 2.7 %collective-permute-start.27 = (bf16[64,2048]{1,0:T(8,128)(2,1)S(1)}, bf16[64,2048]{1,0:T(8,128)(2,1)S(1)}, u32[]{:S(2)}, u32[]{:S(2)}) collective-permute-start(bf16[64,2048]{1,0:T(8,128)(2,1)S(1)} %shard_map.110), channel_id=1, source_target_pairs={{0,224},{32,0},{64,32},{96,64},{128,96},{160,128},{192,160},{224,1... | collective-permute-start | bytes 786440 | tf_op jit(solution)/shard_map/ppermute | solution.py:25
  142.7 2.7 %collective-permute-start.35 = (bf16[224,2048]{1,0:T(8,128)(2,1)}, bf16[224,2048]{1,0:T(8,128)(2,1)}, u32[]{:S(2)}, u32[]{:S(2)}) collective-permute-start(bf16[224,2048]{1,0:T(8,128)(2,1)} %fusion.1), channel_id=1, source_target_pairs={{0,2},{2,0},{1,3},{3,1},{4,6},{6,4},{5,7},{7,5},{8,10},{10,8},{9,1... | collective-permute-start | bytes 2752520 | tf_op jit(solution)/shard_map/ppermute | solution.py:25
  145.8 5.3 %collective-permute-done.34.b2_ref = bf16[64,2048]{1,0:T(8,128)(2,1)S(1)} collective-permute-done((bf16[64,2048]{1,0:T(8,128)(2,1)S(1)}, bf16[64,2048]{1,0:T(8,128)(2,1)S(1)}, u32[]{:S(2)}, u32[]{:S(2)}) %collective-permute-start.34) | collective-permute-done | bytes 262176 | tf_op jit(solution)/shard_map/ppermute | solution.py:25
  152.3 4.8 %all-to-all-start.1 = ((bf16[32,2,4096]{2,1,0:T(2,128)(2,1)}), bf16[32,2,4096]{2,1,0:T(2,128)(2,1)S(1)}, u32[]{:S(2)}, u32[]{:S(2)}) async-start(bf16[32,2,4096]{2,1,0:T(2,128)(2,1)} %shard_map.116), calls=%async_computation.1 | async-start | bytes 1048576 | tf_op jit(solution)/shard_map/all_to_all | solution.py:29
  164.9 3.6 %all-to-all-done.1.blocks_ref = bf16[32,2,4096]{2,1,0:T(2,128)(2,1)S(1)} async-done(((bf16[32,2,4096]{2,1,0:T(2,128)(2,1)}), bf16[32,2,4096]{2,1,0:T(2,128)(2,1)S(1)}, u32[]{:S(2)}, u32[]{:S(2)}) %all-to-all-start.1) | async-done | bytes 524320 | tf_op jit(solution)/shard_map/all_to_all | solution.py:29
  (129 shorter events, 55.6 us)
Async XLA Ops:
  5.5 8.7 %collective-permute-start = (bf16[336,2048]{1,0:T(8,128)(2,1)}, bf16[336,2048]{1,0:T(8,128)(2,1)S(1)}, u32[]{:S(2)}, u32[]{:S(2)}) collective-permute-start(bf16[336,2048]{1,0:T(8,128)(2,1)} %shard_map.93), channel_id=1, source_target_pairs={{0,2},{2,0},{1,3},{3,1},{4,6},{6,4},{5,7},{7,5},{8,10},{10,8},{9,1... | collective-permute-start | bytes 4128776 | tf_op jit(solution)/shard_map/ppermute | solution.py:25
  8.8 16.9 %all-to-all-start = ((bf16[32,2,4096]{2,1,0:T(2,128)(2,1)}), bf16[32,2,4096]{2,1,0:T(2,128)(2,1)S(1)}, u32[]{:S(2)}, u32[]{:S(2)}) async-start(bf16[32,2,4096]{2,1,0:T(2,128)(2,1)} %shard_map.92), calls=%async_computation | async-start | bytes 1048576 | tf_op jit(solution)/shard_map/all_to_all | solution.py:29
  26.0 12.3 %collective-permute-start.4 = (bf16[64,2048]{1,0:T(8,128)(2,1)S(1)}, bf16[64,2048]{1,0:T(8,128)(2,1)S(1)}, u32[]{:S(2)}, u32[]{:S(2)}) collective-permute-start(bf16[64,2048]{1,0:T(8,128)(2,1)S(1)} %get-tuple-element.55.refs_2_), channel_id=1, source_target_pairs={{0,32},{32,64},{64,96},{96,128},{128,160},{160,192},{192,224},{224... | collective-permute-start | bytes 786440 | tf_op jit(solution)/shard_map/ppermute | solution.py:25
  27.8 16.2 %collective-permute-start.7 = (bf16[64,2048]{1,0:T(8,128)(2,1)S(1)}, bf16[64,2048]{1,0:T(8,128)(2,1)S(1)}, u32[]{:S(2)}, u32[]{:S(2)}) collective-permute-start(bf16[64,2048]{1,0:T(8,128)(2,1)S(1)} %get-tuple-element.56.refs_2_), channel_id=1, source_target_pairs={{0,32},{32,64},{64,96},{96,128},{128,160},{160,192},{192,224},{224... | collective-permute-start | bytes 786440 | tf_op jit(solution)/shard_map/ppermute | solution.py:25
  29.4 14.6 %collective-permute-start.1 = (bf16[64,2048]{1,0:T(8,128)(2,1)S(1)}, bf16[64,2048]{1,0:T(8,128)(2,1)S(1)}, u32[]{:S(2)}, u32[]{:S(2)}) collective-permute-start(bf16[64,2048]{1,0:T(8,128)(2,1)S(1)} %get-tuple-element.55.refs_2_), channel_id=1, source_target_pairs={{0,224},{32,0},{64,32},{96,64},{128,96},{160,128},{192,160},{224,1... | collective-permute-start | bytes 786440 | tf_op jit(solution)/shard_map/ppermute | solution.py:25
  38.4 11.2 %collective-permute-start.5 = (bf16[64,2048]{1,0:T(8,128)(2,1)S(1)}, bf16[64,2048]{1,0:T(8,128)(2,1)S(1)}, u32[]{:S(2)}, u32[]{:S(2)}) collective-permute-start(bf16[64,2048]{1,0:T(8,128)(2,1)S(1)} %collective-permute-done.4.refs_1_), channel_id=1, source_target_pairs={{0,32},{32,64},{64,96},{96,128},{128,160},{160,192},{192,224},{224... | collective-permute-start | bytes 786440 | tf_op jit(solution)/shard_map/ppermute | solution.py:25
  38.4 11.4 %collective-permute-start.9 = (bf16[64,2048]{1,0:T(8,128)(2,1)S(1)}, bf16[64,2048]{1,0:T(8,128)(2,1)S(1)}, u32[]{:S(2)}, u32[]{:S(2)}) collective-permute-start(bf16[64,2048]{1,0:T(8,128)(2,1)S(1)} %get-tuple-element.56.refs_2_), channel_id=1, source_target_pairs={{0,224},{32,0},{64,32},{96,64},{128,96},{160,128},{192,160},{224,1... | collective-permute-start | bytes 786440 | tf_op jit(solution)/shard_map/ppermute | solution.py:25
  44.0 11.2 %collective-permute-start.8 = (bf16[64,2048]{1,0:T(8,128)(2,1)S(1)}, bf16[64,2048]{1,0:T(8,128)(2,1)S(1)}, u32[]{:S(2)}, u32[]{:S(2)}) collective-permute-start(bf16[64,2048]{1,0:T(8,128)(2,1)S(1)} %collective-permute-done.7.refs_1_), channel_id=1, source_target_pairs={{0,32},{32,64},{64,96},{96,128},{128,160},{160,192},{192,224},{224... | collective-permute-start | bytes 786440 | tf_op jit(solution)/shard_map/ppermute | solution.py:25
  44.0 13.5 %collective-permute-start.2 = (bf16[64,2048]{1,0:T(8,128)(2,1)S(1)}, bf16[64,2048]{1,0:T(8,128)(2,1)S(1)}, u32[]{:S(2)}, u32[]{:S(2)}) collective-permute-start(bf16[64,2048]{1,0:T(8,128)(2,1)S(1)} %collective-permute-done.1.refs_3_), channel_id=1, source_target_pairs={{0,224},{32,0},{64,32},{96,64},{128,96},{160,128},{192,160},{224,1... | collective-permute-start | bytes 786440 | tf_op jit(solution)/shard_map/ppermute | solution.py:25
  58.9 8.7 %collective-permute-start.12 = (bf16[64,2048]{1,0:T(8,128)(2,1)S(1)}, bf16[64,2048]{1,0:T(8,128)(2,1)S(1)}, u32[]{:S(2)}, u32[]{:S(2)}) collective-permute-start(bf16[64,2048]{1,0:T(8,128)(2,1)S(1)} %collective-permute-done.8.refs_0_), channel_id=1, source_target_pairs={{0,32},{32,64},{64,96},{96,128},{128,160},{160,192},{192,224},{224... | collective-permute-start | bytes 786440 | tf_op jit(solution)/shard_map/ppermute | solution.py:25
  58.9 12.0 %collective-permute-start.15 = (bf16[64,2048]{1,0:T(8,128)(2,1)S(1)}, bf16[64,2048]{1,0:T(8,128)(2,1)S(1)}, u32[]{:S(2)}, u32[]{:S(2)}) collective-permute-start(bf16[64,2048]{1,0:T(8,128)(2,1)S(1)} %collective-permute-done.9.refs_3_), channel_id=1, source_target_pairs={{0,224},{32,0},{64,32},{96,64},{128,96},{160,128},{192,160},{224,1... | collective-permute-start | bytes 786440 | tf_op jit(solution)/shard_map/ppermute | solution.py:25
  65.3 11.0 %collective-permute-start.14 = (f32[336,256]{1,0:T(8,128)S(1)}, f32[336,256]{1,0:T(8,128)S(1)}, u32[]{:S(2)}, u32[]{:S(2)}) collective-permute-start(f32[336,256]{1,0:T(8,128)S(1)} %add.26.sum_ref), channel_id=1, source_target_pairs={{0,1},{1,0},{2,3},{3,2},{4,5},{5,4},{6,7},{7,6},{8,9},{9,8},{10,11... | collective-permute-start | bytes 1032200 | tf_op jit(solution)/shard_map/ppermute | solution.py:25
  67.7 8.7 %collective-permute-start.11 = (bf16[64,2048]{1,0:T(8,128)(2,1)S(1)}, bf16[64,2048]{1,0:T(8,128)(2,1)S(1)}, u32[]{:S(2)}, u32[]{:S(2)}) collective-permute-start(bf16[64,2048]{1,0:T(8,128)(2,1)S(1)} %collective-permute-done.3.refs_1_), channel_id=1, source_target_pairs={{0,224},{32,0},{64,32},{96,64},{128,96},{160,128},{192,160},{224,1... | collective-permute-start | bytes 786440 | tf_op jit(solution)/shard_map/ppermute | solution.py:25
  70.3 10.8 %collective-permute-start.6 = (bf16[64,2048]{1,0:T(8,128)(2,1)S(1)}, bf16[64,2048]{1,0:T(8,128)(2,1)S(1)}, u32[]{:S(2)}, u32[]{:S(2)}) collective-permute-start(bf16[64,2048]{1,0:T(8,128)(2,1)S(1)} %collective-permute-done.5.refs_0_), channel_id=1, source_target_pairs={{0,32},{32,64},{64,96},{96,128},{128,160},{160,192},{192,224},{224... | collective-permute-start | bytes 786440 | tf_op jit(solution)/shard_map/ppermute | solution.py:25
  70.9 11.0 %collective-permute-start.16 = (bf16[64,2048]{1,0:T(8,128)(2,1)S(1)}, bf16[64,2048]{1,0:T(8,128)(2,1)S(1)}, u32[]{:S(2)}, u32[]{:S(2)}) collective-permute-start(bf16[64,2048]{1,0:T(8,128)(2,1)S(1)} %collective-permute-done.15.refs_0_), channel_id=1, source_target_pairs={{0,224},{32,0},{64,32},{96,64},{128,96},{160,128},{192,160},{224,1... | collective-permute-start | bytes 786440 | tf_op jit(solution)/shard_map/ppermute | solution.py:25
  86.3 10.9 %collective-permute-start.18 = (f32[336,256]{1,0:T(8,128)S(1)}, f32[336,256]{1,0:T(8,128)S(1)}, u32[]{:S(2)}, u32[]{:S(2)}) collective-permute-start(f32[336,256]{1,0:T(8,128)S(1)} %add.27.sum_ref), channel_id=1, source_target_pairs={{0,1},{1,0},{2,3},{3,2},{4,5},{5,4},{6,7},{7,6},{8,9},{9,8},{10,11... | collective-permute-start | bytes 1032200 | tf_op jit(solution)/shard_map/ppermute | solution.py:25
  102.2 9.0 %collective-permute-start.21 = (bf16[64,2048]{1,0:T(8,128)(2,1)}, bf16[64,2048]{1,0:T(8,128)(2,1)}, u32[]{:S(2)}, u32[]{:S(2)}) collective-permute-start(bf16[64,2048]{1,0:T(8,128)(2,1)} %get-tuple-element.98), channel_id=1, source_target_pairs={{0,32},{32,64},{64,96},{96,128},{128,160},{160,192},{192,224},{224... | collective-permute-start | bytes 786440 | tf_op jit(solution)/shard_map/ppermute | solution.py:25
  105.2 11.7 %collective-permute-start.28 = (bf16[64,2048]{1,0:T(8,128)(2,1)}, bf16[64,2048]{1,0:T(8,128)(2,1)}, u32[]{:S(2)}, u32[]{:S(2)}) collective-permute-start(bf16[64,2048]{1,0:T(8,128)(2,1)} %get-tuple-element.96), channel_id=1, source_target_pairs={{0,32},{32,64},{64,96},{96,128},{128,160},{160,192},{192,224},{224... | collective-permute-start | bytes 786440 | tf_op jit(solution)/shard_map/ppermute | solution.py:25
  106.3 16.6 %collective-permute-start.23 = (bf16[64,2048]{1,0:T(8,128)(2,1)}, bf16[64,2048]{1,0:T(8,128)(2,1)S(1)}, u32[]{:S(2)}, u32[]{:S(2)}) collective-permute-start(bf16[64,2048]{1,0:T(8,128)(2,1)} %get-tuple-element.97), channel_id=1, source_target_pairs={{0,224},{32,0},{64,32},{96,64},{128,96},{160,128},{192,160},{224,1... | collective-permute-start | bytes 786440 | tf_op jit(solution)/shard_map/ppermute | solution.py:25
  107.8 12.5 %collective-permute-start.31 = (bf16[64,2048]{1,0:T(8,128)(2,1)}, bf16[64,2048]{1,0:T(8,128)(2,1)S(1)}, u32[]{:S(2)}, u32[]{:S(2)}) collective-permute-start(bf16[64,2048]{1,0:T(8,128)(2,1)} %get-tuple-element.95), channel_id=1, source_target_pairs={{0,224},{32,0},{64,32},{96,64},{128,96},{160,128},{192,160},{224,1... | collective-permute-start | bytes 786440 | tf_op jit(solution)/shard_map/ppermute | solution.py:25
  114.0 8.9 %collective-permute-start.22 = (bf16[64,2048]{1,0:T(8,128)(2,1)S(1)}, bf16[64,2048]{1,0:T(8,128)(2,1)S(1)}, u32[]{:S(2)}, u32[]{:S(2)}) collective-permute-start(bf16[64,2048]{1,0:T(8,128)(2,1)S(1)} %shard_map.106), channel_id=1, source_target_pairs={{0,32},{32,64},{64,96},{96,128},{128,160},{160,192},{192,224},{224... | collective-permute-start | bytes 786440 | tf_op jit(solution)/shard_map/ppermute | solution.py:25
  117.9 9.7 %collective-permute-start.29 = (bf16[64,2048]{1,0:T(8,128)(2,1)S(1)}, bf16[64,2048]{1,0:T(8,128)(2,1)S(1)}, u32[]{:S(2)}, u32[]{:S(2)}) collective-permute-start(bf16[64,2048]{1,0:T(8,128)(2,1)S(1)} %shard_map.111), channel_id=1, source_target_pairs={{0,32},{32,64},{64,96},{96,128},{128,160},{160,192},{192,224},{224... | collective-permute-start | bytes 786440 | tf_op jit(solution)/shard_map/ppermute | solution.py:25
  123.0 13.7 %collective-permute-start.24 = (bf16[64,2048]{1,0:T(8,128)(2,1)S(1)}, bf16[64,2048]{1,0:T(8,128)(2,1)S(1)}, u32[]{:S(2)}, u32[]{:S(2)}) collective-permute-start(bf16[64,2048]{1,0:T(8,128)(2,1)S(1)} %shard_map.107), channel_id=1, source_target_pairs={{0,32},{32,64},{64,96},{96,128},{128,160},{160,192},{192,224},{224... | collective-permute-start | bytes 786440 | tf_op jit(solution)/shard_map/ppermute | solution.py:25
  123.4 13.6 %collective-permute-start.26 = (bf16[64,2048]{1,0:T(8,128)(2,1)S(1)}, bf16[64,2048]{1,0:T(8,128)(2,1)S(1)}, u32[]{:S(2)}, u32[]{:S(2)}) collective-permute-start(bf16[64,2048]{1,0:T(8,128)(2,1)S(1)} %shard_map.109), channel_id=1, source_target_pairs={{0,224},{32,0},{64,32},{96,64},{128,96},{160,128},{192,160},{224,1... | collective-permute-start | bytes 786440 | tf_op jit(solution)/shard_map/ppermute | solution.py:25
  127.7 15.0 %collective-permute-start.30 = (bf16[64,2048]{1,0:T(8,128)(2,1)S(1)}, bf16[64,2048]{1,0:T(8,128)(2,1)S(1)}, u32[]{:S(2)}, u32[]{:S(2)}) collective-permute-start(bf16[64,2048]{1,0:T(8,128)(2,1)S(1)} %shard_map.112), channel_id=1, source_target_pairs={{0,32},{32,64},{64,96},{96,128},{128,160},{160,192},{192,224},{224... | collective-permute-start | bytes 786440 | tf_op jit(solution)/shard_map/ppermute | solution.py:25
  127.9 11.9 %collective-permute-start.33 = (bf16[64,2048]{1,0:T(8,128)(2,1)S(1)}, bf16[64,2048]{1,0:T(8,128)(2,1)S(1)}, u32[]{:S(2)}, u32[]{:S(2)}) collective-permute-start(bf16[64,2048]{1,0:T(8,128)(2,1)S(1)} %shard_map.114), channel_id=1, source_target_pairs={{0,224},{32,0},{64,32},{96,64},{128,96},{160,128},{192,160},{224,1... | collective-permute-start | bytes 786440 | tf_op jit(solution)/shard_map/ppermute | solution.py:25
  132.0 25.4 %collective-permute-start.36 = (bf16[112,2048]{1,0:T(8,128)(2,1)}, bf16[112,2048]{1,0:T(8,128)(2,1)}, u32[]{:S(2)}, u32[]{:S(2)}) collective-permute-start(bf16[112,2048]{1,0:T(8,128)(2,1)} %fusion.3), channel_id=1, source_target_pairs={{0,2},{2,0},{1,3},{3,1},{4,6},{6,4},{5,7},{7,5},{8,10},{10,8},{9,1... | collective-permute-start | bytes 1376264 | tf_op jit(solution)/shard_map/ppermute | solution.py:25
  136.8 9.0 %collective-permute-start.25 = (bf16[64,2048]{1,0:T(8,128)(2,1)S(1)}, bf16[64,2048]{1,0:T(8,128)(2,1)S(1)}, u32[]{:S(2)}, u32[]{:S(2)}) collective-permute-start(bf16[64,2048]{1,0:T(8,128)(2,1)S(1)} %shard_map.108), channel_id=1, source_target_pairs={{0,32},{32,64},{64,96},{96,128},{128,160},{160,192},{192,224},{224... | collective-permute-start | bytes 786440 | tf_op jit(solution)/shard_map/ppermute | solution.py:25
  137.0 8.8 %collective-permute-start.27 = (bf16[64,2048]{1,0:T(8,128)(2,1)S(1)}, bf16[64,2048]{1,0:T(8,128)(2,1)S(1)}, u32[]{:S(2)}, u32[]{:S(2)}) collective-permute-start(bf16[64,2048]{1,0:T(8,128)(2,1)S(1)} %shard_map.110), channel_id=1, source_target_pairs={{0,224},{32,0},{64,32},{96,64},{128,96},{160,128},{192,160},{224,1... | collective-permute-start | bytes 786440 | tf_op jit(solution)/shard_map/ppermute | solution.py:25
  139.8 11.3 %collective-permute-start.34 = (bf16[64,2048]{1,0:T(8,128)(2,1)S(1)}, bf16[64,2048]{1,0:T(8,128)(2,1)S(1)}, u32[]{:S(2)}, u32[]{:S(2)}) collective-permute-start(bf16[64,2048]{1,0:T(8,128)(2,1)S(1)} %shard_map.115), channel_id=1, source_target_pairs={{0,224},{32,0},{64,32},{96,64},{128,96},{160,128},{192,160},{224,1... | collective-permute-start | bytes 786440 | tf_op jit(solution)/shard_map/ppermute | solution.py:25
  142.7 19.6 %collective-permute-start.35 = (bf16[224,2048]{1,0:T(8,128)(2,1)}, bf16[224,2048]{1,0:T(8,128)(2,1)}, u32[]{:S(2)}, u32[]{:S(2)}) collective-permute-start(bf16[224,2048]{1,0:T(8,128)(2,1)} %fusion.1), channel_id=1, source_target_pairs={{0,2},{2,0},{1,3},{3,1},{4,6},{6,4},{5,7},{7,5},{8,10},{10,8},{9,1... | collective-permute-start | bytes 2752520 | tf_op jit(solution)/shard_map/ppermute | solution.py:25
  152.3 16.2 %all-to-all-start.1 = ((bf16[32,2,4096]{2,1,0:T(2,128)(2,1)}), bf16[32,2,4096]{2,1,0:T(2,128)(2,1)S(1)}, u32[]{:S(2)}, u32[]{:S(2)}) async-start(bf16[32,2,4096]{2,1,0:T(2,128)(2,1)} %shard_map.116), calls=%async_computation.1 | async-start | bytes 1048576 | tf_op jit(solution)/shard_map/all_to_all | solution.py:29
  (26 other events, 127.4 us)
